TPU v7x, 256 devices: a whole 4x4x8 slice. The times are simulated.
256 devices in a mesh: gx: 128 (over z, x, y), ta: 2 (over core).
Axes of the slice: x: 4, y: 4, z: 8, core: 2. Of those that a mesh axis runs over, the one named last changes fastest.
Arguments:
- embeddings: bfloat16 [131072, 512], P('gx'), may hold values from -12 to 12
- labels: bfloat16 [131072, 256], P('gx'), may hold values from -6 to 6
- bucket_ids: int32 [2, 131072, 1], P('ta', 'gx'), may hold values from 0 to 127, as said below
Outputs:
- diffused: float32 [131072, 256], P('gx')
Inputs may be any that keep to these rules, and one draw needn't show every extreme that they name: `bucket_ids`: in each table, the items of one index of gx name any one bucket at most 16 times; in each table one bucket is named exactly 16 times by the items of every index of gx.
All inputs are finite; a program needn't handle non-finite values.
Results may differ from a plain program's by a relative error of at most 0.00032.
Values may be sent and summed in bfloat16 or wider, within the bound.
A program may use at most 64 MiB of HBM per device.

v0:
```python
import jax
import jax.numpy as jnp
from jax import lax
from jax.sharding import PartitionSpec as P

CAP = 2048
PAD_MARK = -1024.0


sharpness = 8.0
alpha_mix = 0.8


def normalize(embeds):
    wide = embeds.astype(jnp.float32)
    return (wide * lax.rsqrt(jnp.sum(wide * wide, axis=1, keepdims=True) + 1e-06)).astype(
        jnp.bfloat16
    )


def bucket_weights(unit, valid):
    cap = unit.shape[0]
    block = min(512, cap)
    cols = jnp.arange(cap)
    blocks = []
    dens = []
    for start in range(0, cap, block):
        gram = lax.dot_general(
            unit[start : start + block],
            unit,
            (((1,), (1,)), ((), ())),
            preferred_element_type=jnp.float32,
        )
        keep = valid[None, :] * (cols[None, :] != (start + jnp.arange(block))[:, None]).astype(
            jnp.float32
        )
        weights = (jnp.exp(sharpness * gram) * keep).astype(jnp.bfloat16)
        blocks.append(weights)
        dens.append(jnp.sum(weights.astype(jnp.float32), axis=1))
    return blocks, jnp.concatenate(dens, axis=0)


def weighted_sums(blocks, feats):
    return jnp.concatenate(
        [jnp.dot(w, feats, preferred_element_type=jnp.float32) for w in blocks], axis=0
    )


def body(embeddings, labels, bucket_ids):
    groups = lax.axis_size("gx")
    rows = embeddings.shape[0]
    slot = CAP // groups
    width_l = labels.shape[1]
    ids = bucket_ids[0, :, 0]
    pos = jnp.arange(rows, dtype=jnp.int32)
    same = (ids[:, None] == ids[None, :]) & (pos[None, :] < pos[:, None])
    rank = jnp.sum(same.astype(jnp.int32), axis=1)
    target = ids * slot + rank
    slots = jnp.arange(groups * slot, dtype=jnp.int32)
    place_mat = (target[None, :] == slots[:, None]).astype(jnp.bfloat16)
    occupied = jnp.sum(place_mat.astype(jnp.float32), axis=1) > 0.5
    prior = labels.astype(jnp.float32)

    def place(payload):
        return jnp.dot(place_mat, payload, preferred_element_type=jnp.float32).astype(payload.dtype)

    def exchange(buffer):
        return lax.all_to_all(buffer, "gx", split_axis=0, concat_axis=0, tiled=True)

    def other_core(values):
        return lax.ppermute(values, "ta", perm=[(0, 1), (1, 0)])

    unit_here = normalize(embeddings)
    placed = place(jnp.concatenate([unit_here, labels], axis=1))
    mark = jnp.where(occupied, placed[:, unit_here.shape[1]], PAD_MARK)
    placed = placed.at[:, unit_here.shape[1]].set(mark.astype(jnp.bfloat16))
    got = exchange(placed.reshape(groups, slot, -1)).reshape(groups * slot, -1)
    unit = got[:, : unit_here.shape[1]]
    feats0 = got[:, unit_here.shape[1] :]
    valid = (feats0[:, 0].astype(jnp.float32) > PAD_MARK * 0.5).astype(jnp.float32)

    blocks, den = bucket_weights(unit, valid)
    num1 = weighted_sums(blocks, feats0)

    packed = jnp.concatenate(
        [
            num1.reshape(groups, slot * width_l),
            jnp.pad(den.reshape(groups, slot), ((0, 0), (0, 128 - slot))),
        ],
        axis=1,
    )
    back = exchange(packed)
    back_num = back[:, : slot * width_l].reshape(groups * slot, width_l)
    back_den = back[:, slot * width_l : slot * width_l + slot].reshape(groups * slot)
    row_num = back_num[target]
    row_den = back_den[target]
    other_num, other_den = other_core((row_num, row_den))
    total_num = row_num + other_num
    total_den = row_den + other_den
    scale = (1.0 + total_den)[:, None]
    first = (1.0 - alpha_mix) * prior + alpha_mix * total_num / scale

    feats1 = exchange(place(first.astype(jnp.bfloat16)).reshape(groups, slot, -1))
    num2 = weighted_sums(blocks, feats1.reshape(groups * slot, -1))
    back2 = exchange(num2.reshape(groups, slot, -1)).reshape(groups * slot, -1)
    row_num2 = back2[target]
    total_num2 = row_num2 + other_core(row_num2)
    return (1.0 - alpha_mix) * prior + alpha_mix * total_num2 / scale


def solution(mesh):
    return jax.shard_map(
        body,
        mesh=mesh,
        in_specs=(P("gx", None), P("gx", None), P("ta", "gx", None)),
        out_specs=P("gx", None),
        check_vma=False,
    )
```

profile of v0, /device:TPU:1, one launch (start us, length us, event | category | flops | bytes accessed | tf_op | source)
XLA Modules:
  0.0 314.2 jit_solution(11342513255760513233)
XLA Ops:
  0.0 0.7 compare_reduce_fusion
  0.7 1.3 convert_reduce_fusion.5
  2.0 0.7 multiply_add_fusion
  2.7 1.5 fusion.8
  4.2 1.5 fusion.9
  5.7 0.9 convert_reduce_fusion
  6.7 0.0 copy-done.2
  6.7 4.0 %fusion.6 = bf16[2048,768]{1,0:T(8,128)(2,1)S(1)} fusion(s32[1024]{0:T(1024)S(1)} %multiply_add_fusion, bf16[1024,256]{1,0:T(8,128)(2,1)S(1)} %copy-done.2, bf16[1024,512]{1,0:T(8,128)(2,1)S(1)} %fusion.9), kind=kOutput, calls=%fused_computation.25 | convolution fusion | flops 3228041216 | bytes 4722688 | tf_op jit(solution)/shard_map/dot_general | solution.py:65
  10.6 1.8 fusion.17
  12.5 2.5 scatter.4
  15.0 0.0 copy-start.1
  15.0 1.7 copy-done.1
  16.7 16.5 %all-to-all-start = ((bf16[128,16,768]{2,1,0:T(8,128)(2,1)}), bf16[128,16,768]{2,1,0:T(8,128)(2,1)S(1)}, u32[]{:S(2)}, u32[]{:S(2)}) async-start(bf16[128,16,768]{2,1,0:T(8,128)(2,1)} %bitcast.41), calls=%async_computation | async-start | bytes 6291456 | tf_op jit(solution)/shard_map/all_to_all | solution.py:68
  33.2 70.6 %all-to-all-done = bf16[128,16,768]{2,1,0:T(8,128)(2,1)S(1)} async-done(((bf16[128,16,768]{2,1,0:T(8,128)(2,1)}), bf16[128,16,768]{2,1,0:T(8,128)(2,1)S(1)}, u32[]{:S(2)}, u32[]{:S(2)}) %all-to-all-start) | async-done | bytes 3145760 | tf_op jit(solution)/shard_map/all_to_all | solution.py:68
  103.9 0.2 convert_reduce_fusion.6
  104.1 1.5 convert_reduce_fusion.4
  105.6 0.7 fusion.24
  106.3 1.8 convert_reduce_fusion.3
  108.1 0.7 fusion.22
  108.8 1.8 convert_reduce_fusion.2
  110.6 0.7 fusion.20
  111.3 1.8 convert_reduce_fusion.1
  113.1 0.0 copy-done.9
  113.1 0.0 copy-start.11
  113.1 0.7 fusion.18
  113.9 0.6 copy-done.11
  114.4 1.5 pad_maximum_fusion.1
  115.9 1.7 reshape.137
  117.7 0.1 concatenate.28
  117.7 0.1 concatenate.29
  117.8 0.1 concatenate.30
  117.9 0.1 concatenate.31
  118.0 0.2 pad_maximum_fusion
  118.2 2.8 all_to_all.18
  121.0 10.9 %all-to-all-start.1 = ((f32[128,1,4224]{2,1,0:T(1,128)}), f32[128,1,4224]{2,1,0:T(1,128)S(1)}, u32[]{:S(2)}, u32[]{:S(2)}) async-start(f32[128,1,4224]{2,1,0:T(1,128)} %all_to_all.18), calls=%async_computation.1 | async-start | bytes 4325376 | tf_op jit(solution)/shard_map/all_to_all | solution.py:68
  132.0 49.9 %all-to-all-done.1 = f32[128,1,4224]{2,1,0:T(1,128)S(1)} async-done(((f32[128,1,4224]{2,1,0:T(1,128)}), f32[128,1,4224]{2,1,0:T(1,128)S(1)}, u32[]{:S(2)}, u32[]{:S(2)}) %all-to-all-start.1) | async-done | bytes 2162720 | tf_op jit(solution)/shard_map/all_to_all | solution.py:68
  181.8 0.1 copy.16
  182.0 1.3 copy-done
  183.3 1.5 slice.74
  184.8 1.7 reshape.138
  186.6 3.5 %gather_fusion = f32[1024,256]{1,0:T(8,128)S(1)} fusion(f32[2048,256]{1,0:T(8,128)S(1)} %reshape.138, s32[1024]{0:T(1024)S(1)} %broadcast_clamp_fusion), kind=kCustom, calls=%fused_computation | custom fusion | bytes 2101248 | tf_op jit(solution)/shard_map/gather | solution.py:95
  190.0 0.0 copy-start.3
  190.0 5.2 %collective-permute-start = (f32[1024,256]{1,0:T(8,128)S(1)}, f32[1024,256]{1,0:T(8,128)S(1)}, u32[]{:S(2)}, u32[]{:S(2)}) collective-permute-start(f32[1024,256]{1,0:T(8,128)S(1)} %gather_fusion), channel_id=1, source_target_pairs={{0,1},{1,0},{2,3},{3,2},{4,5},{5,4},{6,7},{7,6},{8,9},{9,8},{10,11... | collective-permute-start | bytes 3145736 | tf_op jit(solution)/shard_map/ppermute | solution.py:71
  195.3 0.8 slice.75
  196.1 0.1 reshape.139
  196.2 6.1 %gather_fusion.1 = f32[1024]{0:T(1024)S(1)} fusion(f32[2048]{0:T(1024)S(1)} %reshape.139, s32[1024]{0:T(1024)S(1)} %broadcast_clamp_fusion), kind=kCustom, calls=%fused_computation.1 | custom fusion | bytes 12288 | tf_op jit(solution)/shard_map/gather | solution.py:96
  202.4 0.1 collective-permute-start.1
  202.5 1.1 collective-permute-done.1
  203.6 0.0 collective-permute-done
  203.6 0.0 copy-done.3
  203.7 1.9 fusion.7
  205.6 36.3 %all_to_all.27 = bf16[128,16,256]{2,1,0:T(8,128)(2,1)S(1)} all-to-all(bf16[128,16,256]{2,1,0:T(8,128)(2,1)S(1)} %bitcast.46), channel_id=1, replica_groups=mesh['gx'=128,'ta'=2] {'gx'}, dimensions={0} | all-to-all | bytes 2097152 | tf_op jit(solution)/shard_map/all_to_all | solution.py:68
  241.8 0.7 fusion.33
  242.6 0.7 fusion.34
  243.3 0.1 copy-done.10
  243.4 0.7 fusion.35
  244.1 0.2 copy-done.12
  244.3 0.7 fusion.36
  245.0 0.1 pad_maximum_fusion.2
  245.2 56.0 %all_to_all.28 = f32[128,16,256]{2,1,0:T(8,128)S(1)} all-to-all(f32[128,16,256]{2,1,0:T(8,128)S(1)} %bitcast.31), channel_id=1, replica_groups=mesh['gx'=128,'ta'=2] {'gx'}, dimensions={0} | all-to-all | bytes 4194304 | tf_op jit(solution)/shard_map/all_to_all | solution.py:68
  301.2 3.5 %gather_fusion.2 = f32[1024,256]{1,0:T(8,128)S(1)} fusion(f32[2048,256]{1,0:T(8,128)S(1)} %bitcast.28, s32[1024]{0:T(1024)S(1)} %broadcast_clamp_fusion), kind=kCustom, calls=%fused_computation.2 | custom fusion | bytes 2101248 | tf_op jit(solution)/shard_map/gather | solution.py:106
  304.6 4.9 %collective-permute-start.2 = (f32[1024,256]{1,0:T(8,128)S(1)}, f32[1024,256]{1,0:T(8,128)S(1)}, u32[]{:S(2)}, u32[]{:S(2)}) collective-permute-start(f32[1024,256]{1,0:T(8,128)S(1)} %gather_fusion.2), channel_id=1, source_target_pairs={{0,1},{1,0},{2,3},{3,2},{4,5},{5,4},{6,7},{7,6},{8,9},{9,8},{10,11... | collective-permute-start | bytes 3145736 | tf_op jit(solution)/shard_map/ppermute | solution.py:71
  309.6 2.3 collective-permute-done.2
  311.8 2.3 divide_add_fusion
  (24 shorter events, 0.1 us)
Async XLA Ops:
  0.0 6.7 %copy-start.2 = (bf16[1024,256]{1,0:T(8,128)(2,1)S(1)}, bf16[1024,256]{1,0:T(8,128)(2,1)}, u32[]{:S(2)}) copy-start(bf16[1024,256]{1,0:T(8,128)(2,1)} %param.6) | copy-start | bytes 1572868
  15.0 1.7 copy-start.1
  16.7 87.2 %all-to-all-start = ((bf16[128,16,768]{2,1,0:T(8,128)(2,1)}), bf16[128,16,768]{2,1,0:T(8,128)(2,1)S(1)}, u32[]{:S(2)}, u32[]{:S(2)}) async-start(bf16[128,16,768]{2,1,0:T(8,128)(2,1)} %bitcast.41), calls=%async_computation | async-start | bytes 6291456 | tf_op jit(solution)/shard_map/all_to_all | solution.py:68
  105.6 2.5 copy-start.5
  108.1 2.5 copy-start.7
  110.6 2.5 copy-start.9
  113.1 1.3 copy-start.11
  121.0 10.9 %copy-start.4 = (s32[1,1024,1]{1,2,0:T(1,128)S(1)}, s32[1,1024,1]{1,2,0:T(1,128)}, u32[]{:S(2)}) copy-start(s32[1,1024,1]{1,2,0:T(1,128)} %param.7) | copy-start | bytes 12292
  121.0 60.8 %all-to-all-start.1 = ((f32[128,1,4224]{2,1,0:T(1,128)}), f32[128,1,4224]{2,1,0:T(1,128)S(1)}, u32[]{:S(2)}, u32[]{:S(2)}) async-start(f32[128,1,4224]{2,1,0:T(1,128)} %all_to_all.18), calls=%async_computation.1 | async-start | bytes 4325376 | tf_op jit(solution)/shard_map/all_to_all | solution.py:68
  182.0 1.4 copy-start
  190.0 13.6 %copy-start.3 = (bf16[1024,256]{1,0:T(8,128)(2,1)S(1)}, bf16[1024,256]{1,0:T(8,128)(2,1)}, u32[]{:S(2)}) copy-start(bf16[1024,256]{1,0:T(8,128)(2,1)} %param.6) | copy-start | bytes 1572868
  190.0 13.6 %collective-permute-start = (f32[1024,256]{1,0:T(8,128)S(1)}, f32[1024,256]{1,0:T(8,128)S(1)}, u32[]{:S(2)}, u32[]{:S(2)}) collective-permute-start(f32[1024,256]{1,0:T(8,128)S(1)} %gather_fusion), channel_id=1, source_target_pairs={{0,1},{1,0},{2,3},{3,2},{4,5},{5,4},{6,7},{7,6},{8,9},{9,8},{10,11... | collective-permute-start | bytes 3145736 | tf_op jit(solution)/shard_map/ppermute | solution.py:71
  202.4 1.3 collective-permute-start.1
  203.6 38.2 %copy-start.6 = (bf16[512,2048]{1,0:T(8,128)(2,1)S(1)}, bf16[512,2048]{1,0:T(8,128)(2,1)}, u32[]{:S(2)}) copy-start(bf16[512,2048]{1,0:T(8,128)(2,1)} %copy-done.5) | copy-start | bytes 6291460
  205.5 37.0 %copy-start.8 = (bf16[512,2048]{1,0:T(8,128)(2,1)S(1)}, bf16[512,2048]{1,0:T(8,128)(2,1)}, u32[]{:S(2)}) copy-start(bf16[512,2048]{1,0:T(8,128)(2,1)} %copy-done.7) | copy-start | bytes 6291460
  241.8 1.6 copy-start.10
  242.6 1.7 copy-start.12
  304.6 7.2 %collective-permute-start.2 = (f32[1024,256]{1,0:T(8,128)S(1)}, f32[1024,256]{1,0:T(8,128)S(1)}, u32[]{:S(2)}, u32[]{:S(2)}) collective-permute-start(f32[1024,256]{1,0:T(8,128)S(1)} %gather_fusion.2), channel_id=1, source_target_pairs={{0,1},{1,0},{2,3},{3,2},{4,5},{5,4},{6,7},{7,6},{8,9},{9,8},{10,11... | collective-permute-start | bytes 3145736 | tf_op jit(solution)/shard_map/ppermute | solution.py:71
where the time goes:
time: 315 us; the launch traced here: 314 us
  waiting for transfers between devices  124 us (39%)
  blocking collectives  92.2 us (29%)
  starting transfers between devices  37.7 us (12%)
  local copies, waits for them, and re-layouts  28.7 us (9%)
  matrix products  18.3 us (6%)
  other arithmetic  12.9 us (4%)
    all_to_all x2, waiting for transfers between devices, exchange(): return lax.all_to_all(buffer, 'gx', split_axis=0, concat_axis=0, tiled=True)  120 us
    all_to_all x2, blocking collectives, exchange(): return lax.all_to_all(buffer, 'gx', split_axis=0, concat_axis=0, tiled=True)  92.2 us
    all_to_all x2, starting transfers between devices, exchange(): return lax.all_to_all(buffer, 'gx', split_axis=0, concat_axis=0, tiled=True)  27.4 us
    ppermute x3, starting transfers between devices, other_core(): return lax.ppermute(values, 'ta', perm=[(0, 1), (1, 0)])  10.3 us
    dot_general x4, matrix products, bucket_weights(): lax.dot_general(unit[start:start + block], unit, (((1,), (1,)), ((), ()))...  6.76 us
  transfers between devices with their start and end apart: 5, of which 4 were waited for; matrix products, arithmetic and copies ran while one was open for 2% of the time, Pallas kernels for 0%

commit v1 on v0

--- a/solution.py
+++ b/solution.py
@@ -1,6 +1,8 @@
 import jax
 import jax.numpy as jnp
 from jax import lax
+from jax.experimental import pallas as pl
+from jax.experimental.pallas import tpu as pltpu
 from jax.sharding import PartitionSpec as P
 
 CAP = 2048
@@ -16,6 +18,65 @@
     return (wide * lax.rsqrt(jnp.sum(wide * wide, axis=1, keepdims=True) + 1e-06)).astype(
         jnp.bfloat16
     )
+
+
+def a2a_kernel(x_ref, o_ref, send_sem, recv_sem, local_sem):
+    n = x_ref.shape[0]
+    me = lax.axis_index("gx")
+    core = lax.axis_index("ta")
+    mesh_ids = pl.DeviceIdType.MESH
+    barrier = pltpu.get_barrier_semaphore()
+
+    def greet(i, carry):
+        peer = lax.rem(me + 1 + i, n)
+        pl.semaphore_signal(barrier, 1, device_id=(peer, core), device_id_type=mesh_ids)
+        return carry
+
+    lax.fori_loop(0, n - 1, greet, 0)
+    pl.semaphore_wait(barrier, n - 1)
+    local = pltpu.make_async_copy(x_ref.at[me], o_ref.at[me], local_sem)
+    local.start()
+
+    def copy_with(peer, block_from, block_to):
+        return pltpu.make_async_remote_copy(
+            x_ref.at[block_from],
+            o_ref.at[block_to],
+            send_sem.at[block_from],
+            recv_sem.at[block_to],
+            device_id=(peer, core),
+            device_id_type=mesh_ids,
+        )
+
+    def send(i, carry):
+        peer = lax.rem(me + 1 + i, n)
+        copy_with(peer, peer, me).start()
+        return carry
+
+    lax.fori_loop(0, n - 1, send, 0)
+
+    def finish(i, carry):
+        peer = lax.rem(me + 1 + i, n)
+        copy_with(peer, peer, me).wait_send()
+        copy_with(peer, peer, peer).wait_recv()
+        return carry
+
+    lax.fori_loop(0, n - 1, finish, 0)
+    local.wait()
+
+
+def all_to_all(x, collective_id):
+    return pl.pallas_call(
+        a2a_kernel,
+        out_shape=jax.ShapeDtypeStruct(x.shape, x.dtype),
+        in_specs=[pl.BlockSpec(memory_space=pl.ANY)],
+        out_specs=pl.BlockSpec(memory_space=pl.ANY),
+        scratch_shapes=[
+            pltpu.SemaphoreType.DMA((x.shape[0],)),
+            pltpu.SemaphoreType.DMA((x.shape[0],)),
+            pltpu.SemaphoreType.DMA(()),
+        ],
+        compiler_params=pltpu.CompilerParams(collective_id=collective_id, has_side_effects=True),
+    )(x)
 
 
 def bucket_weights(unit, valid):
@@ -64,8 +125,11 @@
     def place(payload):
         return jnp.dot(place_mat, payload, preferred_element_type=jnp.float32).astype(payload.dtype)
 
+    calls = []
+
     def exchange(buffer):
-        return lax.all_to_all(buffer, "gx", split_axis=0, concat_axis=0, tiled=True)
+        calls.append(None)
+        return all_to_all(buffer, len(calls) - 1)
 
     def other_core(values):
         return lax.ppermute(values, "ta", perm=[(0, 1), (1, 0)])

time: 315 us -> 327 us (1.038)
  Pallas kernels: 0 us -> 249 us
  waiting for transfers between devices: 124 us -> 3.43 us
  blocking collectives: 92.2 us -> 0 us
  starting transfers between devices: 37.7 us -> 1.92 us
  matrix products: 18.3 us -> 26.2 us
    pallas_call x0 -> x4, Pallas kernels: none -> 249 us  [all_to_all(): pl.pallas_call(a2a_kernel, out_shape=jax.ShapeDtypeStruct(x.shape, x.dtyp...]
    all_to_all x2 -> x0, waiting for transfers between devices: 120 us -> none  [exchange(): return lax.all_to_all(buffer, 'gx', split_axis=0, concat_axis=0, tiled=True)]
    all_to_all x2 -> x0, blocking collectives: 92.2 us -> none  [exchange(): return lax.all_to_all(buffer, 'gx', split_axis=0, concat_axis=0, tiled=True)]
    all_to_all x2 -> x0, starting transfers between devices: 27.4 us -> none  [exchange(): return lax.all_to_all(buffer, 'gx', split_axis=0, concat_axis=0, tiled=True)]
    ppermute x3, starting transfers between devices: 10.3 us -> 1.92 us  [other_core(): return lax.ppermute(values, 'ta', perm=[(0, 1), (1, 0)])]
    dot_general x8, matrix products: 5.74 us -> 9.44 us  [weighted_sums(): jnp.dot(w, feats, preferred_element_type=jnp.float32)]
  transfers between devices with their start and end apart: 5 -> 3, of which waited for: 4 -> 2; matrix products, arithmetic and copies ran while one was open for 2% -> 2% of each run, Pallas kernels for 0% -> 0%
where the time goes in v1:
time: 327 us; the launch traced here: 324 us
  Pallas kernels  249 us (76%)
  local copies, waits for them, and re-layouts  28 us (9%)
  matrix products  26.2 us (8%)
  other arithmetic  14.3 us (4%)
  waiting for transfers between devices  3.43 us (1%)
    pallas_call x4, Pallas kernels, all_to_all(): pl.pallas_call(a2a_kernel, out_shape=jax.ShapeDtypeStruct(x.shape, x.dtyp...  249 us
    dot_general x8, matrix products, weighted_sums(): jnp.dot(w, feats, preferred_element_type=jnp.float32)  9.44 us
    dot_general x4, matrix products, bucket_weights(): lax.dot_general(unit[start:start + block], unit, (((1,), (1,)), ((), ()))...  8.76 us
    dot_general x2, matrix products, place(): jnp.dot(place_mat, payload, preferred_element_type=jnp.float32)  8 us
  transfers between devices with their start and end apart: 3, of which 2 were waited for; matrix products, arithmetic and copies ran while one was open for 2% of the time, Pallas kernels for 0%

profile of v1, /device:TPU:1, one launch (start us, length us, event | category | flops | bytes accessed | tf_op | source)
XLA Modules:
  0.0 323.7 jit_solution(634497348331843830)
XLA Ops:
  0.0 0.7 compare_reduce_fusion
  0.7 1.3 convert_reduce_fusion.5
  2.0 0.7 multiply_add_fusion
  2.7 1.5 fusion.8
  4.2 1.5 fusion.9
  5.7 0.9 convert_reduce_fusion
  6.7 0.0 copy-done.3
  6.7 4.0 %fusion.6 = bf16[2048,768]{1,0:T(8,128)(2,1)S(1)} fusion(s32[1024]{0:T(1024)S(1)} %multiply_add_fusion, bf16[1024,256]{1,0:T(8,128)(2,1)S(1)} %copy-done.3, bf16[1024,512]{1,0:T(8,128)(2,1)S(1)} %fusion.9), kind=kOutput, calls=%fused_computation.25 | convolution fusion | flops 3228041216 | bytes 4722688 | tf_op jit(solution)/shard_map/dot_general | solution.py:126
  10.7 1.8 fusion.17
  12.5 2.5 scatter.4
  15.0 0.0 copy-start.1
  15.0 1.7 copy-done.1
  16.7 85.2 %shard_map.37 = bf16[128,16,768]{2,1,0:T(8,128)(2,1)} custom-call(bf16[128,16,768]{2,1,0:T(8,128)(2,1)} %bitcast.37), custom_call_target="tpu_custom_call" | custom-call | tf_op jit(solution)/shard_map/pallas_call | solution.py:68
  101.9 1.1 slice.69
  103.0 0.2 copy.15
  103.2 0.0 copy-start
  103.3 3.4 %convert_reduce_fusion.4 = (f32[512]{0:T(512)S(1)}, bf16[512,2048]{1,0:T(8,128)(2,1)S(1)}) fusion(f32[2048]{0:T(1024)S(1)} %bitcast.47, bf16[2048,768]{1,0:T(8,128)(2,1)} %bitcast.29), kind=kOutput, calls=%fused_computation.11 | convolution fusion | flops 1081081344 | bytes 4728832 | tf_op jit(solution)/shard_map/dot_general | solution.py:89
  106.6 0.0 copy-done
  106.6 0.7 fusion.24
  107.4 1.8 convert_reduce_fusion.3
  109.2 0.0 copy-done.6
  109.2 0.0 copy-start.7
  109.2 0.7 fusion.22
  109.9 1.8 convert_reduce_fusion.2
  111.7 0.0 copy-done.7
  111.7 0.0 copy-start.8
  111.7 0.7 fusion.20
  112.4 1.8 convert_reduce_fusion.1
  114.2 0.0 copy-done.8
  114.2 0.0 copy-start.10
  114.3 0.7 fusion.18
  115.0 0.6 copy-done.10
  115.6 1.5 pad_maximum_fusion.1
  117.1 1.7 reshape.135
  118.8 0.1 concatenate.28
  118.9 0.1 concatenate.29
  119.0 0.1 concatenate.30
  119.0 0.1 concatenate.31
  119.2 1.5 pad_maximum_fusion.x_ref
  120.6 64.1 %shard_map.38 = f32[128,4224]{1,0:T(8,128)} custom-call(f32[128,4224]{1,0:T(8,128)} %pad_maximum_fusion.x_ref), custom_call_target="tpu_custom_call" | custom-call | tf_op jit(solution)/shard_map/pallas_call | solution.py:68
  184.8 3.1 slice.58
  187.9 1.7 reshape.136
  189.6 0.0 slice-start
  189.6 3.5 %gather_fusion = f32[1024,256]{1,0:T(8,128)S(1)} fusion(f32[2048,256]{1,0:T(8,128)S(1)} %reshape.136, s32[1024]{0:T(1024)S(1)} %broadcast_clamp_fusion), kind=kCustom, calls=%fused_computation | custom fusion | bytes 2101248 | tf_op jit(solution)/shard_map/gather | solution.py:159
  193.1 0.0 copy-start.4
  193.1 0.6 collective-permute-start
  193.7 0.1 reshape.137
  193.7 6.4 %gather_fusion.1 = f32[1024]{0:T(1024)S(1)} fusion(f32[2048]{0:T(1024)S(1)} %reshape.137, s32[1024]{0:T(1024)S(1)} %broadcast_clamp_fusion), kind=kCustom, calls=%fused_computation.1 | custom fusion | bytes 12288 | tf_op jit(solution)/shard_map/gather | solution.py:160
  200.1 0.1 collective-permute-start.1
  200.2 1.1 collective-permute-done.1
  201.4 0.0 collective-permute-done
  201.4 0.0 copy-done.4
  201.4 4.0 %fusion.7 = bf16[2048,256]{1,0:T(8,128)(2,1)} fusion(s32[1024]{0:T(1024)S(1)} %multiply_add_fusion, f32[1024,256]{1,0:T(8,128)S(1)} %gather_fusion, f32[1024,256]{1,0:T(8,128)} %collective-permute-done, bf16[1024,256]{1,0:T(8,128)(2,1)S(1)} %copy-done.4, f32[1024]{0:T(1024)S(1)} %add_add_fusion), kind=kOutput, calls=%fused_computation.28 | convolution fusion | flops 1078198272 | bytes 3678208 | tf_op jit(solution)/shard_map/dot_general | solution.py:126
  205.4 38.8 %shard_map.39 = bf16[128,16,256]{2,1,0:T(8,128)(2,1)} custom-call(bf16[128,16,256]{2,1,0:T(8,128)(2,1)} %bitcast.42), custom_call_target="tpu_custom_call" | custom-call | tf_op jit(solution)/shard_map/pallas_call | solution.py:68
  244.2 2.7 fusion.33
  247.0 2.4 fusion.34
  249.4 0.7 fusion.35
  250.2 0.7 fusion.36
  250.9 1.5 pad_maximum_fusion.2
  252.4 61.5 %shard_map.40 = f32[128,16,256]{2,1,0:T(8,128)} custom-call(f32[128,16,256]{2,1,0:T(8,128)} %bitcast.27), custom_call_target="tpu_custom_call" | custom-call | tf_op jit(solution)/shard_map/pallas_call | solution.py:68
  313.8 5.1 %gather_fusion.2 = f32[1024,256]{1,0:T(8,128)S(1)} fusion(f32[2048,256]{1,0:T(8,128)} %bitcast.26, s32[1024]{0:T(1024)S(1)} %broadcast_clamp_fusion), kind=kCustom, calls=%fused_computation.2 | custom fusion | bytes 2101248 | tf_op jit(solution)/shard_map/gather | solution.py:170
  318.9 1.2 collective-permute-start.2
  320.1 2.3 collective-permute-done.2
  322.4 1.3 divide_add_fusion
  (21 shorter events, 0.1 us)
Async XLA Ops:
  0.0 6.7 %copy-start.3 = (bf16[1024,256]{1,0:T(8,128)(2,1)S(1)}, bf16[1024,256]{1,0:T(8,128)(2,1)}, u32[]{:S(2)}) copy-start(bf16[1024,256]{1,0:T(8,128)(2,1)} %param.6) | copy-start | bytes 1572868
  15.0 1.7 copy-start.1
  103.2 3.4 %copy-start = (bf16[128,16,768]{2,1,0:T(8,128)(2,1)S(1)}, bf16[128,16,768]{2,1,0:T(8,128)(2,1)}, u32[]{:S(2)}) copy-start(bf16[128,16,768]{2,1,0:T(8,128)(2,1)} %shard_map.37) | copy-start | bytes 9437188
  106.6 2.5 copy-start.6
  109.2 2.5 copy-start.7
  111.7 2.5 copy-start.8
  114.2 1.3 copy-start.10
  120.6 64.1 %copy-start.5 = (s32[1,1024,1]{1,2,0:T(1,128)S(1)}, s32[1,1024,1]{1,2,0:T(1,128)}, u32[]{:S(2)}) copy-start(s32[1,1024,1]{1,2,0:T(1,128)} %param.7) | copy-start | bytes 12292
  189.6 4.1 %slice-start = ((f32[128,4224]{1,0:T(8,128)}), f32[128,16]{1,0:T(8,128)S(1)}, s32[]{:S(2)}) async-start(f32[128,4224]{1,0:T(8,128)} %shard_map.38), calls=%async_computation | async-start | bytes 131072 | tf_op jit(solution)/shard_map/slice | solution.py:158
  193.1 8.3 %copy-start.4 = (bf16[1024,256]{1,0:T(8,128)(2,1)S(1)}, bf16[1024,256]{1,0:T(8,128)(2,1)}, u32[]{:S(2)}) copy-start(bf16[1024,256]{1,0:T(8,128)(2,1)} %param.6) | copy-start | bytes 1572868
  193.1 8.3 %collective-permute-start = (f32[1024,256]{1,0:T(8,128)S(1)}, f32[1024,256]{1,0:T(8,128)}, u32[]{:S(2)}, u32[]{:S(2)}) collective-permute-start(f32[1024,256]{1,0:T(8,128)S(1)} %gather_fusion), channel_id=1, source_target_pairs={{0,1},{1,0},{2,3},{3,2},{4,5},{5,4},{6,7},{7,6},{8,9},{9,8},{10,11... | collective-permute-start | bytes 3145736 | tf_op jit(solution)/shard_map/ppermute | solution.py:135
  200.1 1.3 collective-permute-start.1
  244.2 2.7 copy-start.2
  244.2 5.2 %copy-start.9 = (bf16[512,2048]{1,0:T(8,128)(2,1)S(1)}, bf16[512,2048]{1,0:T(8,128)(2,1)}, u32[]{:S(2)}) copy-start(bf16[512,2048]{1,0:T(8,128)(2,1)} %copy-done.8) | copy-start | bytes 6291460
  247.0 3.2 copy-start.11
  318.9 3.5 %collective-permute-start.2 = (f32[1024,256]{1,0:T(8,128)S(1)}, f32[1024,256]{1,0:T(8,128)S(1)}, u32[]{:S(2)}, u32[]{:S(2)}) collective-permute-start(f32[1024,256]{1,0:T(8,128)S(1)} %gather_fusion.2), channel_id=1, source_target_pairs={{0,1},{1,0},{2,3},{3,2},{4,5},{5,4},{6,7},{7,6},{8,9},{9,8},{10,11... | collective-permute-start | bytes 3145736 | tf_op jit(solution)/shard_map/ppermute | solution.py:135

commit v2 on v1

--- a/solution.py
+++ b/solution.py
@@ -125,20 +125,18 @@
     def place(payload):
         return jnp.dot(place_mat, payload, preferred_element_type=jnp.float32).astype(payload.dtype)
 
-    calls = []
-
     def exchange(buffer):
-        calls.append(None)
-        return all_to_all(buffer, len(calls) - 1)
+        return lax.all_to_all(buffer, "gx", split_axis=0, concat_axis=0, tiled=True)
 
     def other_core(values):
         return lax.ppermute(values, "ta", perm=[(0, 1), (1, 0)])
 
     unit_here = normalize(embeddings)
     placed = place(jnp.concatenate([unit_here, labels], axis=1))
-    mark = jnp.where(occupied, placed[:, unit_here.shape[1]], PAD_MARK)
-    placed = placed.at[:, unit_here.shape[1]].set(mark.astype(jnp.bfloat16))
-    got = exchange(placed.reshape(groups, slot, -1)).reshape(groups * slot, -1)
+    column = lax.broadcasted_iota(jnp.int32, placed.shape, 1)
+    pad_here = (column == unit_here.shape[1]) & ~occupied[:, None]
+    placed = jnp.where(pad_here, jnp.bfloat16(PAD_MARK), placed)
+    got = all_to_all(placed.reshape(groups, slot, -1), 0).reshape(groups * slot, -1)
     unit = got[:, : unit_here.shape[1]]
     feats0 = got[:, unit_here.shape[1] :]
     valid = (feats0[:, 0].astype(jnp.float32) > PAD_MARK * 0.5).astype(jnp.float32)
@@ -157,7 +155,7 @@
     back_num = back[:, : slot * width_l].reshape(groups * slot, width_l)
     back_den = back[:, slot * width_l : slot * width_l + slot].reshape(groups * slot)
     row_num = back_num[target]
-    row_den = back_den[target]
+    row_den = jnp.broadcast_to(back_den[:, None], (groups * slot, 128))[target][:, 0]
     other_num, other_den = other_core((row_num, row_den))
     total_num = row_num + other_num
     total_den = row_den + other_den

time: 327 us -> 319 us (0.976)
  Pallas kernels: 249 us -> 85.1 us
  blocking collectives: 0 us -> 92.1 us
  waiting for transfers between devices: 3.43 us -> 53.4 us
  starting transfers between devices: 1.92 us -> 26.9 us
  other arithmetic: 14.3 us -> 10.2 us
  matrix products: 26.2 us -> 22.9 us
    pallas_call x4 -> x1, Pallas kernels: 249 us -> 85.1 us  [all_to_all(): pl.pallas_call(a2a_kernel, out_shape=jax.ShapeDtypeStruct(x.shape, x.dtyp...]
    all_to_all x0 -> x2, blocking collectives: none -> 92.1 us  [exchange(): return lax.all_to_all(buffer, 'gx', split_axis=0, concat_axis=0, tiled=True)]
    all_to_all x0 -> x1, waiting for transfers between devices: none -> 50 us  [exchange(): return lax.all_to_all(buffer, 'gx', split_axis=0, concat_axis=0, tiled=True)]
    all_to_all x0 -> x1, starting transfers between devices: none -> 16.7 us  [exchange(): return lax.all_to_all(buffer, 'gx', split_axis=0, concat_axis=0, tiled=True)]
    ppermute x3, starting transfers between devices: 1.92 us -> 10.2 us  [other_core(): return lax.ppermute(values, 'ta', perm=[(0, 1), (1, 0)])]
    unnamed x25 -> x28, local copies, waits for them, and re-layouts: 2.56 us -> 6.81 us
    dot_general x8, matrix products: 9.44 us -> 5.69 us  [weighted_sums(): jnp.dot(w, feats, preferred_element_type=jnp.float32)]
    gather x1, local copies, waits for them, and re-layouts: 6.37 us -> 2.81 us  [body(): jnp.broadcast_to(back_den[:, None], (groups * slot, 128))[target][:, 0]]
  transfers between devices with their start and end apart: 3 -> 4, of which waited for: 2 -> 3; matrix products, arithmetic and copies ran while one was open for 2% -> 1% of each run, Pallas kernels for 0% -> 0%
where the time goes in v2:
time: 319 us; the launch traced here: 318 us
  blocking collectives  92.1 us (29%)
  Pallas kernels  85.1 us (27%)
  waiting for transfers between devices  53.4 us (17%)
  local copies, waits for them, and re-layouts  27.4 us (9%)
  starting transfers between devices  26.9 us (8%)
  matrix products  22.9 us (7%)
  other arithmetic  10.2 us (3%)
    all_to_all x2, blocking collectives, exchange(): return lax.all_to_all(buffer, 'gx', split_axis=0, concat_axis=0, tiled=True)  92.1 us
    pallas_call x1, Pallas kernels, all_to_all(): pl.pallas_call(a2a_kernel, out_shape=jax.ShapeDtypeStruct(x.shape, x.dtyp...  85.1 us
    all_to_all x1, waiting for transfers between devices, exchange(): return lax.all_to_all(buffer, 'gx', split_axis=0, concat_axis=0, tiled=True)  50 us
    all_to_all x1, starting transfers between devices, exchange(): return lax.all_to_all(buffer, 'gx', split_axis=0, concat_axis=0, tiled=True)  16.7 us
    ppermute x3, starting transfers between devices, other_core(): return lax.ppermute(values, 'ta', perm=[(0, 1), (1, 0)])  10.2 us
    dot_general x4, matrix products, bucket_weights(): lax.dot_general(unit[start:start + block], unit, (((1,), (1,)), ((), ()))...  8.76 us
    dot_general x2, matrix products, place(): jnp.dot(place_mat, payload, preferred_element_type=jnp.float32)  8.48 us
    unnamed x28, local copies, waits for them, and re-layouts  6.81 us
  transfers between devices with their start and end apart: 4, of which 3 were waited for; matrix products, arithmetic and copies ran while one was open for 1% of the time, Pallas kernels for 0%

profile of v2, /device:TPU:1, one launch (start us, length us, event | category | flops | bytes accessed | tf_op | source)
XLA Modules:
  0.0 318.4 jit_solution(10786164305414576948)
XLA Ops:
  0.0 1.3 convert_reduce_fusion.5
  1.3 0.7 multiply_add_fusion
  2.0 0.9 convert_reduce_fusion
  3.0 1.5 fusion.8
  4.5 1.5 fusion.9
  6.0 0.0 copy-done.2
  6.0 5.3 %and_select_fusion = bf16[2048,768]{1,0:T(8,128)(2,1)} fusion(pred[768]{0:T(1024)(128)(4,1)S(1)} %iota_compare_fusion.15, pred[2048]{0:T(1024)(128)(4,1)S(1)} %compare_not_fusion, s32[1024]{0:T(1024)S(1)} %multiply_add_fusion, bf16[1024,256]{1,0:T(8,128)(2,1)S(1)} %copy-done.2, bf16[1024,512]{1,0:T(8,128)(2,1)S(1)} %fusion.9), kind=kOutput, calls=%fused_computation.8 | convolution fusion | flops 3231186944 | bytes 4725504 | tf_op jit(solution)/shard_map/dot_general | solution.py:126
  11.3 85.1 %shard_map.37 = bf16[128,16,768]{2,1,0:T(8,128)(2,1)} custom-call(bf16[128,16,768]{2,1,0:T(8,128)(2,1)} %bitcast.42), custom_call_target="tpu_custom_call" | custom-call | tf_op jit(solution)/shard_map/pallas_call | solution.py:68
  96.4 1.1 slice.53
  97.5 0.2 copy.13
  97.8 0.0 copy-start.1
  97.8 3.4 %convert_reduce_fusion.4 = (f32[512]{0:T(512)S(1)}, bf16[512,2048]{1,0:T(8,128)(2,1)S(1)}) fusion(f32[2048]{0:T(1024)S(1)} %bitcast.52, bf16[2048,768]{1,0:T(8,128)(2,1)} %bitcast.34), kind=kOutput, calls=%fused_computation.12 | convolution fusion | flops 1081081344 | bytes 4728832 | tf_op jit(solution)/shard_map/dot_general | solution.py:89
  101.1 0.7 fusion.23
  101.9 0.6 copy-done.5
  102.5 1.8 convert_reduce_fusion.3
  104.3 0.7 fusion.21
  105.0 0.6 copy-done.7
  105.6 1.8 convert_reduce_fusion.2
  107.4 0.7 fusion.19
  108.2 0.6 copy-done.9
  108.8 1.8 convert_reduce_fusion.1
  110.6 0.7 fusion.17
  111.3 0.6 copy-done.11
  111.9 1.5 pad_maximum_fusion.1
  113.4 1.9 reshape.108
  115.3 0.1 concatenate.26
  115.4 0.1 concatenate.27
  115.5 0.1 concatenate.28
  115.6 0.1 concatenate.29
  115.7 0.2 pad_maximum_fusion
  115.8 2.9 all_to_all.14
  118.7 16.7 %all-to-all-start = ((f32[128,1,4224]{2,1,0:T(1,128)}), f32[128,1,4224]{2,1,0:T(1,128)S(1)}, u32[]{:S(2)}, u32[]{:S(2)}) async-start(f32[128,1,4224]{2,1,0:T(1,128)} %all_to_all.14), calls=%async_computation | async-start | bytes 4325376 | tf_op jit(solution)/shard_map/all_to_all | solution.py:129
  135.5 50.0 %all-to-all-done = f32[128,1,4224]{2,1,0:T(1,128)S(1)} async-done(((f32[128,1,4224]{2,1,0:T(1,128)}), f32[128,1,4224]{2,1,0:T(1,128)S(1)}, u32[]{:S(2)}, u32[]{:S(2)}) %all-to-all-start) | async-done | bytes 2162720 | tf_op jit(solution)/shard_map/all_to_all | solution.py:129
  185.4 0.1 copy.15
  185.6 0.0 copy-start
  185.6 1.4 copy-done
  187.0 1.5 slice.58
  188.5 1.7 reshape.109
  190.2 3.5 %gather_fusion = f32[1024,256]{1,0:T(8,128)S(1)} fusion(f32[2048,256]{1,0:T(8,128)S(1)} %reshape.109, s32[1024]{0:T(1024)S(1)} %broadcast_clamp_fusion), kind=kCustom, calls=%fused_computation | custom fusion | bytes 2101248 | tf_op jit(solution)/shard_map/gather | solution.py:157
  193.7 5.1 %collective-permute-start = (f32[1024,256]{1,0:T(8,128)S(1)}, f32[1024,256]{1,0:T(8,128)}, u32[]{:S(2)}, u32[]{:S(2)}) collective-permute-start(f32[1024,256]{1,0:T(8,128)S(1)} %gather_fusion), channel_id=1, source_target_pairs={{0,1},{1,0},{2,3},{3,2},{4,5},{5,4},{6,7},{7,6},{8,9},{9,8},{10,11... | collective-permute-start | bytes 3145736 | tf_op jit(solution)/shard_map/ppermute | solution.py:132
  198.8 0.8 slice.59
  199.7 0.1 broadcast_in_dim.9
  199.8 0.3 broadcast_in_dim.10
  200.1 0.0 copy-start.3
  200.1 2.8 gather_fusion.1
  202.9 0.2 slice_reduce_fusion
  203.1 0.1 collective-permute-start.1
  203.2 1.2 collective-permute-done.1
  204.4 0.0 collective-permute-done
  204.4 3.2 %fusion.7 = bf16[2048,256]{1,0:T(8,128)(2,1)S(1)} fusion(s32[1024]{0:T(1024)S(1)} %multiply_add_fusion, f32[1024,256]{1,0:T(8,128)S(1)} %gather_fusion, f32[1024,256]{1,0:T(8,128)} %collective-permute-done, bf16[1024,256]{1,0:T(8,128)(2,1)S(1)} %copy-done.3, f32[1024]{0:T(1024)S(1)} %add_add_fusion), kind=kOutput, calls=%fused_computation.29 | convolution fusion | flops 1078198272 | bytes 3678208 | tf_op jit(solution)/shard_map/dot_general | solution.py:126
  207.6 36.1 %all_to_all.22 = bf16[128,16,256]{2,1,0:T(8,128)(2,1)S(1)} all-to-all(bf16[128,16,256]{2,1,0:T(8,128)(2,1)S(1)} %bitcast.47), channel_id=1, replica_groups=mesh['gx'=128,'ta'=2] {'gx'}, dimensions={0} | all-to-all | bytes 2097152 | tf_op jit(solution)/shard_map/all_to_all | solution.py:129
  243.8 0.7 fusion.32
  244.5 0.9 copy-done.8
  245.4 0.7 fusion.33
  246.1 0.9 copy-done.10
  246.9 0.7 fusion.34
  247.7 0.9 copy-done.12
  248.5 0.7 fusion.35
  249.2 0.1 pad_maximum_fusion.2
  249.4 56.0 %all_to_all.23 = f32[128,16,256]{2,1,0:T(8,128)S(1)} all-to-all(f32[128,16,256]{2,1,0:T(8,128)S(1)} %bitcast.32), channel_id=1, replica_groups=mesh['gx'=128,'ta'=2] {'gx'}, dimensions={0} | all-to-all | bytes 4194304 | tf_op jit(solution)/shard_map/all_to_all | solution.py:129
  305.4 3.5 %gather_fusion.2 = f32[1024,256]{1,0:T(8,128)S(1)} fusion(f32[2048,256]{1,0:T(8,128)S(1)} %bitcast.29, s32[1024]{0:T(1024)S(1)} %broadcast_clamp_fusion), kind=kCustom, calls=%fused_computation.2 | custom fusion | bytes 2101248 | tf_op jit(solution)/shard_map/gather | solution.py:168
  308.8 4.9 %collective-permute-start.2 = (f32[1024,256]{1,0:T(8,128)S(1)}, f32[1024,256]{1,0:T(8,128)S(1)}, u32[]{:S(2)}, u32[]{:S(2)}) collective-permute-start(f32[1024,256]{1,0:T(8,128)S(1)} %gather_fusion.2), channel_id=1, source_target_pairs={{0,1},{1,0},{2,3},{3,2},{4,5},{5,4},{6,7},{7,6},{8,9},{9,8},{10,11... | collective-permute-start | bytes 3145736 | tf_op jit(solution)/shard_map/ppermute | solution.py:132
  313.8 2.3 collective-permute-done.2
  316.1 2.3 divide_add_fusion
  (25 shorter events, 0.1 us)
Async XLA Ops:
  0.0 6.0 %copy-start.2 = (bf16[1024,256]{1,0:T(8,128)(2,1)S(1)}, bf16[1024,256]{1,0:T(8,128)(2,1)}, u32[]{:S(2)}) copy-start(bf16[1024,256]{1,0:T(8,128)(2,1)} %param.4) | copy-start | bytes 1572868
  97.8 3.4 %copy-start.1 = (bf16[128,16,768]{2,1,0:T(8,128)(2,1)S(1)}, bf16[128,16,768]{2,1,0:T(8,128)(2,1)}, u32[]{:S(2)}) copy-start(bf16[128,16,768]{2,1,0:T(8,128)(2,1)} %shard_map.37) | copy-start | bytes 9437188
  101.1 1.4 copy-start.5
  104.3 1.4 copy-start.7
  107.4 1.3 copy-start.9
  110.6 1.3 copy-start.11
  118.7 16.7 %copy-start.4 = (s32[1,1024,1]{1,2,0:T(1,128)S(1)}, s32[1,1024,1]{1,2,0:T(1,128)}, u32[]{:S(2)}) copy-start(s32[1,1024,1]{1,2,0:T(1,128)} %param.5) | copy-start | bytes 12292
  118.7 66.7 %all-to-all-start = ((f32[128,1,4224]{2,1,0:T(1,128)}), f32[128,1,4224]{2,1,0:T(1,128)S(1)}, u32[]{:S(2)}, u32[]{:S(2)}) async-start(f32[128,1,4224]{2,1,0:T(1,128)} %all_to_all.14), calls=%async_computation | async-start | bytes 4325376 | tf_op jit(solution)/shard_map/all_to_all | solution.py:129
  185.6 1.4 copy-start
  193.7 10.7 %collective-permute-start = (f32[1024,256]{1,0:T(8,128)S(1)}, f32[1024,256]{1,0:T(8,128)}, u32[]{:S(2)}, u32[]{:S(2)}) collective-permute-start(f32[1024,256]{1,0:T(8,128)S(1)} %gather_fusion), channel_id=1, source_target_pairs={{0,1},{1,0},{2,3},{3,2},{4,5},{5,4},{6,7},{7,6},{8,9},{9,8},{10,11... | collective-permute-start | bytes 3145736 | tf_op jit(solution)/shard_map/ppermute | solution.py:132
  200.1 4.3 %copy-start.3 = (bf16[1024,256]{1,0:T(8,128)(2,1)S(1)}, bf16[1024,256]{1,0:T(8,128)(2,1)}, u32[]{:S(2)}) copy-start(bf16[1024,256]{1,0:T(8,128)(2,1)} %param.4) | copy-start | bytes 1572868
  203.1 1.3 collective-permute-start.1
  204.4 39.4 %copy-start.6 = (bf16[512,2048]{1,0:T(8,128)(2,1)S(1)}, bf16[512,2048]{1,0:T(8,128)(2,1)}, u32[]{:S(2)}) copy-start(bf16[512,2048]{1,0:T(8,128)(2,1)} %copy-done.5) | copy-start | bytes 6291460
  243.8 1.6 copy-start.8
  245.4 1.6 copy-start.10
  246.9 1.6 copy-start.12
  308.8 7.2 %collective-permute-start.2 = (f32[1024,256]{1,0:T(8,128)S(1)}, f32[1024,256]{1,0:T(8,128)S(1)}, u32[]{:S(2)}, u32[]{:S(2)}) collective-permute-start(f32[1024,256]{1,0:T(8,128)S(1)} %gather_fusion.2), channel_id=1, source_target_pairs={{0,1},{1,0},{2,3},{3,2},{4,5},{5,4},{6,7},{7,6},{8,9},{9,8},{10,11... | collective-permute-start | bytes 3145736 | tf_op jit(solution)/shard_map/ppermute | solution.py:132

commit v3 on v2

--- a/solution.py
+++ b/solution.py
@@ -1,3 +1,5 @@
+import functools
+
 import jax
 import jax.numpy as jnp
 from jax import lax
@@ -20,8 +22,11 @@
     )
 
 
-def a2a_kernel(x_ref, o_ref, send_sem, recv_sem, local_sem):
-    n = x_ref.shape[0]
+def a2a_kernel(count, *refs):
+    x_refs = refs[:count]
+    o_refs = refs[count : 2 * count]
+    send_sem, recv_sem, local_sem = refs[2 * count :]
+    n = x_refs[0].shape[0]
     me = lax.axis_index("gx")
     core = lax.axis_index("ta")
     mesh_ids = pl.DeviceIdType.MESH
@@ -34,49 +39,58 @@
 
     lax.fori_loop(0, n - 1, greet, 0)
     pl.semaphore_wait(barrier, n - 1)
-    local = pltpu.make_async_copy(x_ref.at[me], o_ref.at[me], local_sem)
-    local.start()
+    locals_ = [
+        pltpu.make_async_copy(x.at[me], o.at[me], local_sem.at[k])
+        for k, (x, o) in enumerate(zip(x_refs, o_refs))
+    ]
+    for local in locals_:
+        local.start()
 
-    def copy_with(peer, block_from, block_to):
+    def copy_with(k, peer, block_from, block_to):
         return pltpu.make_async_remote_copy(
-            x_ref.at[block_from],
-            o_ref.at[block_to],
-            send_sem.at[block_from],
-            recv_sem.at[block_to],
+            x_refs[k].at[block_from],
+            o_refs[k].at[block_to],
+            send_sem.at[k, block_from],
+            recv_sem.at[k, block_to],
             device_id=(peer, core),
             device_id_type=mesh_ids,
         )
 
     def send(i, carry):
         peer = lax.rem(me + 1 + i, n)
-        copy_with(peer, peer, me).start()
+        for k in range(count):
+            copy_with(k, peer, peer, me).start()
         return carry
 
     lax.fori_loop(0, n - 1, send, 0)
 
     def finish(i, carry):
         peer = lax.rem(me + 1 + i, n)
-        copy_with(peer, peer, me).wait_send()
-        copy_with(peer, peer, peer).wait_recv()
+        for k in range(count):
+            copy_with(k, peer, peer, me).wait_send()
+            copy_with(k, peer, peer, peer).wait_recv()
         return carry
 
     lax.fori_loop(0, n - 1, finish, 0)
-    local.wait()
+    for local in locals_:
+        local.wait()
 
 
-def all_to_all(x, collective_id):
+def all_to_all(arrays, collective_id):
+    count = len(arrays)
+    n = arrays[0].shape[0]
     return pl.pallas_call(
-        a2a_kernel,
-        out_shape=jax.ShapeDtypeStruct(x.shape, x.dtype),
-        in_specs=[pl.BlockSpec(memory_space=pl.ANY)],
-        out_specs=pl.BlockSpec(memory_space=pl.ANY),
+        functools.partial(a2a_kernel, count),
+        out_shape=[jax.ShapeDtypeStruct(x.shape, x.dtype) for x in arrays],
+        in_specs=[pl.BlockSpec(memory_space=pl.ANY)] * count,
+        out_specs=[pl.BlockSpec(memory_space=pl.ANY)] * count,
         scratch_shapes=[
-            pltpu.SemaphoreType.DMA((x.shape[0],)),
-            pltpu.SemaphoreType.DMA((x.shape[0],)),
-            pltpu.SemaphoreType.DMA(()),
+            pltpu.SemaphoreType.DMA((count, n)),
+            pltpu.SemaphoreType.DMA((count, n)),
+            pltpu.SemaphoreType.DMA((count,)),
         ],
         compiler_params=pltpu.CompilerParams(collective_id=collective_id, has_side_effects=True),
-    )(x)
+    )(*arrays)
 
 
 def bucket_weights(unit, valid):
@@ -136,7 +150,7 @@
     column = lax.broadcasted_iota(jnp.int32, placed.shape, 1)
     pad_here = (column == unit_here.shape[1]) & ~occupied[:, None]
     placed = jnp.where(pad_here, jnp.bfloat16(PAD_MARK), placed)
-    got = all_to_all(placed.reshape(groups, slot, -1), 0).reshape(groups * slot, -1)
+    got = exchange(placed.reshape(groups, slot, -1)).reshape(groups * slot, -1)
     unit = got[:, : unit_here.shape[1]]
     feats0 = got[:, unit_here.shape[1] :]
     valid = (feats0[:, 0].astype(jnp.float32) > PAD_MARK * 0.5).astype(jnp.float32)
@@ -144,16 +158,9 @@
     blocks, den = bucket_weights(unit, valid)
     num1 = weighted_sums(blocks, feats0)
 
-    packed = jnp.concatenate(
-        [
-            num1.reshape(groups, slot * width_l),
-            jnp.pad(den.reshape(groups, slot), ((0, 0), (0, 128 - slot))),
-        ],
-        axis=1,
-    )
-    back = exchange(packed)
-    back_num = back[:, : slot * width_l].reshape(groups * slot, width_l)
-    back_den = back[:, slot * width_l : slot * width_l + slot].reshape(groups * slot)
+    back_num, back_den = all_to_all([num1.reshape(groups, slot, width_l), den.reshape(groups, slot)], 0)
+    back_num = back_num.reshape(groups * slot, width_l)
+    back_den = back_den.reshape(groups * slot)
     row_num = back_num[target]
     row_den = jnp.broadcast_to(back_den[:, None], (groups * slot, 128))[target][:, 0]
     other_num, other_den = other_core((row_num, row_den))

time: 319 us -> 309 us (0.969)
  Pallas kernels: 85.1 us -> 61.2 us
  waiting for transfers between devices: 53.4 us -> 74 us
  local copies, waits for them, and re-layouts: 27.4 us -> 12.6 us
  blocking collectives: 92.1 us -> 99.5 us
    pallas_call x1, Pallas kernels: 85.1 us -> 61.2 us  [all_to_all(): pl.pallas_call(functools.partial(a2a_kernel, count), out_shape=[jax.Shape...]
    all_to_all x1, waiting for transfers between devices: 50 us -> 70.6 us  [exchange(): return lax.all_to_all(buffer, 'gx', split_axis=0, concat_axis=0, tiled=True)]
    all_to_all x2, blocking collectives: 92.1 us -> 99.5 us  [exchange(): return lax.all_to_all(buffer, 'gx', split_axis=0, concat_axis=0, tiled=True)]
    unnamed x28 -> x24, local copies, waits for them, and re-layouts: 6.81 us -> 0.35 us
    reshape x2 -> x0, local copies, waits for them, and re-layouts: 3.64 us -> none  [the longest x1 1.93 us: body(): num1.reshape(groups, slot * width_l)]
    slice x3 -> x0, local copies, waits for them, and re-layouts: 3.45 us -> none  [the longest x1 1.53 us: body(): back_num = back[:, :slot * width_l].reshape(groups * slot, width_l)]
    dot_general x8, matrix products: 5.69 us -> 8.95 us  [weighted_sums(): jnp.dot(w, feats, preferred_element_type=jnp.float32)]
where the time goes in v3:
time: 309 us
  blocking collectives  99.5 us (32%)
  waiting for transfers between devices  74 us (24%)
  Pallas kernels  61.2 us (20%)
  starting transfers between devices  24.7 us (8%)
  matrix products  24.2 us (8%)
  local copies, waits for them, and re-layouts  12.6 us (4%)
  other arithmetic  12.4 us (4%)
    all_to_all x2, blocking collectives, exchange(): return lax.all_to_all(buffer, 'gx', split_axis=0, concat_axis=0, tiled=True)  99.5 us
    all_to_all x1, waiting for transfers between devices, exchange(): return lax.all_to_all(buffer, 'gx', split_axis=0, concat_axis=0, tiled=True)  70.6 us
    pallas_call x1, Pallas kernels, all_to_all(): pl.pallas_call(functools.partial(a2a_kernel, count), out_shape=[jax.Shape...  61.2 us
    all_to_all x1, starting transfers between devices, exchange(): return lax.all_to_all(buffer, 'gx', split_axis=0, concat_axis=0, tiled=True)  16.7 us
    dot_general x8, matrix products, weighted_sums(): jnp.dot(w, feats, preferred_element_type=jnp.float32)  8.95 us
    dot_general x2, matrix products, place(): jnp.dot(place_mat, payload, preferred_element_type=jnp.float32)  8.48 us
    ppermute x3, starting transfers between devices, other_core(): return lax.ppermute(values, 'ta', perm=[(0, 1), (1, 0)])  8.08 us
    dot_general x4, matrix products, bucket_weights(): lax.dot_general(unit[start:start + block], unit, (((1,), (1,)), ((), ()))...  6.76 us
  transfers between devices with their start and end apart: 4, of which 3 were waited for; matrix products, arithmetic and copies ran while one was open for 1% of the time, Pallas kernels for 0%

profile of v3, /device:TPU:1, one launch (start us, length us, event | category | flops | bytes accessed | tf_op | source)
XLA Modules:
  0.0 308.9 jit_solution(18193739274363049150)
XLA Ops:
  0.0 0.0 copy-start
  0.0 1.3 convert_reduce_fusion.5
  1.3 0.7 multiply_add_fusion
  2.0 0.9 convert_reduce_fusion
  2.9 1.5 fusion.8
  4.4 1.5 fusion.9
  6.0 0.0 copy-done
  6.0 5.3 %and_select_fusion = bf16[2048,768]{1,0:T(8,128)(2,1)} fusion(pred[768]{0:T(1024)(128)(4,1)S(1)} %iota_compare_fusion.14, pred[2048]{0:T(1024)(128)(4,1)S(1)} %compare_not_fusion, s32[1024]{0:T(1024)S(1)} %multiply_add_fusion, bf16[1024,256]{1,0:T(8,128)(2,1)S(1)} %copy-done, bf16[1024,512]{1,0:T(8,128)(2,1)S(1)} %fusion.9), kind=kOutput, calls=%fused_computation.8 | convolution fusion | flops 3231186944 | bytes 4725504 | tf_op jit(solution)/shard_map/dot_general | solution.py:140
  11.2 0.0 copy-start.3
  11.2 16.7 %all-to-all-start = ((bf16[128,16,768]{2,1,0:T(8,128)(2,1)}), bf16[128,16,768]{2,1,0:T(8,128)(2,1)S(1)}, u32[]{:S(2)}, u32[]{:S(2)}) async-start(bf16[128,16,768]{2,1,0:T(8,128)(2,1)} %bitcast.40), calls=%async_computation | async-start | bytes 6291456 | tf_op jit(solution)/shard_map/all_to_all | solution.py:143
  27.9 0.0 copy-done.3
  28.0 70.6 %all-to-all-done = bf16[128,16,768]{2,1,0:T(8,128)(2,1)S(1)} async-done(((bf16[128,16,768]{2,1,0:T(8,128)(2,1)}), bf16[128,16,768]{2,1,0:T(8,128)(2,1)S(1)}, u32[]{:S(2)}, u32[]{:S(2)}) %all-to-all-start) | async-done | bytes 3145760 | tf_op jit(solution)/shard_map/all_to_all | solution.py:143
  98.6 0.2 convert_reduce_fusion.6
  98.8 1.5 convert_reduce_fusion.4
  100.3 1.8 convert_reduce_fusion.1
  102.1 1.5 fusion.17
  103.6 1.8 convert_reduce_fusion.2
  105.3 0.0 copy-done.6
  105.4 0.0 copy-start.8
  105.4 1.5 fusion.19
  106.9 1.8 convert_reduce_fusion.3
  108.7 0.0 copy-done.8
  108.7 0.0 copy-start.10
  108.7 1.5 fusion.21
  110.2 0.0 copy-done.4
  110.2 1.5 fusion.23
  111.7 0.0 copy-done.10
  111.7 0.1 concatenate.26
  111.8 0.1 concatenate.25
  111.9 0.1 concatenate.24
  112.0 0.1 concatenate.23
  112.1 3.1 pad_maximum_fusion
  115.1 0.6 pad_maximum_fusion.2.refs_1_
  115.8 61.2 %shard_map.37 = (f32[128,16,256]{2,1,0:T(8,128)}, f32[128,16]{1,0:T(8,128)}) custom-call(f32[128,16,256]{2,1,0:T(8,128)} %bitcast.29, f32[128,16]{1,0:T(8,128)} %pad_maximum_fusion.2.refs_1_), custom_call_target="tpu_custom_call" | custom-call | tf_op jit(solution)/shard_map/pallas_call | solution.py:82
  176.9 0.0 copy-start.2
  176.9 5.1 %gather_fusion = f32[1024,256]{1,0:T(8,128)S(1)} fusion(f32[2048,256]{1,0:T(8,128)} %bitcast.28, s32[1024]{0:T(1024)S(1)} %broadcast_clamp_fusion), kind=kCustom, calls=%fused_computation | custom fusion | bytes 2101248 | tf_op jit(solution)/shard_map/gather | solution.py:164
  182.0 2.8 collective-permute-start
  184.8 0.0 copy-done.2
  184.8 0.1 broadcast_in_dim.9
  184.9 0.3 broadcast_in_dim.10
  185.2 2.8 gather_fusion.1
  188.1 0.2 slice_reduce_fusion
  188.3 0.3 collective-permute-start.1
  188.6 1.1 collective-permute-done.1
  189.8 0.0 collective-permute-done
  189.8 0.0 copy-done.1
  189.8 3.2 %fusion.7 = bf16[2048,256]{1,0:T(8,128)(2,1)S(1)} fusion(s32[1024]{0:T(1024)S(1)} %multiply_add_fusion, f32[1024,256]{1,0:T(8,128)S(1)} %gather_fusion, f32[1024,256]{1,0:T(8,128)} %collective-permute-done, bf16[1024,256]{1,0:T(8,128)(2,1)S(1)} %copy-done.1, f32[1024]{0:T(1024)S(1)} %add_add_fusion), kind=kOutput, calls=%fused_computation.29 | convolution fusion | flops 1078198272 | bytes 3678208 | tf_op jit(solution)/shard_map/dot_general | solution.py:140
  193.0 0.0 copy-start.9
  193.0 43.5 %all_to_all.15 = bf16[128,16,256]{2,1,0:T(8,128)(2,1)S(1)} all-to-all(bf16[128,16,256]{2,1,0:T(8,128)(2,1)S(1)} %bitcast.45), channel_id=1, replica_groups=mesh['gx'=128,'ta'=2] {'gx'}, dimensions={0} | all-to-all | bytes 2097152 | tf_op jit(solution)/shard_map/all_to_all | solution.py:143
  236.5 0.0 copy-done.7
  236.5 0.7 fusion.35
  237.2 0.0 copy-done.9
  237.3 0.0 copy-start.5
  237.3 0.7 fusion.34
  238.0 0.1 copy-done.11
  238.1 0.7 fusion.33
  238.8 0.2 copy-done.5
  239.0 0.7 fusion.32
  239.7 0.1 pad_maximum_fusion.1
  239.9 56.0 %all_to_all.16 = f32[128,16,256]{2,1,0:T(8,128)S(1)} all-to-all(f32[128,16,256]{2,1,0:T(8,128)S(1)} %bitcast.30), channel_id=1, replica_groups=mesh['gx'=128,'ta'=2] {'gx'}, dimensions={0} | all-to-all | bytes 4194304 | tf_op jit(solution)/shard_map/all_to_all | solution.py:143
  295.8 3.5 %gather_fusion.2 = f32[1024,256]{1,0:T(8,128)S(1)} fusion(f32[2048,256]{1,0:T(8,128)S(1)} %bitcast.27, s32[1024]{0:T(1024)S(1)} %broadcast_clamp_fusion), kind=kCustom, calls=%fused_computation.2 | custom fusion | bytes 2101248 | tf_op jit(solution)/shard_map/gather | solution.py:175
  299.3 4.9 %collective-permute-start.2 = (f32[1024,256]{1,0:T(8,128)S(1)}, f32[1024,256]{1,0:T(8,128)S(1)}, u32[]{:S(2)}, u32[]{:S(2)}) collective-permute-start(f32[1024,256]{1,0:T(8,128)S(1)} %gather_fusion.2), channel_id=1, source_target_pairs={{0,1},{1,0},{2,3},{3,2},{4,5},{5,4},{6,7},{7,6},{8,9},{9,8},{10,11... | collective-permute-start | bytes 3145736 | tf_op jit(solution)/shard_map/ppermute | solution.py:146
  304.2 2.3 collective-permute-done.2
  306.5 2.3 divide_add_fusion
  (14 shorter events, 0.1 us)
Async XLA Ops:
  0.0 6.0 %copy-start = (bf16[1024,256]{1,0:T(8,128)(2,1)S(1)}, bf16[1024,256]{1,0:T(8,128)(2,1)}, u32[]{:S(2)}) copy-start(bf16[1024,256]{1,0:T(8,128)(2,1)} %param.4) | copy-start | bytes 1572868
  11.2 16.7 %copy-start.3 = (s32[1,1024,1]{1,2,0:T(1,128)S(1)}, s32[1,1024,1]{1,2,0:T(1,128)}, u32[]{:S(2)}) copy-start(s32[1,1024,1]{1,2,0:T(1,128)} %param.5) | copy-start | bytes 12292
  11.2 87.3 %all-to-all-start = ((bf16[128,16,768]{2,1,0:T(8,128)(2,1)}), bf16[128,16,768]{2,1,0:T(8,128)(2,1)S(1)}, u32[]{:S(2)}, u32[]{:S(2)}) async-start(bf16[128,16,768]{2,1,0:T(8,128)(2,1)} %bitcast.40), calls=%async_computation | async-start | bytes 6291456 | tf_op jit(solution)/shard_map/all_to_all | solution.py:143
  100.3 9.9 %copy-start.4 = (bf16[512,2048]{1,0:T(8,128)(2,1)}, bf16[512,2048]{1,0:T(8,128)(2,1)S(1)}, u32[]{:S(2)}) copy-start(bf16[512,2048]{1,0:T(8,128)(2,1)S(1)} %get-tuple-element.16) | copy-start | bytes 6291460
  102.1 3.3 %copy-start.6 = (bf16[512,2048]{1,0:T(8,128)(2,1)}, bf16[512,2048]{1,0:T(8,128)(2,1)S(1)}, u32[]{:S(2)}) copy-start(bf16[512,2048]{1,0:T(8,128)(2,1)S(1)} %get-tuple-element.10) | copy-start | bytes 6291460
  105.4 3.3 %copy-start.8 = (bf16[512,2048]{1,0:T(8,128)(2,1)}, bf16[512,2048]{1,0:T(8,128)(2,1)S(1)}, u32[]{:S(2)}) copy-start(bf16[512,2048]{1,0:T(8,128)(2,1)S(1)} %get-tuple-element.12) | copy-start | bytes 6291460
  108.7 3.1 copy-start.10
  176.9 7.9 %copy-start.2 = (f32[128,16]{1,0:T(8,128)S(1)}, f32[128,16]{1,0:T(8,128)}, u32[]{:S(2)}) copy-start(f32[128,16]{1,0:T(8,128)} %get-tuple-element.8) | copy-start | bytes 24580
  182.0 7.7 %collective-permute-start = (f32[1024,256]{1,0:T(8,128)S(1)}, f32[1024,256]{1,0:T(8,128)}, u32[]{:S(2)}, u32[]{:S(2)}) collective-permute-start(f32[1024,256]{1,0:T(8,128)S(1)} %gather_fusion), channel_id=1, source_target_pairs={{0,1},{1,0},{2,3},{3,2},{4,5},{5,4},{6,7},{7,6},{8,9},{9,8},{10,11... | collective-permute-start | bytes 3145736 | tf_op jit(solution)/shard_map/ppermute | solution.py:146
  184.9 4.9 %copy-start.1 = (bf16[1024,256]{1,0:T(8,128)(2,1)S(1)}, bf16[1024,256]{1,0:T(8,128)(2,1)}, u32[]{:S(2)}) copy-start(bf16[1024,256]{1,0:T(8,128)(2,1)} %param.4) | copy-start | bytes 1572868
  188.3 1.5 collective-permute-start.1
  189.8 46.8 %copy-start.7 = (bf16[512,2048]{1,0:T(8,128)(2,1)S(1)}, bf16[512,2048]{1,0:T(8,128)(2,1)}, u32[]{:S(2)}) copy-start(bf16[512,2048]{1,0:T(8,128)(2,1)} %copy-done.6) | copy-start | bytes 6291460
  193.0 44.3 %copy-start.9 = (bf16[512,2048]{1,0:T(8,128)(2,1)S(1)}, bf16[512,2048]{1,0:T(8,128)(2,1)}, u32[]{:S(2)}) copy-start(bf16[512,2048]{1,0:T(8,128)(2,1)} %copy-done.8) | copy-start | bytes 6291460
  236.5 1.6 copy-start.11
  237.3 1.7 copy-start.5
  299.3 7.2 %collective-permute-start.2 = (f32[1024,256]{1,0:T(8,128)S(1)}, f32[1024,256]{1,0:T(8,128)S(1)}, u32[]{:S(2)}, u32[]{:S(2)}) collective-permute-start(f32[1024,256]{1,0:T(8,128)S(1)} %gather_fusion.2), channel_id=1, source_target_pairs={{0,1},{1,0},{2,3},{3,2},{4,5},{5,4},{6,7},{7,6},{8,9},{9,8},{10,11... | collective-permute-start | bytes 3145736 | tf_op jit(solution)/shard_map/ppermute | solution.py:146

commit v4 on v3

--- a/solution.py
+++ b/solution.py
@@ -95,7 +95,7 @@
 
 def bucket_weights(unit, valid):
     cap = unit.shape[0]
-    block = min(512, cap)
+    block = cap
     cols = jnp.arange(cap)
     blocks = []
     dens = []

time: 309 us -> 303 us (0.981)
  other arithmetic: 12.4 us -> 8.52 us
    concatenate x3 -> x0, other arithmetic: 3.84 us -> none  [the longest x2 3.2 us: weighted_sums(): jnp.concatenate([jnp.dot(w, feats, preferred_element_type=jnp.float32) fo...]
    dot_general x8 -> x2, matrix products: 8.95 us -> 6.43 us  [weighted_sums(): jnp.dot(w, feats, preferred_element_type=jnp.float32)]
    dot_general x4 -> x1, matrix products: 6.76 us -> 7.36 us  [bucket_weights(): lax.dot_general(unit[start:start + block], unit, (((1,), (1,)), ((), ()))...]
where the time goes in v4:
time: 303 us
  blocking collectives  99.4 us (33%)
  waiting for transfers between devices  74 us (24%)
  Pallas kernels  61.2 us (20%)
  starting transfers between devices  24.5 us (8%)
  matrix products  22.3 us (7%)
  local copies, waits for them, and re-layouts  12.7 us (4%)
  other arithmetic  8.52 us (3%)
    all_to_all x2, blocking collectives, exchange(): return lax.all_to_all(buffer, 'gx', split_axis=0, concat_axis=0, tiled=True)  99.4 us
    all_to_all x1, waiting for transfers between devices, exchange(): return lax.all_to_all(buffer, 'gx', split_axis=0, concat_axis=0, tiled=True)  70.6 us
    pallas_call x1, Pallas kernels, all_to_all(): pl.pallas_call(functools.partial(a2a_kernel, count), out_shape=[jax.Shape...  61.2 us
    all_to_all x1, starting transfers between devices, exchange(): return lax.all_to_all(buffer, 'gx', split_axis=0, concat_axis=0, tiled=True)  16.6 us
    dot_general x2, matrix products, place(): jnp.dot(place_mat, payload, preferred_element_type=jnp.float32)  8.48 us
    ppermute x3, starting transfers between devices, other_core(): return lax.ppermute(values, 'ta', perm=[(0, 1), (1, 0)])  7.88 us
    dot_general x1, matrix products, bucket_weights(): lax.dot_general(unit[start:start + block], unit, (((1,), (1,)), ((), ()))...  7.36 us
    dot_general x2, matrix products, weighted_sums(): jnp.dot(w, feats, preferred_element_type=jnp.float32)  6.43 us
  transfers between devices with their start and end apart: 4, of which 3 were waited for; matrix products, arithmetic and copies ran while one was open for 1% of the time, Pallas kernels for 0%

profile of v4, /device:TPU:1, one launch (start us, length us, event | category | flops | bytes accessed | tf_op | source)
XLA Modules:
  0.0 302.8 jit_solution(13681685336455590401)
XLA Ops:
  0.0 0.0 copy-start
  0.0 1.3 convert_reduce_fusion.2
  1.3 0.7 multiply_add_fusion
  2.0 1.5 fusion.8
  3.5 0.9 convert_reduce_fusion.1
  4.4 1.5 fusion.9
  6.0 0.0 copy-done
  6.0 5.3 %and_select_fusion = bf16[2048,768]{1,0:T(8,128)(2,1)} fusion(pred[768]{0:T(1024)(128)(4,1)S(1)} %iota_compare_fusion.11, pred[2048]{0:T(1024)(128)(4,1)S(1)} %compare_not_fusion, s32[1024]{0:T(1024)S(1)} %multiply_add_fusion, bf16[1024,256]{1,0:T(8,128)(2,1)S(1)} %copy-done, bf16[1024,512]{1,0:T(8,128)(2,1)S(1)} %fusion.9), kind=kOutput, calls=%fused_computation.11 | convolution fusion | flops 3231186944 | bytes 4725504 | tf_op jit(solution)/shard_map/dot_general | solution.py:140
  11.2 0.0 copy-start.3
  11.2 16.6 %all-to-all-start = ((bf16[128,16,768]{2,1,0:T(8,128)(2,1)}), bf16[128,16,768]{2,1,0:T(8,128)(2,1)S(1)}, u32[]{:S(2)}, u32[]{:S(2)}) async-start(bf16[128,16,768]{2,1,0:T(8,128)(2,1)} %bitcast.25), calls=%async_computation | async-start | bytes 6291456 | tf_op jit(solution)/shard_map/all_to_all | solution.py:143
  27.9 0.0 copy-done.3
  27.9 70.6 %all-to-all-done = bf16[128,16,768]{2,1,0:T(8,128)(2,1)S(1)} async-done(((bf16[128,16,768]{2,1,0:T(8,128)(2,1)}), bf16[128,16,768]{2,1,0:T(8,128)(2,1)S(1)}, u32[]{:S(2)}, u32[]{:S(2)}) %all-to-all-start) | async-done | bytes 3145760 | tf_op jit(solution)/shard_map/all_to_all | solution.py:143
  98.6 0.2 convert_reduce_fusion.3
  98.8 7.4 %convert_reduce_fusion = (f32[2048]{0:T(1024)S(1)}, bf16[2048,2048]{1,0:T(8,128)(2,1)S(1)}) fusion(f32[2048]{0:T(1024)S(1)} %convert_reduce_fusion.3, bf16[2048,768]{1,0:T(8,128)(2,1)S(1)} %bitcast.23), kind=kOutput, calls=%fused_computation.3 | convolution fusion | flops 4324325376 | bytes 10502144 | tf_op jit(solution)/shard_map/dot_general | solution.py:103
  106.2 0.0 copy-start.4
  106.2 4.0 %fusion.14 = f32[2048,256]{1,0:T(8,128)} fusion(bf16[2048,2048]{1,0:T(8,128)(2,1)S(1)} %get-tuple-element.10, bf16[2048,768]{1,0:T(8,128)(2,1)S(1)} %bitcast.24), kind=kOutput, calls=%fused_computation.27 | convolution fusion | flops 2147483648 | bytes 11534336 | tf_op jit(solution)/shard_map/dot_general | solution.py:120
  110.2 0.0 copy-done.4
  110.2 0.7 reshape.92.refs_1_
  110.9 61.2 %shard_map.37 = (f32[128,16,256]{2,1,0:T(8,128)}, f32[128,16]{1,0:T(8,128)}) custom-call(f32[128,16,256]{2,1,0:T(8,128)} %bitcast.26, f32[128,16]{1,0:T(8,128)} %reshape.92.refs_1_), custom_call_target="tpu_custom_call" | custom-call | tf_op jit(solution)/shard_map/pallas_call | solution.py:82
  172.0 0.0 copy-start.2
  172.1 5.1 %gather_fusion = f32[1024,256]{1,0:T(8,128)S(1)} fusion(f32[2048,256]{1,0:T(8,128)} %bitcast.21, s32[1024]{0:T(1024)S(1)} %broadcast_clamp_fusion), kind=kCustom, calls=%fused_computation | custom fusion | bytes 2101248 | tf_op jit(solution)/shard_map/gather | solution.py:164
  177.1 2.8 collective-permute-start
  180.0 0.0 copy-done.2
  180.0 0.1 broadcast_in_dim.9
  180.1 0.0 copy-start.1
  180.1 0.3 broadcast_in_dim.10
  180.4 2.8 gather_fusion.1
  183.2 0.2 slice_reduce_fusion
  183.4 0.1 collective-permute-start.1
  183.5 1.1 collective-permute-done.1
  184.7 0.0 slice-start
  184.7 0.0 slice-start.1
  184.7 0.0 collective-permute-done
  184.7 0.0 copy-done.1
  184.7 3.2 %fusion.7 = bf16[2048,256]{1,0:T(8,128)(2,1)S(1)} fusion(s32[1024]{0:T(1024)S(1)} %multiply_add_fusion, f32[1024,256]{1,0:T(8,128)S(1)} %gather_fusion, f32[1024,256]{1,0:T(8,128)} %collective-permute-done, bf16[1024,256]{1,0:T(8,128)(2,1)S(1)} %copy-done.1, f32[1024]{0:T(1024)S(1)} %add_add_fusion), kind=kOutput, calls=%fused_computation.20 | convolution fusion | flops 1078198272 | bytes 3678208 | tf_op jit(solution)/shard_map/dot_general | solution.py:140
  187.9 43.4 %all_to_all.15 = bf16[128,16,256]{2,1,0:T(8,128)(2,1)S(1)} all-to-all(bf16[128,16,256]{2,1,0:T(8,128)(2,1)S(1)} %bitcast.27), channel_id=1, replica_groups=mesh['gx'=128,'ta'=2] {'gx'}, dimensions={0} | all-to-all | bytes 2097152 | tf_op jit(solution)/shard_map/all_to_all | solution.py:143
  231.3 0.0 slice-done
  231.3 0.0 slice-done.1
  231.3 2.5 fusion.19
  233.8 56.0 %all_to_all.16 = f32[128,16,256]{2,1,0:T(8,128)S(1)} all-to-all(f32[128,16,256]{2,1,0:T(8,128)S(1)} %fusion.19), channel_id=1, replica_groups=mesh['gx'=128,'ta'=2] {'gx'}, dimensions={0} | all-to-all | bytes 4194304 | tf_op jit(solution)/shard_map/all_to_all | solution.py:143
  289.8 3.5 %gather_fusion.2 = f32[1024,256]{1,0:T(8,128)S(1)} fusion(f32[2048,256]{1,0:T(8,128)S(1)} %bitcast.20, s32[1024]{0:T(1024)S(1)} %broadcast_clamp_fusion), kind=kCustom, calls=%fused_computation.2 | custom fusion | bytes 2101248 | tf_op jit(solution)/shard_map/gather | solution.py:175
  293.2 4.9 %collective-permute-start.2 = (f32[1024,256]{1,0:T(8,128)S(1)}, f32[1024,256]{1,0:T(8,128)S(1)}, u32[]{:S(2)}, u32[]{:S(2)}) collective-permute-start(f32[1024,256]{1,0:T(8,128)S(1)} %gather_fusion.2), channel_id=1, source_target_pairs={{0,1},{1,0},{2,3},{3,2},{4,5},{5,4},{6,7},{7,6},{8,9},{9,8},{10,11... | collective-permute-start | bytes 3145736 | tf_op jit(solution)/shard_map/ppermute | solution.py:146
  298.2 2.3 collective-permute-done.2
  300.4 2.3 divide_add_fusion
  (7 shorter events, 0.0 us)
Async XLA Ops:
  0.0 6.0 %copy-start = (bf16[1024,256]{1,0:T(8,128)(2,1)S(1)}, bf16[1024,256]{1,0:T(8,128)(2,1)}, u32[]{:S(2)}) copy-start(bf16[1024,256]{1,0:T(8,128)(2,1)} %param.4) | copy-start | bytes 1572868
  11.2 16.7 %copy-start.3 = (s32[1,1024,1]{1,2,0:T(1,128)S(1)}, s32[1,1024,1]{1,2,0:T(1,128)}, u32[]{:S(2)}) copy-start(s32[1,1024,1]{1,2,0:T(1,128)} %param.5) | copy-start | bytes 12292
  11.2 87.3 %all-to-all-start = ((bf16[128,16,768]{2,1,0:T(8,128)(2,1)}), bf16[128,16,768]{2,1,0:T(8,128)(2,1)S(1)}, u32[]{:S(2)}, u32[]{:S(2)}) async-start(bf16[128,16,768]{2,1,0:T(8,128)(2,1)} %bitcast.25), calls=%async_computation | async-start | bytes 6291456 | tf_op jit(solution)/shard_map/all_to_all | solution.py:143
  106.2 4.0 %copy-start.4 = (bf16[2048,2048]{1,0:T(8,128)(2,1)}, bf16[2048,2048]{1,0:T(8,128)(2,1)S(1)}, u32[]{:S(2)}) copy-start(bf16[2048,2048]{1,0:T(8,128)(2,1)S(1)} %get-tuple-element.10) | copy-start | bytes 25165828
  172.0 7.9 %copy-start.2 = (f32[128,16]{1,0:T(8,128)S(1)}, f32[128,16]{1,0:T(8,128)}, u32[]{:S(2)}) copy-start(f32[128,16]{1,0:T(8,128)} %get-tuple-element.8) | copy-start | bytes 24580
  177.1 7.5 %collective-permute-start = (f32[1024,256]{1,0:T(8,128)S(1)}, f32[1024,256]{1,0:T(8,128)}, u32[]{:S(2)}, u32[]{:S(2)}) collective-permute-start(f32[1024,256]{1,0:T(8,128)S(1)} %gather_fusion), channel_id=1, source_target_pairs={{0,1},{1,0},{2,3},{3,2},{4,5},{5,4},{6,7},{7,6},{8,9},{9,8},{10,11... | collective-permute-start | bytes 3145736 | tf_op jit(solution)/shard_map/ppermute | solution.py:146
  180.1 4.6 %copy-start.1 = (bf16[1024,256]{1,0:T(8,128)(2,1)S(1)}, bf16[1024,256]{1,0:T(8,128)(2,1)}, u32[]{:S(2)}) copy-start(bf16[1024,256]{1,0:T(8,128)(2,1)} %param.4) | copy-start | bytes 1572868
  183.4 1.3 collective-permute-start.1
  184.7 46.6 %slice-start = ((s8[8388608]{0:T(1024)(128)(4,1)}), s8[4194304]{0:T(1024)(128)(4,1)S(1)}, s32[]{:S(2)}) async-start(s8[8388608]{0:T(1024)(128)(4,1)} %bitcast.33), calls=%async_computation.3 | async-start | bytes 8388608
  184.7 46.6 %slice-start.1 = ((s8[8388608]{0:T(1024)(128)(4,1)}), s8[4194304]{0:T(1024)(128)(4,1)S(1)}, s32[]{:S(2)}) async-start(s8[8388608]{0:T(1024)(128)(4,1)} %bitcast.33), calls=%async_computation.4 | async-start | bytes 8388608
  293.2 7.2 %collective-permute-start.2 = (f32[1024,256]{1,0:T(8,128)S(1)}, f32[1024,256]{1,0:T(8,128)S(1)}, u32[]{:S(2)}, u32[]{:S(2)}) collective-permute-start(f32[1024,256]{1,0:T(8,128)S(1)} %gather_fusion.2), channel_id=1, source_target_pairs={{0,1},{1,0},{2,3},{3,2},{4,5},{5,4},{6,7},{7,6},{8,9},{9,8},{10,11... | collective-permute-start | bytes 3145736 | tf_op jit(solution)/shard_map/ppermute | solution.py:146

commit v5 on v4

--- a/solution.py
+++ b/solution.py
@@ -146,13 +146,14 @@
         return lax.ppermute(values, "ta", perm=[(0, 1), (1, 0)])
 
     unit_here = normalize(embeddings)
-    placed = place(jnp.concatenate([unit_here, labels], axis=1))
-    column = lax.broadcasted_iota(jnp.int32, placed.shape, 1)
-    pad_here = (column == unit_here.shape[1]) & ~occupied[:, None]
-    placed = jnp.where(pad_here, jnp.bfloat16(PAD_MARK), placed)
-    got = exchange(placed.reshape(groups, slot, -1)).reshape(groups * slot, -1)
-    unit = got[:, : unit_here.shape[1]]
-    feats0 = got[:, unit_here.shape[1] :]
+    placed_l = place(labels)
+    column = lax.broadcasted_iota(jnp.int32, placed_l.shape, 1)
+    placed_l = jnp.where((column == 0) & ~occupied[:, None], jnp.bfloat16(PAD_MARK), placed_l)
+    unit, feats0 = all_to_all(
+        [place(unit_here).reshape(groups, slot, -1), placed_l.reshape(groups, slot, -1)], 1
+    )
+    unit = unit.reshape(groups * slot, -1)
+    feats0 = feats0.reshape(groups * slot, -1)
     valid = (feats0[:, 0].astype(jnp.float32) > PAD_MARK * 0.5).astype(jnp.float32)
 
     blocks, den = bucket_weights(unit, valid)
@@ -169,7 +170,7 @@
     scale = (1.0 + total_den)[:, None]
     first = (1.0 - alpha_mix) * prior + alpha_mix * total_num / scale
 
-    feats1 = exchange(place(first.astype(jnp.bfloat16)).reshape(groups, slot, -1))
+    (feats1,) = all_to_all([place(first.astype(jnp.bfloat16)).reshape(groups, slot, -1)], 2)
     num2 = weighted_sums(blocks, feats1.reshape(groups * slot, -1))
     back2 = exchange(num2.reshape(groups, slot, -1)).reshape(groups * slot, -1)
     row_num2 = back2[target]

time: 303 us -> 326 us (1.076)
  Pallas kernels: 61.2 us -> 194 us
  waiting for transfers between devices: 74 us -> 3.44 us
  blocking collectives: 99.4 us -> 63.9 us
  starting transfers between devices: 24.5 us -> 5.98 us
  matrix products: 22.3 us -> 36.6 us
    pallas_call x1 -> x3, Pallas kernels: 61.2 us -> 194 us  [all_to_all(): pl.pallas_call(functools.partial(a2a_kernel, count), out_shape=[jax.Shape...]
    all_to_all x1 -> x0, waiting for transfers between devices: 70.6 us -> none  [exchange(): return lax.all_to_all(buffer, 'gx', split_axis=0, concat_axis=0, tiled=True)]
    all_to_all x2 -> x1, blocking collectives: 99.4 us -> 63.9 us  [exchange(): return lax.all_to_all(buffer, 'gx', split_axis=0, concat_axis=0, tiled=True)]
    all_to_all x1 -> x0, starting transfers between devices: 16.6 us -> none  [exchange(): return lax.all_to_all(buffer, 'gx', split_axis=0, concat_axis=0, tiled=True)]
    dot_general x2, matrix products: 6.43 us -> 13.2 us  [weighted_sums(): jnp.dot(w, feats, preferred_element_type=jnp.float32)]
    dot_general x1, matrix products: 7.36 us -> 11.8 us  [bucket_weights(): lax.dot_general(unit[start:start + block], unit, (((1,), (1,)), ((), ()))...]
    dot_general x2 -> x3, matrix products: 8.48 us -> 11.6 us  [place(): jnp.dot(place_mat, payload, preferred_element_type=jnp.float32)]
  transfers between devices with their start and end apart: 4 -> 3, of which waited for: 3 -> 2; matrix products, arithmetic and copies ran while one was open for 1% -> 1% of each run, Pallas kernels for 0% -> 0%
where the time goes in v5:
time: 326 us
  Pallas kernels  194 us (60%)
  blocking collectives  63.9 us (20%)
  matrix products  36.6 us (11%)
  local copies, waits for them, and re-layouts  14 us (4%)
  other arithmetic  7.47 us (2%)
  starting transfers between devices  5.98 us (2%)
  waiting for transfers between devices  3.44 us (1%)
    pallas_call x3, Pallas kernels, all_to_all(): pl.pallas_call(functools.partial(a2a_kernel, count), out_shape=[jax.Shape...  194 us
    all_to_all x1, blocking collectives, exchange(): return lax.all_to_all(buffer, 'gx', split_axis=0, concat_axis=0, tiled=True)  63.9 us
    dot_general x2, matrix products, weighted_sums(): jnp.dot(w, feats, preferred_element_type=jnp.float32)  13.2 us
    dot_general x1, matrix products, bucket_weights(): lax.dot_general(unit[start:start + block], unit, (((1,), (1,)), ((), ()))...  11.8 us
    dot_general x3, matrix products, place(): jnp.dot(place_mat, payload, preferred_element_type=jnp.float32)  11.6 us
  transfers between devices with their start and end apart: 3, of which 2 were waited for; matrix products, arithmetic and copies ran while one was open for 1% of the time, Pallas kernels for 0%

profile of v5, /device:TPU:1, one launch (start us, length us, event | category | flops | bytes accessed | tf_op | source)
XLA Modules:
  0.0 325.6 jit_solution(2182941594656168879)
XLA Ops:
  0.0 1.3 convert_reduce_fusion.2
  1.3 0.7 multiply_add_fusion
  2.0 0.7 compare_select_fusion
  2.7 1.5 fusion.12
  4.2 0.9 convert_reduce_fusion.1
  5.1 0.0 copy-start
  5.2 5.1 %fusion.8 = bf16[2048,512]{1,0:T(8,128)(2,1)} fusion(s32[1024]{0:T(1024)S(1)} %multiply_add_fusion, bf16[1024,512]{1,0:T(8,128)(2,1)} %param.3, f32[1024]{0:T(1024)S(1)} %add_rsqrt_fusion), kind=kOutput, calls=%fused_computation.18 | convolution fusion | flops 2152202240 | bytes 3153920 | tf_op jit(solution)/shard_map/dot_general | solution.py:140
  10.2 0.0 copy-done
  10.2 2.5 fusion.11
  12.8 89.0 %shard_map.37 = (bf16[128,16,512]{2,1,0:T(8,128)(2,1)}, bf16[128,16,256]{2,1,0:T(8,128)(2,1)}) custom-call(bf16[128,16,512]{2,1,0:T(8,128)(2,1)} %bitcast.30, bf16[128,16,256]{2,1,0:T(8,128)(2,1)} %bitcast.31), custom_call_target="tpu_custom_call" | custom-call | tf_op jit(solution)/shard_map/pallas_call | solution.py:82
  101.8 1.1 slice.14
  102.9 0.2 copy.14
  103.1 0.0 copy-start.1
  103.1 11.8 %convert_reduce_fusion = (f32[2048]{0:T(1024)S(1)}, bf16[2048,2048]{1,0:T(8,128)(2,1)}) fusion(f32[2048]{0:T(1024)S(1)} %bitcast.40, bf16[2048,512]{1,0:T(8,128)(2,1)} %bitcast.41), kind=kOutput, calls=%fused_computation.3 | convolution fusion | flops 4324325376 | bytes 10502144 | tf_op jit(solution)/shard_map/dot_general | solution.py:103
  114.9 0.7 reshape.98.refs_1_
  115.6 0.0 copy-done.1
  115.6 7.1 %fusion.18.refs_0_ = f32[128,16,256]{2,1,0:T(8,128)} fusion(bf16[128,16,2048]{2,1,0:T(8,128)(2,1)} %bitcast.42, bf16[2048,256,1]{1,0,2:T(8,128)(2,1)S(1)} %bitcast.35), kind=kOutput, calls=%fused_computation.42 | convolution fusion | flops 2147483648 | bytes 11534336 | tf_op jit(solution)/shard_map/dot_general | solution.py:120
  122.7 65.9 %shard_map.38 = (f32[128,16,256]{2,1,0:T(8,128)}, f32[128,16]{1,0:T(8,128)}) custom-call(f32[128,16,256]{2,1,0:T(8,128)} %fusion.18.refs_0_, f32[128,16]{1,0:T(8,128)} %reshape.98.refs_1_), custom_call_target="tpu_custom_call" | custom-call | tf_op jit(solution)/shard_map/pallas_call | solution.py:82
  188.6 0.0 copy-start.2
  188.6 5.1 %gather_fusion = f32[1024,256]{1,0:T(8,128)S(1)} fusion(f32[2048,256]{1,0:T(8,128)} %bitcast.29, s32[1024]{0:T(1024)S(1)} %broadcast_clamp_fusion), kind=kCustom, calls=%fused_computation | custom fusion | bytes 2101248 | tf_op jit(solution)/shard_map/gather | solution.py:165
  193.7 0.9 collective-permute-start
  194.7 0.0 copy-done.2
  194.7 0.1 broadcast_in_dim.9
  194.7 0.3 broadcast_in_dim.10
  195.1 2.8 gather_fusion.1
  197.9 0.2 slice_reduce_fusion
  198.1 0.3 collective-permute-start.1
  198.4 1.1 collective-permute-done.1
  199.6 0.0 collective-permute-done
  199.6 4.0 %fusion.10 = bf16[2048,256]{1,0:T(8,128)(2,1)} fusion(s32[1024]{0:T(1024)S(1)} %multiply_add_fusion, f32[1024,256]{1,0:T(8,128)S(1)} %gather_fusion, f32[1024,256]{1,0:T(8,128)} %collective-permute-done, bf16[1024,256]{1,0:T(8,128)(2,1)S(1)} %copy-done, f32[1024]{0:T(1024)S(1)} %add_add_fusion), kind=kOutput, calls=%fused_computation.22 | convolution fusion | flops 1078198272 | bytes 3678208 | tf_op jit(solution)/shard_map/dot_general | solution.py:140
  203.6 39.2 %shard_map.39 = bf16[128,16,256]{2,1,0:T(8,128)(2,1)} custom-call(bf16[128,16,256]{2,1,0:T(8,128)(2,1)} %bitcast.32), custom_call_target="tpu_custom_call" | custom-call | tf_op jit(solution)/shard_map/pallas_call | solution.py:82
  242.9 6.1 %fusion.19 = f32[128,16,256]{2,1,0:T(8,128)S(1)} fusion(bf16[128,16,2048]{2,1,0:T(8,128)(2,1)} %bitcast.43, bf16[2048,256,1]{1,0,2:T(8,128)(2,1)} %bitcast.33), kind=kOutput, calls=%fused_computation.43 | convolution fusion | flops 2147483648 | bytes 11534336 | tf_op jit(solution)/shard_map/dot_general | solution.py:120
  249.0 63.9 %all_to_all.5 = f32[128,16,256]{2,1,0:T(8,128)S(1)} all-to-all(f32[128,16,256]{2,1,0:T(8,128)S(1)} %fusion.19), channel_id=1, replica_groups=mesh['gx'=128,'ta'=2] {'gx'}, dimensions={0} | all-to-all | bytes 4194304 | tf_op jit(solution)/shard_map/all_to_all | solution.py:143
  312.8 3.5 %gather_fusion.2 = f32[1024,256]{1,0:T(8,128)S(1)} fusion(f32[2048,256]{1,0:T(8,128)S(1)} %bitcast.28, s32[1024]{0:T(1024)S(1)} %broadcast_clamp_fusion), kind=kCustom, calls=%fused_computation.2 | custom fusion | bytes 2101248 | tf_op jit(solution)/shard_map/gather | solution.py:176
  316.3 4.7 %collective-permute-start.2 = (f32[1024,256]{1,0:T(8,128)S(1)}, f32[1024,256]{1,0:T(8,128)S(1)}, u32[]{:S(2)}, u32[]{:S(2)}) collective-permute-start(f32[1024,256]{1,0:T(8,128)S(1)} %gather_fusion.2), channel_id=1, source_target_pairs={{0,1},{1,0},{2,3},{3,2},{4,5},{5,4},{6,7},{7,6},{8,9},{9,8},{10,11... | collective-permute-start | bytes 3145736 | tf_op jit(solution)/shard_map/ppermute | solution.py:146
  321.0 2.3 collective-permute-done.2
  323.3 2.3 divide_add_fusion
  (6 shorter events, 0.0 us)
Async XLA Ops:
  5.1 5.1 %copy-start = (bf16[1024,256]{1,0:T(8,128)(2,1)S(1)}, bf16[1024,256]{1,0:T(8,128)(2,1)}, u32[]{:S(2)}) copy-start(bf16[1024,256]{1,0:T(8,128)(2,1)} %param.4) | copy-start | bytes 1572868
  103.1 12.5 %copy-start.1 = (bf16[128,16,256]{2,1,0:T(8,128)(2,1)S(1)}, bf16[128,16,256]{2,1,0:T(8,128)(2,1)}, u32[]{:S(2)}) copy-start(bf16[128,16,256]{2,1,0:T(8,128)(2,1)} %get-tuple-element.10) | copy-start | bytes 3145732
  188.6 6.0 %copy-start.2 = (f32[128,16]{1,0:T(8,128)S(1)}, f32[128,16]{1,0:T(8,128)}, u32[]{:S(2)}) copy-start(f32[128,16]{1,0:T(8,128)} %get-tuple-element.12) | copy-start | bytes 24580
  193.7 5.9 %collective-permute-start = (f32[1024,256]{1,0:T(8,128)S(1)}, f32[1024,256]{1,0:T(8,128)}, u32[]{:S(2)}, u32[]{:S(2)}) collective-permute-start(f32[1024,256]{1,0:T(8,128)S(1)} %gather_fusion), channel_id=1, source_target_pairs={{0,1},{1,0},{2,3},{3,2},{4,5},{5,4},{6,7},{7,6},{8,9},{9,8},{10,11... | collective-permute-start | bytes 3145736 | tf_op jit(solution)/shard_map/ppermute | solution.py:146
  198.1 1.5 collective-permute-start.1
  316.3 7.0 %collective-permute-start.2 = (f32[1024,256]{1,0:T(8,128)S(1)}, f32[1024,256]{1,0:T(8,128)S(1)}, u32[]{:S(2)}, u32[]{:S(2)}) collective-permute-start(f32[1024,256]{1,0:T(8,128)S(1)} %gather_fusion.2), channel_id=1, source_target_pairs={{0,1},{1,0},{2,3},{3,2},{4,5},{5,4},{6,7},{7,6},{8,9},{9,8},{10,11... | collective-permute-start | bytes 3145736 | tf_op jit(solution)/shard_map/ppermute | solution.py:146

commit v6 on v4

--- a/solution.py
+++ b/solution.py
@@ -162,7 +162,7 @@
     back_num = back_num.reshape(groups * slot, width_l)
     back_den = back_den.reshape(groups * slot)
     row_num = back_num[target]
-    row_den = jnp.broadcast_to(back_den[:, None], (groups * slot, 128))[target][:, 0]
+    row_den = jnp.sum(jnp.where(target[None, :] == slots[:, None], back_den[:, None], 0.0), axis=0)
     other_num, other_den = other_core((row_num, row_den))
     total_num = row_num + other_num
     total_den = row_den + other_den
@@ -172,9 +172,15 @@
     feats1 = exchange(place(first.astype(jnp.bfloat16)).reshape(groups, slot, -1))
     num2 = weighted_sums(blocks, feats1.reshape(groups * slot, -1))
     back2 = exchange(num2.reshape(groups, slot, -1)).reshape(groups * slot, -1)
-    row_num2 = back2[target]
-    total_num2 = row_num2 + other_core(row_num2)
-    return (1.0 - alpha_mix) * prior + alpha_mix * total_num2 / scale
+    halves = []
+    for part in range(2):
+        rows_part = slice(part * (rows // 2), (part + 1) * (rows // 2))
+        row_num2 = back2[target[rows_part]]
+        total_num2 = row_num2 + other_core(row_num2)
+        halves.append(
+            (1.0 - alpha_mix) * prior[rows_part] + alpha_mix * total_num2 / scale[rows_part]
+        )
+    return jnp.concatenate(halves, axis=0)
 
 
 def solution(mesh):

time: 303 us -> 301 us (level)
  blocking collectives: 99.4 us -> 43.5 us
  waiting for transfers between devices: 74 us -> 121 us
  starting transfers between devices: 24.5 us -> 32.6 us
  local copies, waits for them, and re-layouts: 12.7 us -> 9.07 us
    all_to_all x2 -> x1, blocking collectives: 99.4 us -> 43.5 us  [exchange(): return lax.all_to_all(buffer, 'gx', split_axis=0, concat_axis=0, tiled=True)]
    all_to_all x1 -> x2, waiting for transfers between devices: 70.6 us -> 119 us  [exchange(): return lax.all_to_all(buffer, 'gx', split_axis=0, concat_axis=0, tiled=True)]
    all_to_all x1 -> x2, starting transfers between devices: 16.6 us -> 24.3 us  [exchange(): return lax.all_to_all(buffer, 'gx', split_axis=0, concat_axis=0, tiled=True)]
    gather x2, local copies, waits for them, and re-layouts: 6.27 us -> 3.13 us  [body(): row_num2 = back2[target[rows_part]]]
    ppermute x3 -> x4, starting transfers between devices: 7.88 us -> 8.29 us  [other_core(): return lax.ppermute(values, 'ta', perm=[(0, 1), (1, 0)])]
  transfers between devices with their start and end apart: 4 -> 6, of which waited for: 3 -> 4; matrix products, arithmetic and copies ran while one was open for 1% -> 1% of each run, Pallas kernels for 0% -> 0%
where the time goes in v6:
time: 301 us
  waiting for transfers between devices  121 us (40%)
  Pallas kernels  61.2 us (20%)
  blocking collectives  43.5 us (14%)
  starting transfers between devices  32.6 us (11%)
  matrix products  22.4 us (7%)
  other arithmetic  10.6 us (4%)
  local copies, waits for them, and re-layouts  9.07 us (3%)
    all_to_all x2, waiting for transfers between devices, exchange(): return lax.all_to_all(buffer, 'gx', split_axis=0, concat_axis=0, tiled=True)  119 us
    pallas_call x1, Pallas kernels, all_to_all(): pl.pallas_call(functools.partial(a2a_kernel, count), out_shape=[jax.Shape...  61.2 us
    all_to_all x1, blocking collectives, exchange(): return lax.all_to_all(buffer, 'gx', split_axis=0, concat_axis=0, tiled=True)  43.5 us
    all_to_all x2, starting transfers between devices, exchange(): return lax.all_to_all(buffer, 'gx', split_axis=0, concat_axis=0, tiled=True)  24.3 us
    ppermute x4, starting transfers between devices, other_core(): return lax.ppermute(values, 'ta', perm=[(0, 1), (1, 0)])  8.29 us
    dot_general x2, matrix products, weighted_sums(): jnp.dot(w, feats, preferred_element_type=jnp.float32)  7.73 us
    dot_general x1, matrix products, bucket_weights(): lax.dot_general(unit[start:start + block], unit, (((1,), (1,)), ((), ()))...  7.6 us
    dot_general x2, matrix products, place(): jnp.dot(place_mat, payload, preferred_element_type=jnp.float32)  7.1 us
  transfers between devices with their start and end apart: 6, of which 4 were waited for; matrix products, arithmetic and copies ran while one was open for 1% of the time, Pallas kernels for 0%

profile of v6, /device:TPU:1, one launch (start us, length us, event | category | flops | bytes accessed | tf_op | source)
XLA Modules:
  0.0 300.5 jit_solution(1420372489664870488)
XLA Ops:
  0.0 0.0 copy-start
  0.0 1.3 convert_reduce_fusion.2
  1.3 0.7 multiply_add_fusion
  2.0 0.9 convert_reduce_fusion.1
  2.9 1.5 fusion.8
  4.4 1.5 fusion.9
  6.0 0.0 copy-done
  6.0 5.2 %and_select_fusion = bf16[2048,768]{1,0:T(8,128)(2,1)} fusion(pred[768]{0:T(1024)(128)(4,1)S(1)} %iota_compare_fusion.11, pred[2048]{0:T(1024)(128)(4,1)S(1)} %compare_not_fusion, s32[1024]{0:T(1024)S(1)} %multiply_add_fusion, bf16[1024,256]{1,0:T(8,128)(2,1)S(1)} %copy-done, bf16[1024,512]{1,0:T(8,128)(2,1)S(1)} %fusion.9), kind=kOutput, calls=%fused_computation.12 | convolution fusion | flops 3231186944 | bytes 4725504 | tf_op jit(solution)/shard_map/dot_general | solution.py:140
  11.2 0.0 copy-start.3
  11.2 16.6 %all-to-all-start = ((bf16[128,16,768]{2,1,0:T(8,128)(2,1)}), bf16[128,16,768]{2,1,0:T(8,128)(2,1)S(1)}, u32[]{:S(2)}, u32[]{:S(2)}) async-start(bf16[128,16,768]{2,1,0:T(8,128)(2,1)} %bitcast.26), calls=%async_computation | async-start | bytes 6291456 | tf_op jit(solution)/shard_map/all_to_all | solution.py:143
  27.9 0.0 copy-done.3
  27.9 70.6 %all-to-all-done = bf16[128,16,768]{2,1,0:T(8,128)(2,1)S(1)} async-done(((bf16[128,16,768]{2,1,0:T(8,128)(2,1)}), bf16[128,16,768]{2,1,0:T(8,128)(2,1)S(1)}, u32[]{:S(2)}, u32[]{:S(2)}) %all-to-all-start) | async-done | bytes 3145760 | tf_op jit(solution)/shard_map/all_to_all | solution.py:143
  98.5 0.2 convert_reduce_fusion.3
  98.8 7.6 %convert_reduce_fusion = (f32[2048]{0:T(1024)S(1)}, bf16[2048,2048]{1,0:T(8,128)(2,1)S(1)}) fusion(f32[2048]{0:T(1024)S(1)} %convert_reduce_fusion.3, bf16[2048,768]{1,0:T(8,128)(2,1)S(1)} %bitcast.24), kind=kOutput, calls=%fused_computation.3 | convolution fusion | flops 4324325376 | bytes 10502144 | tf_op jit(solution)/shard_map/dot_general | solution.py:103
  106.4 0.0 copy-start.4
  106.4 4.0 %fusion.14 = f32[2048,256]{1,0:T(8,128)} fusion(bf16[2048,2048]{1,0:T(8,128)(2,1)S(1)} %get-tuple-element.16, bf16[2048,768]{1,0:T(8,128)(2,1)S(1)} %bitcast.25), kind=kOutput, calls=%fused_computation.28 | convolution fusion | flops 2147483648 | bytes 11534336 | tf_op jit(solution)/shard_map/dot_general | solution.py:120
  110.4 0.0 copy-done.4
  110.4 0.7 reshape.96.refs_1_
  111.1 61.2 %shard_map.37 = (f32[128,16,256]{2,1,0:T(8,128)}, f32[128,16]{1,0:T(8,128)}) custom-call(f32[128,16,256]{2,1,0:T(8,128)} %bitcast.27, f32[128,16]{1,0:T(8,128)} %reshape.96.refs_1_), custom_call_target="tpu_custom_call" | custom-call | tf_op jit(solution)/shard_map/pallas_call | solution.py:82
  172.2 0.0 copy-start.2
  172.2 0.0 copy-start.1
  172.3 5.1 %gather_fusion = f32[1024,256]{1,0:T(8,128)S(1)} fusion(f32[2048,256]{1,0:T(8,128)} %bitcast.22, s32[1024]{0:T(1024)S(1)} %broadcast_clamp_fusion), kind=kCustom, calls=%fused_computation | custom fusion | bytes 2101248 | tf_op jit(solution)/shard_map/gather | solution.py:164
  177.4 2.8 collective-permute-start
  180.2 0.0 copy-done.2
  180.2 0.1 broadcast_in_dim.23
  180.2 1.0 select_reduce_fusion
  181.2 0.1 collective-permute-start.1
  181.3 1.1 collective-permute-done.1
  182.5 0.0 slice-start
  182.5 0.0 slice-start.1
  182.5 0.0 collective-permute-done
  182.5 0.0 copy-done.1
  182.5 1.8 fusion.7
  184.4 43.5 %all_to_all.15 = bf16[128,16,256]{2,1,0:T(8,128)(2,1)S(1)} all-to-all(bf16[128,16,256]{2,1,0:T(8,128)(2,1)S(1)} %bitcast.28), channel_id=1, replica_groups=mesh['gx'=128,'ta'=2] {'gx'}, dimensions={0} | all-to-all | bytes 2097152 | tf_op jit(solution)/shard_map/all_to_all | solution.py:143
  227.9 0.0 slice-done
  227.9 0.0 slice-done.1
  227.9 3.8 %fusion.23 = f32[128,16,256]{2,1,0:T(8,128)} fusion(bf16[128,16,2048]{2,1,0:T(8,128)(2,1)S(1)} %bitcast.36, bf16[2048,256,1]{1,0,2:T(8,128)(2,1)S(1)} %bitcast.29), kind=kOutput, calls=%fused_computation.55 | convolution fusion | flops 2147483648 | bytes 11534336 | tf_op jit(solution)/shard_map/dot_general | solution.py:120
  231.6 7.6 %all-to-all-start.2 = ((f32[128,16,256]{2,1,0:T(8,128)}), f32[128,16,256]{2,1,0:T(8,128)S(1)}, u32[]{:S(2)}, u32[]{:S(2)}) async-start(f32[128,16,256]{2,1,0:T(8,128)} %fusion.23), calls=%async_computation.2 | async-start | bytes 4194304 | tf_op jit(solution)/shard_map/all_to_all | solution.py:143
  239.3 48.4 %all-to-all-done.2 = f32[128,16,256]{2,1,0:T(8,128)S(1)} async-done(((f32[128,16,256]{2,1,0:T(8,128)}), f32[128,16,256]{2,1,0:T(8,128)S(1)}, u32[]{:S(2)}, u32[]{:S(2)}) %all-to-all-start.2) | async-done | bytes 2097184 | tf_op jit(solution)/shard_map/all_to_all | solution.py:143
  287.8 1.6 gather_fusion.2
  289.3 5.3 %collective-permute-start.3 = (f32[512,256]{1,0:T(8,128)S(1)}, f32[512,256]{1,0:T(8,128)}, u32[]{:S(2)}, u32[]{:S(2)}) collective-permute-start(f32[512,256]{1,0:T(8,128)S(1)} %gather_fusion.2), channel_id=1, source_target_pairs={{0,1},{1,0},{2,3},{3,2},{4,5},{5,4},{6,7},{7,6},{8,9},{9,8},{10,11... | collective-permute-start | bytes 1572872 | tf_op jit(solution)/shard_map/ppermute | solution.py:146
  294.6 1.6 gather_fusion.1
  296.2 0.1 collective-permute-start.2
  296.3 1.1 convert_element_type.52
  297.4 0.0 collective-permute-done.3
  297.4 0.7 collective-permute-done.2
  298.2 2.3 fusion.17
  (12 shorter events, 0.1 us)
Async XLA Ops:
  0.0 6.0 %copy-start = (bf16[1024,256]{1,0:T(8,128)(2,1)S(1)}, bf16[1024,256]{1,0:T(8,128)(2,1)}, u32[]{:S(2)}) copy-start(bf16[1024,256]{1,0:T(8,128)(2,1)} %param.4) | copy-start | bytes 1572868
  11.2 16.7 %copy-start.3 = (s32[1,1024,1]{1,2,0:T(1,128)S(1)}, s32[1,1024,1]{1,2,0:T(1,128)}, u32[]{:S(2)}) copy-start(s32[1,1024,1]{1,2,0:T(1,128)} %param.5) | copy-start | bytes 12292
  11.2 87.3 %all-to-all-start = ((bf16[128,16,768]{2,1,0:T(8,128)(2,1)}), bf16[128,16,768]{2,1,0:T(8,128)(2,1)S(1)}, u32[]{:S(2)}, u32[]{:S(2)}) async-start(bf16[128,16,768]{2,1,0:T(8,128)(2,1)} %bitcast.26), calls=%async_computation | async-start | bytes 6291456 | tf_op jit(solution)/shard_map/all_to_all | solution.py:143
  106.4 4.0 %copy-start.4 = (bf16[2048,2048]{1,0:T(8,128)(2,1)}, bf16[2048,2048]{1,0:T(8,128)(2,1)S(1)}, u32[]{:S(2)}) copy-start(bf16[2048,2048]{1,0:T(8,128)(2,1)S(1)} %get-tuple-element.16) | copy-start | bytes 25165828
  172.2 7.9 %copy-start.2 = (f32[128,16]{1,0:T(8,128)S(1)}, f32[128,16]{1,0:T(8,128)}, u32[]{:S(2)}) copy-start(f32[128,16]{1,0:T(8,128)} %get-tuple-element.8) | copy-start | bytes 24580
  172.2 10.3 %copy-start.1 = (bf16[1024,256]{1,0:T(8,128)(2,1)S(1)}, bf16[1024,256]{1,0:T(8,128)(2,1)}, u32[]{:S(2)}) copy-start(bf16[1024,256]{1,0:T(8,128)(2,1)} %param.4) | copy-start | bytes 1572868
  177.4 5.1 %collective-permute-start = (f32[1024,256]{1,0:T(8,128)S(1)}, f32[1024,256]{1,0:T(8,128)S(1)}, u32[]{:S(2)}, u32[]{:S(2)}) collective-permute-start(f32[1024,256]{1,0:T(8,128)S(1)} %gather_fusion), channel_id=1, source_target_pairs={{0,1},{1,0},{2,3},{3,2},{4,5},{5,4},{6,7},{7,6},{8,9},{9,8},{10,11... | collective-permute-start | bytes 3145736 | tf_op jit(solution)/shard_map/ppermute | solution.py:146
  181.2 1.3 collective-permute-start.1
  182.5 45.4 %slice-start = ((s8[8388608]{0:T(1024)(128)(4,1)}), s8[4194304]{0:T(1024)(128)(4,1)S(1)}, s32[]{:S(2)}) async-start(s8[8388608]{0:T(1024)(128)(4,1)} %bitcast.34), calls=%async_computation.3 | async-start | bytes 8388608
  182.5 45.4 %slice-start.1 = ((s8[8388608]{0:T(1024)(128)(4,1)}), s8[4194304]{0:T(1024)(128)(4,1)S(1)}, s32[]{:S(2)}) async-start(s8[8388608]{0:T(1024)(128)(4,1)} %bitcast.34), calls=%async_computation.4 | async-start | bytes 8388608
  231.6 56.1 %all-to-all-start.2 = ((f32[128,16,256]{2,1,0:T(8,128)}), f32[128,16,256]{2,1,0:T(8,128)S(1)}, u32[]{:S(2)}, u32[]{:S(2)}) async-start(f32[128,16,256]{2,1,0:T(8,128)} %fusion.23), calls=%async_computation.2 | async-start | bytes 4194304 | tf_op jit(solution)/shard_map/all_to_all | solution.py:143
  289.3 8.1 %collective-permute-start.3 = (f32[512,256]{1,0:T(8,128)S(1)}, f32[512,256]{1,0:T(8,128)}, u32[]{:S(2)}, u32[]{:S(2)}) collective-permute-start(f32[512,256]{1,0:T(8,128)S(1)} %gather_fusion.2), channel_id=1, source_target_pairs={{0,1},{1,0},{2,3},{3,2},{4,5},{5,4},{6,7},{7,6},{8,9},{9,8},{10,11... | collective-permute-start | bytes 1572872 | tf_op jit(solution)/shard_map/ppermute | solution.py:146
  296.2 2.0 collective-permute-start.2

commit v7 on v6

--- a/solution.py
+++ b/solution.py
@@ -150,7 +150,8 @@
     column = lax.broadcasted_iota(jnp.int32, placed.shape, 1)
     pad_here = (column == unit_here.shape[1]) & ~occupied[:, None]
     placed = jnp.where(pad_here, jnp.bfloat16(PAD_MARK), placed)
-    got = exchange(placed.reshape(groups, slot, -1)).reshape(groups * slot, -1)
+    (got,) = all_to_all([placed.reshape(groups, slot, -1)], 1)
+    got = got.reshape(groups * slot, -1)
     unit = got[:, : unit_here.shape[1]]
     feats0 = got[:, unit_here.shape[1] :]
     valid = (feats0[:, 0].astype(jnp.float32) > PAD_MARK * 0.5).astype(jnp.float32)

time: 301 us -> 312 us (1.037)
  Pallas kernels: 61.2 us -> 153 us
  waiting for transfers between devices: 121 us -> 50.4 us
  starting transfers between devices: 32.6 us -> 14.3 us
  matrix products: 22.4 us -> 27.5 us
    pallas_call x1 -> x2, Pallas kernels: 61.2 us -> 153 us  [all_to_all(): pl.pallas_call(functools.partial(a2a_kernel, count), out_shape=[jax.Shape...]
    all_to_all x2 -> x1, waiting for transfers between devices: 119 us -> 48.4 us  [exchange(): return lax.all_to_all(buffer, 'gx', split_axis=0, concat_axis=0, tiled=True)]
    all_to_all x2 -> x1, starting transfers between devices: 24.3 us -> 7.63 us  [exchange(): return lax.all_to_all(buffer, 'gx', split_axis=0, concat_axis=0, tiled=True)]
  transfers between devices with their start and end apart: 6 -> 5, of which waited for: 4 -> 4; matrix products, arithmetic and copies ran while one was open for 1% -> 1% of each run, Pallas kernels for 0% -> 0%
where the time goes in v7:
time: 312 us; the launch traced here: 311 us
  Pallas kernels  153 us (49%)
  waiting for transfers between devices  50.4 us (16%)
  blocking collectives  45.2 us (14%)
  matrix products  27.5 us (9%)
  starting transfers between devices  14.3 us (5%)
  local copies, waits for them, and re-layouts  10.4 us (3%)
  other arithmetic  10.4 us (3%)
    pallas_call x2, Pallas kernels, all_to_all(): pl.pallas_call(functools.partial(a2a_kernel, count), out_shape=[jax.Shape...  153 us
    all_to_all x1, waiting for transfers between devices, exchange(): return lax.all_to_all(buffer, 'gx', split_axis=0, concat_axis=0, tiled=True)  48.4 us
    all_to_all x1, blocking collectives, exchange(): return lax.all_to_all(buffer, 'gx', split_axis=0, concat_axis=0, tiled=True)  45.2 us
    dot_general x2, matrix products, weighted_sums(): jnp.dot(w, feats, preferred_element_type=jnp.float32)  9.71 us
    dot_general x1, matrix products, bucket_weights(): lax.dot_general(unit[start:start + block], unit, (((1,), (1,)), ((), ()))...  9.34 us
    dot_general x2, matrix products, place(): jnp.dot(place_mat, payload, preferred_element_type=jnp.float32)  8.5 us
    all_to_all x1, starting transfers between devices, exchange(): return lax.all_to_all(buffer, 'gx', split_axis=0, concat_axis=0, tiled=True)  7.63 us
    ppermute x4, starting transfers between devices, other_core(): return lax.ppermute(values, 'ta', perm=[(0, 1), (1, 0)])  6.7 us
  transfers between devices with their start and end apart: 5, of which 4 were waited for; matrix products, arithmetic and copies ran while one was open for 1% of the time, Pallas kernels for 0%

profile of v7, /device:TPU:1, one launch (start us, length us, event | category | flops | bytes accessed | tf_op | source)
XLA Modules:
  0.0 311.0 jit_solution(9882714062984722306)
XLA Ops:
  0.0 0.0 copy-start
  0.0 1.3 convert_reduce_fusion.2
  1.3 0.7 multiply_add_fusion
  2.0 0.9 convert_reduce_fusion.1
  2.9 1.5 fusion.8
  4.4 1.5 fusion.9
  6.0 0.0 copy-done
  6.0 5.3 %and_select_fusion = bf16[2048,768]{1,0:T(8,128)(2,1)} fusion(pred[768]{0:T(1024)(128)(4,1)S(1)} %iota_compare_fusion.11, pred[2048]{0:T(1024)(128)(4,1)S(1)} %compare_not_fusion, s32[1024]{0:T(1024)S(1)} %multiply_add_fusion, bf16[1024,256]{1,0:T(8,128)(2,1)S(1)} %copy-done, bf16[1024,512]{1,0:T(8,128)(2,1)S(1)} %fusion.9), kind=kOutput, calls=%fused_computation.12 | convolution fusion | flops 3231186944 | bytes 4725504 | tf_op jit(solution)/shard_map/dot_general | solution.py:140
  11.2 85.1 %shard_map.37 = bf16[128,16,768]{2,1,0:T(8,128)(2,1)} custom-call(bf16[128,16,768]{2,1,0:T(8,128)(2,1)} %bitcast.27), custom_call_target="tpu_custom_call" | custom-call | tf_op jit(solution)/shard_map/pallas_call | solution.py:82
  96.4 1.1 slice.47
  97.5 0.2 copy.10
  97.7 9.3 %convert_reduce_fusion = (f32[2048]{0:T(1024)S(1)}, bf16[2048,2048]{1,0:T(8,128)(2,1)S(1)}) fusion(f32[2048]{0:T(1024)S(1)} %bitcast.35, bf16[2048,768]{1,0:T(8,128)(2,1)} %bitcast.25), kind=kOutput, calls=%fused_computation.3 | convolution fusion | flops 4324325376 | bytes 10502144 | tf_op jit(solution)/shard_map/dot_general | solution.py:103
  107.1 0.0 copy-start.3
  107.1 0.0 copy-start.2
  107.1 5.9 %fusion.14 = f32[2048,256]{1,0:T(8,128)} fusion(bf16[2048,2048]{1,0:T(8,128)(2,1)S(1)} %get-tuple-element.16, bf16[2048,768]{1,0:T(8,128)(2,1)} %bitcast.26), kind=kOutput, calls=%fused_computation.28 | convolution fusion | flops 2147483648 | bytes 11534336 | tf_op jit(solution)/shard_map/dot_general | solution.py:120
  113.0 0.0 copy-done.3
  113.0 0.7 reshape.96.refs_1_
  113.7 0.0 copy-done.2
  113.8 67.4 %shard_map.38 = (f32[128,16,256]{2,1,0:T(8,128)}, f32[128,16]{1,0:T(8,128)}) custom-call(f32[128,16,256]{2,1,0:T(8,128)} %bitcast.28, f32[128,16]{1,0:T(8,128)} %reshape.96.refs_1_), custom_call_target="tpu_custom_call" | custom-call | tf_op jit(solution)/shard_map/pallas_call | solution.py:82
  181.2 0.0 copy-start.1
  181.2 5.1 %gather_fusion = f32[1024,256]{1,0:T(8,128)S(1)} fusion(f32[2048,256]{1,0:T(8,128)} %bitcast.23, s32[1024]{0:T(1024)S(1)} %broadcast_clamp_fusion), kind=kCustom, calls=%fused_computation | custom fusion | bytes 2101248 | tf_op jit(solution)/shard_map/gather | solution.py:165
  186.3 1.2 collective-permute-start
  187.5 0.0 copy-done.1
  187.5 0.1 broadcast_in_dim.23
  187.6 1.0 select_reduce_fusion
  188.6 0.1 collective-permute-start.1
  188.7 1.1 collective-permute-done.1
  189.8 0.0 slice-start
  189.8 0.0 slice-start.1
  189.8 0.1 collective-permute-done
  189.9 3.2 %fusion.7 = bf16[2048,256]{1,0:T(8,128)(2,1)S(1)} fusion(s32[1024]{0:T(1024)S(1)} %multiply_add_fusion, f32[1024,256]{1,0:T(8,128)S(1)} %gather_fusion, f32[1024,256]{1,0:T(8,128)} %collective-permute-done, f32[1024]{0:T(1024)S(1)} %add_add_fusion, bf16[1024,256]{1,0:T(8,128)(2,1)S(1)} %copy-done), kind=kOutput, calls=%fused_computation.21 | convolution fusion | flops 1078198272 | bytes 3678208 | tf_op jit(solution)/shard_map/dot_general | solution.py:140
  193.2 45.2 %all_to_all.10 = bf16[128,16,256]{2,1,0:T(8,128)(2,1)S(1)} all-to-all(bf16[128,16,256]{2,1,0:T(8,128)(2,1)S(1)} %bitcast.29), channel_id=1, replica_groups=mesh['gx'=128,'ta'=2] {'gx'}, dimensions={0} | all-to-all | bytes 2097152 | tf_op jit(solution)/shard_map/all_to_all | solution.py:143
  238.4 0.0 slice-done
  238.4 0.0 slice-done.1
  238.4 3.8 %fusion.23 = f32[128,16,256]{2,1,0:T(8,128)} fusion(bf16[128,16,2048]{2,1,0:T(8,128)(2,1)S(1)} %bitcast.38, bf16[2048,256,1]{1,0,2:T(8,128)(2,1)S(1)} %bitcast.30), kind=kOutput, calls=%fused_computation.54 | convolution fusion | flops 2147483648 | bytes 11534336 | tf_op jit(solution)/shard_map/dot_general | solution.py:120
  242.2 7.6 %all-to-all-start.1 = ((f32[128,16,256]{2,1,0:T(8,128)}), f32[128,16,256]{2,1,0:T(8,128)S(1)}, u32[]{:S(2)}, u32[]{:S(2)}) async-start(f32[128,16,256]{2,1,0:T(8,128)} %fusion.23), calls=%async_computation.1 | async-start | bytes 4194304 | tf_op jit(solution)/shard_map/all_to_all | solution.py:143
  249.9 48.4 %all-to-all-done.1 = f32[128,16,256]{2,1,0:T(8,128)S(1)} async-done(((f32[128,16,256]{2,1,0:T(8,128)}), f32[128,16,256]{2,1,0:T(8,128)S(1)}, u32[]{:S(2)}, u32[]{:S(2)}) %all-to-all-start.1) | async-done | bytes 2097184 | tf_op jit(solution)/shard_map/all_to_all | solution.py:143
  298.3 1.6 gather_fusion.2
  299.9 5.3 %collective-permute-start.3 = (f32[512,256]{1,0:T(8,128)S(1)}, f32[512,256]{1,0:T(8,128)}, u32[]{:S(2)}, u32[]{:S(2)}) collective-permute-start(f32[512,256]{1,0:T(8,128)S(1)} %gather_fusion.2), channel_id=1, source_target_pairs={{0,1},{1,0},{2,3},{3,2},{4,5},{5,4},{6,7},{7,6},{8,9},{9,8},{10,11... | collective-permute-start | bytes 1572872 | tf_op jit(solution)/shard_map/ppermute | solution.py:146
  305.2 1.6 gather_fusion.1
  306.7 0.1 collective-permute-start.2
  306.9 1.1 convert_element_type.52
  308.0 0.0 collective-permute-done.3
  308.0 0.7 collective-permute-done.2
  308.7 2.3 fusion.17
  (13 shorter events, 0.1 us)
Async XLA Ops:
  0.0 6.0 %copy-start = (bf16[1024,256]{1,0:T(8,128)(2,1)S(1)}, bf16[1024,256]{1,0:T(8,128)(2,1)}, u32[]{:S(2)}) copy-start(bf16[1024,256]{1,0:T(8,128)(2,1)} %param.4) | copy-start | bytes 1572868
  107.1 6.0 %copy-start.3 = (bf16[2048,2048]{1,0:T(8,128)(2,1)}, bf16[2048,2048]{1,0:T(8,128)(2,1)S(1)}, u32[]{:S(2)}) copy-start(bf16[2048,2048]{1,0:T(8,128)(2,1)S(1)} %get-tuple-element.16) | copy-start | bytes 25165828
  107.1 6.7 %copy-start.2 = (s32[1,1024,1]{1,2,0:T(1,128)S(1)}, s32[1,1024,1]{1,2,0:T(1,128)}, u32[]{:S(2)}) copy-start(s32[1,1024,1]{1,2,0:T(1,128)} %param.5) | copy-start | bytes 12292
  181.2 6.3 %copy-start.1 = (f32[128,16]{1,0:T(8,128)S(1)}, f32[128,16]{1,0:T(8,128)}, u32[]{:S(2)}) copy-start(f32[128,16]{1,0:T(8,128)} %get-tuple-element.8) | copy-start | bytes 24580
  186.3 3.6 %collective-permute-start = (f32[1024,256]{1,0:T(8,128)S(1)}, f32[1024,256]{1,0:T(8,128)}, u32[]{:S(2)}, u32[]{:S(2)}) collective-permute-start(f32[1024,256]{1,0:T(8,128)S(1)} %gather_fusion), channel_id=1, source_target_pairs={{0,1},{1,0},{2,3},{3,2},{4,5},{5,4},{6,7},{7,6},{8,9},{9,8},{10,11... | collective-permute-start | bytes 3145736 | tf_op jit(solution)/shard_map/ppermute | solution.py:146
  188.6 1.3 collective-permute-start.1
  189.8 48.6 %slice-start = ((s8[8388608]{0:T(1024)(128)(4,1)}), s8[4194304]{0:T(1024)(128)(4,1)S(1)}, s32[]{:S(2)}) async-start(s8[8388608]{0:T(1024)(128)(4,1)} %bitcast.36), calls=%async_computation.2 | async-start | bytes 8388608
  189.8 48.6 %slice-start.1 = ((s8[8388608]{0:T(1024)(128)(4,1)}), s8[4194304]{0:T(1024)(128)(4,1)S(1)}, s32[]{:S(2)}) async-start(s8[8388608]{0:T(1024)(128)(4,1)} %bitcast.36), calls=%async_computation.3 | async-start | bytes 8388608
  242.2 56.1 %all-to-all-start.1 = ((f32[128,16,256]{2,1,0:T(8,128)}), f32[128,16,256]{2,1,0:T(8,128)S(1)}, u32[]{:S(2)}, u32[]{:S(2)}) async-start(f32[128,16,256]{2,1,0:T(8,128)} %fusion.23), calls=%async_computation.1 | async-start | bytes 4194304 | tf_op jit(solution)/shard_map/all_to_all | solution.py:143
  299.9 8.1 %collective-permute-start.3 = (f32[512,256]{1,0:T(8,128)S(1)}, f32[512,256]{1,0:T(8,128)}, u32[]{:S(2)}, u32[]{:S(2)}) collective-permute-start(f32[512,256]{1,0:T(8,128)S(1)} %gather_fusion.2), channel_id=1, source_target_pairs={{0,1},{1,0},{2,3},{3,2},{4,5},{5,4},{6,7},{7,6},{8,9},{9,8},{10,11... | collective-permute-start | bytes 1572872 | tf_op jit(solution)/shard_map/ppermute | solution.py:146
  306.7 2.0 collective-permute-start.2

commit v8 on v6

--- a/solution.py
+++ b/solution.py
@@ -93,32 +93,53 @@
     )(*arrays)
 
 
-def bucket_weights(unit, valid):
-    cap = unit.shape[0]
-    block = cap
-    cols = jnp.arange(cap)
-    blocks = []
-    dens = []
-    for start in range(0, cap, block):
-        gram = lax.dot_general(
-            unit[start : start + block],
-            unit,
-            (((1,), (1,)), ((), ())),
-            preferred_element_type=jnp.float32,
-        )
-        keep = valid[None, :] * (cols[None, :] != (start + jnp.arange(block))[:, None]).astype(
-            jnp.float32
-        )
-        weights = (jnp.exp(sharpness * gram) * keep).astype(jnp.bfloat16)
-        blocks.append(weights)
-        dens.append(jnp.sum(weights.astype(jnp.float32), axis=1))
-    return blocks, jnp.concatenate(dens, axis=0)
-
-
-def weighted_sums(blocks, feats):
-    return jnp.concatenate(
-        [jnp.dot(w, feats, preferred_element_type=jnp.float32) for w in blocks], axis=0
+def weights_kernel(rows_ref, unit_ref, feats_ref, valid_ref, w_ref, den_ref, num_ref):
+    block = rows_ref.shape[0]
+    start = pl.program_id(0) * block
+    gram = lax.dot_general(
+        rows_ref[...],
+        unit_ref[...],
+        (((1,), (1,)), ((), ())),
+        preferred_element_type=jnp.float32,
     )
+    cols = lax.broadcasted_iota(jnp.int32, gram.shape, 1)
+    rows = lax.broadcasted_iota(jnp.int32, gram.shape, 0) + start
+    keep = jnp.where(cols != rows, valid_ref[...], 0.0)
+    weights = (jnp.exp(sharpness * gram) * keep).astype(jnp.bfloat16)
+    w_ref[...] = weights
+    den_ref[...] = jnp.sum(weights.astype(jnp.float32), axis=1, keepdims=True)
+    num_ref[...] = jnp.dot(weights, feats_ref[...], preferred_element_type=jnp.float32)
+
+
+def bucket_round_one(unit, feats, valid, block=256):
+    cap, width_e = unit.shape
+    width_l = feats.shape[1]
+    whole = lambda i: (0, 0)
+    return pl.pallas_call(
+        weights_kernel,
+        grid=(cap // block,),
+        out_shape=[
+            jax.ShapeDtypeStruct((cap, cap), jnp.bfloat16),
+            jax.ShapeDtypeStruct((cap, 1), jnp.float32),
+            jax.ShapeDtypeStruct((cap, width_l), jnp.float32),
+        ],
+        in_specs=[
+            pl.BlockSpec((block, width_e), lambda i: (i, 0)),
+            pl.BlockSpec((cap, width_e), whole),
+            pl.BlockSpec((cap, width_l), whole),
+            pl.BlockSpec((1, cap), whole),
+        ],
+        out_specs=[
+            pl.BlockSpec((block, cap), lambda i: (i, 0)),
+            pl.BlockSpec((block, 1), lambda i: (i, 0)),
+            pl.BlockSpec((block, width_l), lambda i: (i, 0)),
+        ],
+        cost_estimate=pl.CostEstimate(
+            flops=2 * cap * cap * (width_e + width_l),
+            transcendentals=cap * cap,
+            bytes_accessed=2 * cap * (cap + width_e + width_l) + 4 * cap * (width_l + 2),
+        ),
+    )(unit, unit, feats, valid[None, :])
 
 
 def body(embeddings, labels, bucket_ids):
@@ -155,8 +176,7 @@
     feats0 = got[:, unit_here.shape[1] :]
     valid = (feats0[:, 0].astype(jnp.float32) > PAD_MARK * 0.5).astype(jnp.float32)
 
-    blocks, den = bucket_weights(unit, valid)
-    num1 = weighted_sums(blocks, feats0)
+    weights, den, num1 = bucket_round_one(unit, feats0, valid)
 
     back_num, back_den = all_to_all([num1.reshape(groups, slot, width_l), den.reshape(groups, slot)], 0)
     back_num = back_num.reshape(groups * slot, width_l)
@@ -170,7 +190,7 @@
     first = (1.0 - alpha_mix) * prior + alpha_mix * total_num / scale
 
     feats1 = exchange(place(first.astype(jnp.bfloat16)).reshape(groups, slot, -1))
-    num2 = weighted_sums(blocks, feats1.reshape(groups * slot, -1))
+    num2 = jnp.dot(weights, feats1.reshape(groups * slot, -1), preferred_element_type=jnp.float32)
     back2 = exchange(num2.reshape(groups, slot, -1)).reshape(groups * slot, -1)
     halves = []
     for part in range(2):

time: 301 us -> 307 us (1.020)
  Pallas kernels: 61.2 us -> 74.3 us
  matrix products: 22.4 us -> 10.9 us
    pallas_call x0 -> x1, Pallas kernels: none -> 13.1 us  [bucket_round_one(): pl.pallas_call(weights_kernel, grid=(cap // block,), out_shape=[jax.Shape...]
    dot_general x3 -> x1, matrix products: 15.3 us -> 3.78 us  [body(): jnp.dot(weights, feats1.reshape(groups * slot, -1), preferred_element_typ...]
where the time goes in v8:
time: 307 us
  waiting for transfers between devices  121 us (39%)
  Pallas kernels  74.3 us (24%)
  blocking collectives  43.6 us (14%)
  starting transfers between devices  32.3 us (11%)
  other arithmetic  12.7 us (4%)
  local copies, waits for them, and re-layouts  11.6 us (4%)
  matrix products  10.9 us (4%)
    all_to_all x2, waiting for transfers between devices, exchange(): return lax.all_to_all(buffer, 'gx', split_axis=0, concat_axis=0, tiled=True)  119 us
    pallas_call x1, Pallas kernels, all_to_all(): pl.pallas_call(functools.partial(a2a_kernel, count), out_shape=[jax.Shape...  61.2 us
    all_to_all x1, blocking collectives, exchange(): return lax.all_to_all(buffer, 'gx', split_axis=0, concat_axis=0, tiled=True)  43.6 us
    all_to_all x2, starting transfers between devices, exchange(): return lax.all_to_all(buffer, 'gx', split_axis=0, concat_axis=0, tiled=True)  23.8 us
    pallas_call x1, Pallas kernels, bucket_round_one(): pl.pallas_call(weights_kernel, grid=(cap // block,), out_shape=[jax.Shape...  13.1 us
    ppermute x4, starting transfers between devices, other_core(): return lax.ppermute(values, 'ta', perm=[(0, 1), (1, 0)])  8.51 us
    dot_general x2, matrix products, place(): jnp.dot(place_mat, payload, preferred_element_type=jnp.float32)  7.13 us
  transfers between devices with their start and end apart: 6, of which 4 were waited for; matrix products, arithmetic and copies ran while one was open for 1% of the time, Pallas kernels for 0%

profile of v8, /device:TPU:1, one launch (start us, length us, event | category | flops | bytes accessed | tf_op | source)
XLA Modules:
  0.0 306.6 jit_solution(10181042372620989134)
XLA Ops:
  0.0 0.0 copy-start
  0.0 1.3 convert_reduce_fusion.1
  1.3 0.7 multiply_add_fusion
  2.0 0.9 convert_reduce_fusion
  2.9 1.5 fusion.8
  4.4 1.5 fusion.9
  6.0 0.0 copy-done
  6.0 5.3 %and_select_fusion = bf16[2048,768]{1,0:T(8,128)(2,1)} fusion(pred[768]{0:T(1024)(128)(4,1)S(1)} %iota_compare_fusion.10, pred[2048]{0:T(1024)(128)(4,1)S(1)} %compare_not_fusion, s32[1024]{0:T(1024)S(1)} %multiply_add_fusion, bf16[1024,256]{1,0:T(8,128)(2,1)S(1)} %copy-done, bf16[1024,512]{1,0:T(8,128)(2,1)S(1)} %fusion.9), kind=kOutput, calls=%fused_computation.9 | convolution fusion | flops 3231186944 | bytes 4725504 | tf_op jit(solution)/shard_map/dot_general | solution.py:161
  11.3 0.0 copy-start.3
  11.3 16.5 %all-to-all-start = ((bf16[128,16,768]{2,1,0:T(8,128)(2,1)}), bf16[128,16,768]{2,1,0:T(8,128)(2,1)S(1)}, u32[]{:S(2)}, u32[]{:S(2)}) async-start(bf16[128,16,768]{2,1,0:T(8,128)(2,1)} %bitcast.26), calls=%async_computation | async-start | bytes 6291456 | tf_op jit(solution)/shard_map/all_to_all | solution.py:164
  27.7 0.0 copy-done.3
  27.8 70.8 %all-to-all-done = bf16[128,16,768]{2,1,0:T(8,128)(2,1)S(1)} async-done(((bf16[128,16,768]{2,1,0:T(8,128)(2,1)}), bf16[128,16,768]{2,1,0:T(8,128)(2,1)S(1)}, u32[]{:S(2)}, u32[]{:S(2)}) %all-to-all-start) | async-done | bytes 3145760 | tf_op jit(solution)/shard_map/all_to_all | solution.py:164
  98.6 1.5 slice.46.rows_ref.unit_ref
  100.0 1.0 slice.47.feats_ref
  101.1 0.8 convert_reduce_fusion.2
  101.9 13.1 %shard_map.37 = (bf16[2048,2048]{1,0:T(8,128)(2,1)}, f32[2048,1]{1,0:T(8,128)}, f32[2048,256]{1,0:T(8,128)}) custom-call(bf16[2048,512]{1,0:T(8,128)(2,1)} %slice.46.rows_ref.unit_ref, bf16[2048,512]{1,0:T(8,128)(2,1)} %slice.46.rows_ref.unit_ref, bf16[2048,256]{1,0:T(8,128)(2,1)} %slice.47.feats_ref, f32[1,2048]{1,0:T(1,128)} %bitcast.34), custom_call_target="tpu_custom_call" | custom-call | flops 6442450944 | bytes 13647872 | tf_op jit(solution)/shard_map/pallas_call | solution.py:118
  115.0 1.6 reduce.1
  116.6 0.7 reshape.105.refs_1_
  117.3 61.2 %shard_map.38 = (f32[128,16,256]{2,1,0:T(8,128)}, f32[128,16]{1,0:T(8,128)}) custom-call(f32[128,16,256]{2,1,0:T(8,128)} %bitcast.27, f32[128,16]{1,0:T(8,128)} %reshape.105.refs_1_), custom_call_target="tpu_custom_call" | custom-call | tf_op jit(solution)/shard_map/pallas_call | solution.py:82
  178.5 0.0 copy-start.2
  178.5 0.0 copy-start.1
  178.5 5.1 %gather_fusion = f32[1024,256]{1,0:T(8,128)S(1)} fusion(f32[2048,256]{1,0:T(8,128)} %bitcast.22, s32[1024]{0:T(1024)S(1)} %broadcast_clamp_fusion), kind=kCustom, calls=%fused_computation | custom fusion | bytes 2101248 | tf_op jit(solution)/shard_map/gather | solution.py:184
  183.6 2.8 collective-permute-start
  186.4 0.0 copy-done.2
  186.4 0.1 broadcast_in_dim.36
  186.5 1.0 select_reduce_fusion
  187.5 0.3 collective-permute-start.1
  187.8 1.1 collective-permute-done.1
  188.9 0.0 slice-start
  188.9 0.0 slice-start.1
  188.9 0.0 collective-permute-done
  188.9 0.0 copy-done.1
  188.9 1.8 fusion.7
  190.8 43.6 %all_to_all.15 = bf16[128,16,256]{2,1,0:T(8,128)(2,1)S(1)} all-to-all(bf16[128,16,256]{2,1,0:T(8,128)(2,1)S(1)} %bitcast.29), channel_id=1, replica_groups=mesh['gx'=128,'ta'=2] {'gx'}, dimensions={0} | all-to-all | bytes 2097152 | tf_op jit(solution)/shard_map/all_to_all | solution.py:164
  234.4 0.0 slice-done
  234.4 0.0 slice-done.1
  234.4 3.8 %fusion.20 = f32[128,16,256]{2,1,0:T(8,128)} fusion(bf16[128,16,2048]{2,1,0:T(8,128)(2,1)S(1)} %bitcast.37, bf16[2048,256,1]{1,0,2:T(8,128)(2,1)S(1)} %bitcast.28), kind=kOutput, calls=%fused_computation.49 | convolution fusion | flops 2147483648 | bytes 11534336 | tf_op jit(solution)/shard_map/dot_general | solution.py:193
  238.2 7.3 %all-to-all-start.2 = ((f32[128,16,256]{2,1,0:T(8,128)}), f32[128,16,256]{2,1,0:T(8,128)S(1)}, u32[]{:S(2)}, u32[]{:S(2)}) async-start(f32[128,16,256]{2,1,0:T(8,128)} %fusion.20), calls=%async_computation.2 | async-start | bytes 4194304 | tf_op jit(solution)/shard_map/all_to_all | solution.py:164
  245.5 48.3 %all-to-all-done.2 = f32[128,16,256]{2,1,0:T(8,128)S(1)} async-done(((f32[128,16,256]{2,1,0:T(8,128)}), f32[128,16,256]{2,1,0:T(8,128)S(1)}, u32[]{:S(2)}, u32[]{:S(2)}) %all-to-all-start.2) | async-done | bytes 2097184 | tf_op jit(solution)/shard_map/all_to_all | solution.py:164
  293.9 1.6 gather_fusion.2
  295.4 5.3 %collective-permute-start.3 = (f32[512,256]{1,0:T(8,128)S(1)}, f32[512,256]{1,0:T(8,128)}, u32[]{:S(2)}, u32[]{:S(2)}) collective-permute-start(f32[512,256]{1,0:T(8,128)S(1)} %gather_fusion.2), channel_id=1, source_target_pairs={{0,1},{1,0},{2,3},{3,2},{4,5},{5,4},{6,7},{7,6},{8,9},{9,8},{10,11... | collective-permute-start | bytes 1572872 | tf_op jit(solution)/shard_map/ppermute | solution.py:167
  300.8 1.6 gather_fusion.1
  302.3 0.1 collective-permute-start.2
  302.5 1.1 convert_element_type.51
  303.6 0.0 collective-permute-done.3
  303.6 0.7 collective-permute-done.2
  304.3 2.3 fusion.14
  (12 shorter events, 0.1 us)
Async XLA Ops:
  0.0 6.0 %copy-start = (bf16[1024,256]{1,0:T(8,128)(2,1)S(1)}, bf16[1024,256]{1,0:T(8,128)(2,1)}, u32[]{:S(2)}) copy-start(bf16[1024,256]{1,0:T(8,128)(2,1)} %param.4) | copy-start | bytes 1572868
  11.3 16.5 %copy-start.3 = (s32[1,1024,1]{1,2,0:T(1,128)S(1)}, s32[1,1024,1]{1,2,0:T(1,128)}, u32[]{:S(2)}) copy-start(s32[1,1024,1]{1,2,0:T(1,128)} %param.5) | copy-start | bytes 12292
  11.3 87.3 %all-to-all-start = ((bf16[128,16,768]{2,1,0:T(8,128)(2,1)}), bf16[128,16,768]{2,1,0:T(8,128)(2,1)S(1)}, u32[]{:S(2)}, u32[]{:S(2)}) async-start(bf16[128,16,768]{2,1,0:T(8,128)(2,1)} %bitcast.26), calls=%async_computation | async-start | bytes 6291456 | tf_op jit(solution)/shard_map/all_to_all | solution.py:164
  178.5 7.9 %copy-start.2 = (f32[128,16]{1,0:T(8,128)S(1)}, f32[128,16]{1,0:T(8,128)}, u32[]{:S(2)}) copy-start(f32[128,16]{1,0:T(8,128)} %get-tuple-element.14) | copy-start | bytes 24580
  178.5 10.4 %copy-start.1 = (bf16[1024,256]{1,0:T(8,128)(2,1)S(1)}, bf16[1024,256]{1,0:T(8,128)(2,1)}, u32[]{:S(2)}) copy-start(bf16[1024,256]{1,0:T(8,128)(2,1)} %param.4) | copy-start | bytes 1572868
  183.6 5.3 %collective-permute-start = (f32[1024,256]{1,0:T(8,128)S(1)}, f32[1024,256]{1,0:T(8,128)S(1)}, u32[]{:S(2)}, u32[]{:S(2)}) collective-permute-start(f32[1024,256]{1,0:T(8,128)S(1)} %gather_fusion), channel_id=1, source_target_pairs={{0,1},{1,0},{2,3},{3,2},{4,5},{5,4},{6,7},{7,6},{8,9},{9,8},{10,11... | collective-permute-start | bytes 3145736 | tf_op jit(solution)/shard_map/ppermute | solution.py:167
  187.5 1.4 collective-permute-start.1
  188.9 45.5 %slice-start = ((s8[8388608]{0:T(1024)(128)(4,1)}), s8[4194304]{0:T(1024)(128)(4,1)S(1)}, s32[]{:S(2)}) async-start(s8[8388608]{0:T(1024)(128)(4,1)} %bitcast.35), calls=%async_computation.3 | async-start | bytes 8388608
  188.9 45.5 %slice-start.1 = ((s8[8388608]{0:T(1024)(128)(4,1)}), s8[4194304]{0:T(1024)(128)(4,1)S(1)}, s32[]{:S(2)}) async-start(s8[8388608]{0:T(1024)(128)(4,1)} %bitcast.35), calls=%async_computation.4 | async-start | bytes 8388608
  238.2 55.7 %all-to-all-start.2 = ((f32[128,16,256]{2,1,0:T(8,128)}), f32[128,16,256]{2,1,0:T(8,128)S(1)}, u32[]{:S(2)}, u32[]{:S(2)}) async-start(f32[128,16,256]{2,1,0:T(8,128)} %fusion.20), calls=%async_computation.2 | async-start | bytes 4194304 | tf_op jit(solution)/shard_map/all_to_all | solution.py:164
  295.4 8.2 %collective-permute-start.3 = (f32[512,256]{1,0:T(8,128)S(1)}, f32[512,256]{1,0:T(8,128)}, u32[]{:S(2)}, u32[]{:S(2)}) collective-permute-start(f32[512,256]{1,0:T(8,128)S(1)} %gather_fusion.2), channel_id=1, source_target_pairs={{0,1},{1,0},{2,3},{3,2},{4,5},{5,4},{6,7},{7,6},{8,9},{9,8},{10,11... | collective-permute-start | bytes 1572872 | tf_op jit(solution)/shard_map/ppermute | solution.py:167
  302.3 2.0 collective-permute-start.2

commit v9 on v6

--- a/solution.py
+++ b/solution.py
@@ -82,8 +82,8 @@
     return pl.pallas_call(
         functools.partial(a2a_kernel, count),
         out_shape=[jax.ShapeDtypeStruct(x.shape, x.dtype) for x in arrays],
-        in_specs=[pl.BlockSpec(memory_space=pl.ANY)] * count,
-        out_specs=[pl.BlockSpec(memory_space=pl.ANY)] * count,
+        in_specs=[pl.BlockSpec(memory_space=pltpu.VMEM)] * count,
+        out_specs=[pl.BlockSpec(memory_space=pltpu.VMEM)] * count,
         scratch_shapes=[
             pltpu.SemaphoreType.DMA((count, n)),
             pltpu.SemaphoreType.DMA((count, n)),

time: 301 us -> 303 us (level)
  no operation moved by 1% of the time
where the time goes in v9:
time: 303 us; the launch traced here: 302 us
  waiting for transfers between devices  121 us (40%)
  Pallas kernels  63.6 us (21%)
  blocking collectives  43.1 us (14%)
  starting transfers between devices  32.4 us (11%)
  matrix products  22.4 us (7%)
  other arithmetic  10.6 us (3%)
  local copies, waits for them, and re-layouts  9.07 us (3%)
    all_to_all x2, waiting for transfers between devices, exchange(): return lax.all_to_all(buffer, 'gx', split_axis=0, concat_axis=0, tiled=True)  119 us
    pallas_call x1, Pallas kernels, all_to_all(): pl.pallas_call(functools.partial(a2a_kernel, count), out_shape=[jax.Shape...  63.6 us
    all_to_all x1, blocking collectives, exchange(): return lax.all_to_all(buffer, 'gx', split_axis=0, concat_axis=0, tiled=True)  43.1 us
    all_to_all x2, starting transfers between devices, exchange(): return lax.all_to_all(buffer, 'gx', split_axis=0, concat_axis=0, tiled=True)  24.3 us
    ppermute x4, starting transfers between devices, other_core(): return lax.ppermute(values, 'ta', perm=[(0, 1), (1, 0)])  8.09 us
    dot_general x2, matrix products, weighted_sums(): jnp.dot(w, feats, preferred_element_type=jnp.float32)  7.73 us
    dot_general x1, matrix products, bucket_weights(): lax.dot_general(unit[start:start + block], unit, (((1,), (1,)), ((), ()))...  7.6 us
    dot_general x2, matrix products, place(): jnp.dot(place_mat, payload, preferred_element_type=jnp.float32)  7.1 us
  transfers between devices with their start and end apart: 6, of which 4 were waited for; matrix products, arithmetic and copies ran while one was open for 1% of the time, Pallas kernels for 0%

profile of v9, /device:TPU:1, one launch (start us, length us, event | category | flops | bytes accessed | tf_op | source)
XLA Modules:
  0.0 302.3 jit_solution(1865718605374286066)
XLA Ops:
  0.0 0.0 copy-start
  0.0 1.3 convert_reduce_fusion.2
  1.3 0.7 multiply_add_fusion
  2.0 0.9 convert_reduce_fusion.1
  2.9 1.5 fusion.8
  4.4 1.5 fusion.9
  6.0 0.0 copy-done
  6.0 5.2 %and_select_fusion = bf16[2048,768]{1,0:T(8,128)(2,1)} fusion(pred[768]{0:T(1024)(128)(4,1)S(1)} %iota_compare_fusion.11, pred[2048]{0:T(1024)(128)(4,1)S(1)} %compare_not_fusion, s32[1024]{0:T(1024)S(1)} %multiply_add_fusion, bf16[1024,256]{1,0:T(8,128)(2,1)S(1)} %copy-done, bf16[1024,512]{1,0:T(8,128)(2,1)S(1)} %fusion.9), kind=kOutput, calls=%fused_computation.12 | convolution fusion | flops 3231186944 | bytes 4725504 | tf_op jit(solution)/shard_map/dot_general | solution.py:140
  11.2 0.0 copy-start.3
  11.2 16.6 %all-to-all-start = ((bf16[128,16,768]{2,1,0:T(8,128)(2,1)}), bf16[128,16,768]{2,1,0:T(8,128)(2,1)S(1)}, u32[]{:S(2)}, u32[]{:S(2)}) async-start(bf16[128,16,768]{2,1,0:T(8,128)(2,1)} %bitcast.26), calls=%async_computation | async-start | bytes 6291456 | tf_op jit(solution)/shard_map/all_to_all | solution.py:143
  27.9 0.0 copy-done.3
  27.9 70.6 %all-to-all-done = bf16[128,16,768]{2,1,0:T(8,128)(2,1)S(1)} async-done(((bf16[128,16,768]{2,1,0:T(8,128)(2,1)}), bf16[128,16,768]{2,1,0:T(8,128)(2,1)S(1)}, u32[]{:S(2)}, u32[]{:S(2)}) %all-to-all-start) | async-done | bytes 3145760 | tf_op jit(solution)/shard_map/all_to_all | solution.py:143
  98.5 0.2 convert_reduce_fusion.3
  98.8 7.6 %convert_reduce_fusion = (f32[2048]{0:T(1024)S(1)}, bf16[2048,2048]{1,0:T(8,128)(2,1)S(1)}) fusion(f32[2048]{0:T(1024)S(1)} %convert_reduce_fusion.3, bf16[2048,768]{1,0:T(8,128)(2,1)S(1)} %bitcast.24), kind=kOutput, calls=%fused_computation.3 | convolution fusion | flops 4324325376 | bytes 10502144 | tf_op jit(solution)/shard_map/dot_general | solution.py:103
  106.4 0.0 copy-start.4
  106.4 4.0 %fusion.14 = f32[2048,256]{1,0:T(8,128)} fusion(bf16[2048,2048]{1,0:T(8,128)(2,1)S(1)} %get-tuple-element.16, bf16[2048,768]{1,0:T(8,128)(2,1)S(1)} %bitcast.25), kind=kOutput, calls=%fused_computation.28 | convolution fusion | flops 2147483648 | bytes 11534336 | tf_op jit(solution)/shard_map/dot_general | solution.py:120
  110.4 0.0 copy-done.4
  110.4 0.7 reshape.96.refs_1_
  111.1 63.6 %shard_map.37 = (f32[128,16,256]{2,1,0:T(8,128)}, f32[128,16]{1,0:T(8,128)}) custom-call(f32[128,16,256]{2,1,0:T(8,128)} %bitcast.27, f32[128,16]{1,0:T(8,128)} %reshape.96.refs_1_), custom_call_target="tpu_custom_call" | custom-call | tf_op jit(solution)/shard_map/pallas_call | solution.py:82
  174.7 0.0 copy-start.2
  174.7 0.0 copy-start.1
  174.7 5.1 %gather_fusion = f32[1024,256]{1,0:T(8,128)S(1)} fusion(f32[2048,256]{1,0:T(8,128)} %bitcast.22, s32[1024]{0:T(1024)S(1)} %broadcast_clamp_fusion), kind=kCustom, calls=%fused_computation | custom fusion | bytes 2101248 | tf_op jit(solution)/shard_map/gather | solution.py:164
  179.8 2.6 collective-permute-start
  182.4 0.0 copy-done.2
  182.4 0.1 broadcast_in_dim.23
  182.5 1.0 select_reduce_fusion
  183.5 0.1 collective-permute-start.1
  183.6 1.1 collective-permute-done.1
  184.7 0.0 slice-start
  184.7 0.0 slice-start.1
  184.7 0.0 collective-permute-done
  184.7 0.0 copy-done.1
  184.8 1.8 fusion.7
  186.6 43.1 %all_to_all.15 = bf16[128,16,256]{2,1,0:T(8,128)(2,1)S(1)} all-to-all(bf16[128,16,256]{2,1,0:T(8,128)(2,1)S(1)} %bitcast.28), channel_id=1, replica_groups=mesh['gx'=128,'ta'=2] {'gx'}, dimensions={0} | all-to-all | bytes 2097152 | tf_op jit(solution)/shard_map/all_to_all | solution.py:143
  229.7 0.0 slice-done
  229.7 0.0 slice-done.1
  229.7 3.8 %fusion.23 = f32[128,16,256]{2,1,0:T(8,128)} fusion(bf16[128,16,2048]{2,1,0:T(8,128)(2,1)S(1)} %bitcast.36, bf16[2048,256,1]{1,0,2:T(8,128)(2,1)S(1)} %bitcast.29), kind=kOutput, calls=%fused_computation.55 | convolution fusion | flops 2147483648 | bytes 11534336 | tf_op jit(solution)/shard_map/dot_general | solution.py:120
  233.5 7.6 %all-to-all-start.2 = ((f32[128,16,256]{2,1,0:T(8,128)}), f32[128,16,256]{2,1,0:T(8,128)S(1)}, u32[]{:S(2)}, u32[]{:S(2)}) async-start(f32[128,16,256]{2,1,0:T(8,128)} %fusion.23), calls=%async_computation.2 | async-start | bytes 4194304 | tf_op jit(solution)/shard_map/all_to_all | solution.py:143
  241.1 48.4 %all-to-all-done.2 = f32[128,16,256]{2,1,0:T(8,128)S(1)} async-done(((f32[128,16,256]{2,1,0:T(8,128)}), f32[128,16,256]{2,1,0:T(8,128)S(1)}, u32[]{:S(2)}, u32[]{:S(2)}) %all-to-all-start.2) | async-done | bytes 2097184 | tf_op jit(solution)/shard_map/all_to_all | solution.py:143
  289.6 1.6 gather_fusion.2
  291.1 5.3 %collective-permute-start.3 = (f32[512,256]{1,0:T(8,128)S(1)}, f32[512,256]{1,0:T(8,128)}, u32[]{:S(2)}, u32[]{:S(2)}) collective-permute-start(f32[512,256]{1,0:T(8,128)S(1)} %gather_fusion.2), channel_id=1, source_target_pairs={{0,1},{1,0},{2,3},{3,2},{4,5},{5,4},{6,7},{7,6},{8,9},{9,8},{10,11... | collective-permute-start | bytes 1572872 | tf_op jit(solution)/shard_map/ppermute | solution.py:146
  296.4 1.6 gather_fusion.1
  298.0 0.1 collective-permute-start.2
  298.1 1.1 convert_element_type.52
  299.3 0.0 collective-permute-done.3
  299.3 0.7 collective-permute-done.2
  300.0 2.3 fusion.17
  (12 shorter events, 0.1 us)
Async XLA Ops:
  0.0 6.0 %copy-start = (bf16[1024,256]{1,0:T(8,128)(2,1)S(1)}, bf16[1024,256]{1,0:T(8,128)(2,1)}, u32[]{:S(2)}) copy-start(bf16[1024,256]{1,0:T(8,128)(2,1)} %param.4) | copy-start | bytes 1572868
  11.2 16.7 %copy-start.3 = (s32[1,1024,1]{1,2,0:T(1,128)S(1)}, s32[1,1024,1]{1,2,0:T(1,128)}, u32[]{:S(2)}) copy-start(s32[1,1024,1]{1,2,0:T(1,128)} %param.5) | copy-start | bytes 12292
  11.2 87.3 %all-to-all-start = ((bf16[128,16,768]{2,1,0:T(8,128)(2,1)}), bf16[128,16,768]{2,1,0:T(8,128)(2,1)S(1)}, u32[]{:S(2)}, u32[]{:S(2)}) async-start(bf16[128,16,768]{2,1,0:T(8,128)(2,1)} %bitcast.26), calls=%async_computation | async-start | bytes 6291456 | tf_op jit(solution)/shard_map/all_to_all | solution.py:143
  106.4 4.0 %copy-start.4 = (bf16[2048,2048]{1,0:T(8,128)(2,1)}, bf16[2048,2048]{1,0:T(8,128)(2,1)S(1)}, u32[]{:S(2)}) copy-start(bf16[2048,2048]{1,0:T(8,128)(2,1)S(1)} %get-tuple-element.16) | copy-start | bytes 25165828
  174.7 7.7 %copy-start.2 = (f32[128,16]{1,0:T(8,128)S(1)}, f32[128,16]{1,0:T(8,128)}, u32[]{:S(2)}) copy-start(f32[128,16]{1,0:T(8,128)} %get-tuple-element.8) | copy-start | bytes 24580
  174.7 10.0 %copy-start.1 = (bf16[1024,256]{1,0:T(8,128)(2,1)S(1)}, bf16[1024,256]{1,0:T(8,128)(2,1)}, u32[]{:S(2)}) copy-start(bf16[1024,256]{1,0:T(8,128)(2,1)} %param.4) | copy-start | bytes 1572868
  179.8 4.9 %collective-permute-start = (f32[1024,256]{1,0:T(8,128)S(1)}, f32[1024,256]{1,0:T(8,128)S(1)}, u32[]{:S(2)}, u32[]{:S(2)}) collective-permute-start(f32[1024,256]{1,0:T(8,128)S(1)} %gather_fusion), channel_id=1, source_target_pairs={{0,1},{1,0},{2,3},{3,2},{4,5},{5,4},{6,7},{7,6},{8,9},{9,8},{10,11... | collective-permute-start | bytes 3145736 | tf_op jit(solution)/shard_map/ppermute | solution.py:146
  183.5 1.3 collective-permute-start.1
  184.7 45.0 %slice-start = ((s8[8388608]{0:T(1024)(128)(4,1)}), s8[4194304]{0:T(1024)(128)(4,1)S(1)}, s32[]{:S(2)}) async-start(s8[8388608]{0:T(1024)(128)(4,1)} %bitcast.34), calls=%async_computation.3 | async-start | bytes 8388608
  184.7 45.0 %slice-start.1 = ((s8[8388608]{0:T(1024)(128)(4,1)}), s8[4194304]{0:T(1024)(128)(4,1)S(1)}, s32[]{:S(2)}) async-start(s8[8388608]{0:T(1024)(128)(4,1)} %bitcast.34), calls=%async_computation.4 | async-start | bytes 8388608
  233.5 56.1 %all-to-all-start.2 = ((f32[128,16,256]{2,1,0:T(8,128)}), f32[128,16,256]{2,1,0:T(8,128)S(1)}, u32[]{:S(2)}, u32[]{:S(2)}) async-start(f32[128,16,256]{2,1,0:T(8,128)} %fusion.23), calls=%async_computation.2 | async-start | bytes 4194304 | tf_op jit(solution)/shard_map/all_to_all | solution.py:143
  291.1 8.1 %collective-permute-start.3 = (f32[512,256]{1,0:T(8,128)S(1)}, f32[512,256]{1,0:T(8,128)}, u32[]{:S(2)}, u32[]{:S(2)}) collective-permute-start(f32[512,256]{1,0:T(8,128)S(1)} %gather_fusion.2), channel_id=1, source_target_pairs={{0,1},{1,0},{2,3},{3,2},{4,5},{5,4},{6,7},{7,6},{8,9},{9,8},{10,11... | collective-permute-start | bytes 1572872 | tf_op jit(solution)/shard_map/ppermute | solution.py:146
  298.0 2.0 collective-permute-start.2

commit v10 on v4

--- a/solution.py
+++ b/solution.py
@@ -139,6 +139,14 @@
     def place(payload):
         return jnp.dot(place_mat, payload, preferred_element_type=jnp.float32).astype(payload.dtype)
 
+    def to_items(values):
+        hi = values.astype(jnp.bfloat16)
+        lo = (values - hi.astype(jnp.float32)).astype(jnp.bfloat16)
+        pick = lambda part: lax.dot_general(
+            place_mat, part, (((0,), (0,)), ((), ())), preferred_element_type=jnp.float32
+        )
+        return pick(hi) + pick(lo)
+
     def exchange(buffer):
         return lax.all_to_all(buffer, "gx", split_axis=0, concat_axis=0, tiled=True)
 
@@ -161,8 +169,8 @@
     back_num, back_den = all_to_all([num1.reshape(groups, slot, width_l), den.reshape(groups, slot)], 0)
     back_num = back_num.reshape(groups * slot, width_l)
     back_den = back_den.reshape(groups * slot)
-    row_num = back_num[target]
-    row_den = jnp.broadcast_to(back_den[:, None], (groups * slot, 128))[target][:, 0]
+    row_num = to_items(back_num)
+    row_den = jnp.sum(jnp.where(target[None, :] == slots[:, None], back_den[:, None], 0.0), axis=0)
     other_num, other_den = other_core((row_num, row_den))
     total_num = row_num + other_num
     total_den = row_den + other_den
@@ -172,7 +180,7 @@
     feats1 = exchange(place(first.astype(jnp.bfloat16)).reshape(groups, slot, -1))
     num2 = weighted_sums(blocks, feats1.reshape(groups * slot, -1))
     back2 = exchange(num2.reshape(groups, slot, -1)).reshape(groups * slot, -1)
-    row_num2 = back2[target]
+    row_num2 = to_items(back2)
     total_num2 = row_num2 + other_core(row_num2)
     return (1.0 - alpha_mix) * prior + alpha_mix * total_num2 / scale
 

time: 303 us -> 300 us (0.990)
  blocking collectives: 99.4 us -> 186 us
  waiting for transfers between devices: 74 us -> 3.43 us
  starting transfers between devices: 24.5 us -> 8.16 us
  local copies, waits for them, and re-layouts: 12.7 us -> 0.81 us
  matrix products: 22.3 us -> 29.4 us
    all_to_all x2 -> x3, blocking collectives: 99.4 us -> 186 us  [exchange(): return lax.all_to_all(buffer, 'gx', split_axis=0, concat_axis=0, tiled=True)]
    all_to_all x1 -> x0, waiting for transfers between devices: 70.6 us -> none  [exchange(): return lax.all_to_all(buffer, 'gx', split_axis=0, concat_axis=0, tiled=True)]
    all_to_all x1 -> x0, starting transfers between devices: 16.6 us -> none  [exchange(): return lax.all_to_all(buffer, 'gx', split_axis=0, concat_axis=0, tiled=True)]
    gather x3 -> x0, local copies, waits for them, and re-layouts: 11.4 us -> none  [the longest x1 5.08 us: body(): row_num = back_num[target]]
    dot_general x0 -> x4, matrix products: none -> 9.43 us  [to_items(): lax.dot_general(place_mat, part, (((0,), (0,)), ((), ())), preferred_elem...]
  transfers between devices with their start and end apart: 4 -> 3, of which waited for: 3 -> 2; matrix products, arithmetic and copies ran while one was open for 1% -> 0% of each run, Pallas kernels for 0% -> 0%
where the time goes in v10:
time: 300 us
  blocking collectives  186 us (62%)
  Pallas kernels  61.2 us (20%)
  matrix products  29.4 us (10%)
  other arithmetic  10.5 us (4%)
  starting transfers between devices  8.16 us (3%)
  waiting for transfers between devices  3.43 us (1%)
    all_to_all x3, blocking collectives, exchange(): return lax.all_to_all(buffer, 'gx', split_axis=0, concat_axis=0, tiled=True)  186 us
    pallas_call x1, Pallas kernels, all_to_all(): pl.pallas_call(functools.partial(a2a_kernel, count), out_shape=[jax.Shape...  61.2 us
    dot_general x4, matrix products, to_items(): lax.dot_general(place_mat, part, (((0,), (0,)), ((), ())), preferred_elem...  9.43 us
    ppermute x3, starting transfers between devices, other_core(): return lax.ppermute(values, 'ta', perm=[(0, 1), (1, 0)])  8.16 us
    dot_general x1, matrix products, bucket_weights(): lax.dot_general(unit[start:start + block], unit, (((1,), (1,)), ((), ()))...  7.46 us
    dot_general x2, matrix products, weighted_sums(): jnp.dot(w, feats, preferred_element_type=jnp.float32)  6.51 us
  transfers between devices with their start and end apart: 3, of which 2 were waited for; matrix products, arithmetic and copies ran while one was open for 0% of the time, Pallas kernels for 0%

profile of v10, /device:TPU:1, one launch (start us, length us, event | category | flops | bytes accessed | tf_op | source)
XLA Modules:
  0.0 300.0 jit_solution(7718646277558543429)
XLA Ops:
  0.0 0.0 copy-start
  0.0 1.3 convert_reduce_fusion.2
  1.3 0.7 multiply_add_fusion
  2.0 1.5 fusion.16
  3.5 0.9 convert_reduce_fusion.1
  4.4 1.5 fusion.17
  6.0 0.0 copy-done
  6.0 4.1 %and_select_fusion = bf16[2048,768]{1,0:T(8,128)(2,1)S(1)} fusion(pred[768]{0:T(1024)(128)(4,1)S(1)} %iota_compare_fusion.19, pred[2048]{0:T(1024)(128)(4,1)S(1)} %compare_not_fusion, s32[1024]{0:T(1024)S(1)} %multiply_add_fusion, bf16[1024,256]{1,0:T(8,128)(2,1)S(1)} %copy-done, bf16[1024,512]{1,0:T(8,128)(2,1)S(1)} %fusion.17), kind=kOutput, calls=%fused_computation.13 | convolution fusion | flops 3231186944 | bytes 4725504 | tf_op jit(solution)/shard_map/dot_general | solution.py:140
  10.1 87.0 %all_to_all.15 = bf16[128,16,768]{2,1,0:T(8,128)(2,1)S(1)} all-to-all(bf16[128,16,768]{2,1,0:T(8,128)(2,1)S(1)} %bitcast.31), channel_id=1, replica_groups=mesh['gx'=128,'ta'=2] {'gx'}, dimensions={0} | all-to-all | bytes 6291456 | tf_op jit(solution)/shard_map/all_to_all | solution.py:151
  97.1 0.2 convert_reduce_fusion.3
  97.3 7.5 %convert_reduce_fusion = (f32[2048]{0:T(1024)S(1)}, bf16[2048,2048]{1,0:T(8,128)(2,1)S(1)}) fusion(f32[2048]{0:T(1024)S(1)} %convert_reduce_fusion.3, bf16[2048,768]{1,0:T(8,128)(2,1)S(1)} %bitcast.29), kind=kOutput, calls=%fused_computation | convolution fusion | flops 4324325376 | bytes 10502144 | tf_op jit(solution)/shard_map/dot_general | solution.py:103
  104.8 0.0 copy-start.2
  104.8 4.0 %fusion.26 = f32[2048,256]{1,0:T(8,128)} fusion(bf16[2048,2048]{1,0:T(8,128)(2,1)S(1)} %get-tuple-element.14, bf16[2048,768]{1,0:T(8,128)(2,1)S(1)} %bitcast.30), kind=kOutput, calls=%fused_computation.41 | convolution fusion | flops 2147483648 | bytes 11534336 | tf_op jit(solution)/shard_map/dot_general | solution.py:120
  108.8 0.0 copy-done.2
  108.8 0.7 reshape.64.refs_1_
  109.5 61.2 %shard_map.37 = (f32[128,16,256]{2,1,0:T(8,128)}, f32[128,16]{1,0:T(8,128)}) custom-call(f32[128,16,256]{2,1,0:T(8,128)} %bitcast.32, f32[128,16]{1,0:T(8,128)} %reshape.64.refs_1_), custom_call_target="tpu_custom_call" | custom-call | tf_op jit(solution)/shard_map/pallas_call | solution.py:82
  170.7 1.8 fusion.20
  172.5 2.4 fusion.3
  174.9 0.0 copy-start.1
  174.9 2.4 fusion.24
  177.2 3.1 %collective-permute-start = (f32[1024,256]{1,0:T(8,128)S(1)}, f32[1024,256]{1,0:T(8,128)S(1)}, u32[]{:S(2)}, u32[]{:S(2)}) collective-permute-start(f32[1024,256]{1,0:T(8,128)S(1)} %fusion.24), channel_id=1, source_target_pairs={{0,1},{1,0},{2,3},{3,2},{4,5},{5,4},{6,7},{7,6},{8,9},{9,8},{10,11... | collective-permute-start | bytes 3145736 | tf_op jit(solution)/shard_map/ppermute | solution.py:154
  180.3 0.0 copy-done.1
  180.3 0.1 broadcast_in_dim.15
  180.4 1.0 select_reduce_fusion
  181.3 0.1 collective-permute-start.1
  181.5 1.1 collective-permute-done.1
  182.6 0.0 slice-start
  182.6 0.0 slice-start.1
  182.6 0.0 collective-permute-done
  182.6 1.9 fusion.15
  184.5 43.2 %all_to_all.16 = bf16[128,16,256]{2,1,0:T(8,128)(2,1)S(1)} all-to-all(bf16[128,16,256]{2,1,0:T(8,128)(2,1)S(1)} %bitcast.33), channel_id=1, replica_groups=mesh['gx'=128,'ta'=2] {'gx'}, dimensions={0} | all-to-all | bytes 2097152 | tf_op jit(solution)/shard_map/all_to_all | solution.py:151
  227.7 0.0 slice-done
  227.7 0.0 slice-done.1
  227.7 2.5 fusion.31
  230.2 56.2 %all_to_all.17 = f32[128,16,256]{2,1,0:T(8,128)S(1)} all-to-all(f32[128,16,256]{2,1,0:T(8,128)S(1)} %fusion.31), channel_id=1, replica_groups=mesh['gx'=128,'ta'=2] {'gx'}, dimensions={0} | all-to-all | bytes 4194304 | tf_op jit(solution)/shard_map/all_to_all | solution.py:151
  286.4 0.3 fusion.19
  286.7 2.4 fusion
  289.1 2.4 fusion.25
  291.4 5.0 %collective-permute-start.2 = (f32[1024,256]{1,0:T(8,128)S(1)}, f32[1024,256]{1,0:T(8,128)S(1)}, u32[]{:S(2)}, u32[]{:S(2)}) collective-permute-start(f32[1024,256]{1,0:T(8,128)S(1)} %fusion.25), channel_id=1, source_target_pairs={{0,1},{1,0},{2,3},{3,2},{4,5},{5,4},{6,7},{7,6},{8,9},{9,8},{10,11... | collective-permute-start | bytes 3145736 | tf_op jit(solution)/shard_map/ppermute | solution.py:154
  296.4 2.3 collective-permute-done.2
  298.7 1.3 divide_add_fusion
  (5 shorter events, 0.0 us)
Async XLA Ops:
  0.0 6.0 %copy-start = (bf16[1024,256]{1,0:T(8,128)(2,1)S(1)}, bf16[1024,256]{1,0:T(8,128)(2,1)}, u32[]{:S(2)}) copy-start(bf16[1024,256]{1,0:T(8,128)(2,1)} %param.4) | copy-start | bytes 1572868
  104.8 4.0 %copy-start.2 = (bf16[2048,2048]{1,0:T(8,128)(2,1)}, bf16[2048,2048]{1,0:T(8,128)(2,1)S(1)}, u32[]{:S(2)}) copy-start(bf16[2048,2048]{1,0:T(8,128)(2,1)S(1)} %get-tuple-element.14) | copy-start | bytes 25165828
  174.9 5.4 %copy-start.1 = (f32[128,16]{1,0:T(8,128)S(1)}, f32[128,16]{1,0:T(8,128)}, u32[]{:S(2)}) copy-start(f32[128,16]{1,0:T(8,128)} %get-tuple-element.8) | copy-start | bytes 24580
  177.2 5.4 %collective-permute-start = (f32[1024,256]{1,0:T(8,128)S(1)}, f32[1024,256]{1,0:T(8,128)S(1)}, u32[]{:S(2)}, u32[]{:S(2)}) collective-permute-start(f32[1024,256]{1,0:T(8,128)S(1)} %fusion.24), channel_id=1, source_target_pairs={{0,1},{1,0},{2,3},{3,2},{4,5},{5,4},{6,7},{7,6},{8,9},{9,8},{10,11... | collective-permute-start | bytes 3145736 | tf_op jit(solution)/shard_map/ppermute | solution.py:154
  181.3 1.3 collective-permute-start.1
  182.6 45.1 %slice-start = ((s8[8388608]{0:T(1024)(128)(4,1)}), s8[4194304]{0:T(1024)(128)(4,1)S(1)}, s32[]{:S(2)}) async-start(s8[8388608]{0:T(1024)(128)(4,1)} %bitcast.37), calls=%async_computation.3 | async-start | bytes 8388608
  182.6 45.1 %slice-start.1 = ((s8[8388608]{0:T(1024)(128)(4,1)}), s8[4194304]{0:T(1024)(128)(4,1)S(1)}, s32[]{:S(2)}) async-start(s8[8388608]{0:T(1024)(128)(4,1)} %bitcast.37), calls=%async_computation.4 | async-start | bytes 8388608
  291.4 7.3 %collective-permute-start.2 = (f32[1024,256]{1,0:T(8,128)S(1)}, f32[1024,256]{1,0:T(8,128)S(1)}, u32[]{:S(2)}, u32[]{:S(2)}) collective-permute-start(f32[1024,256]{1,0:T(8,128)S(1)} %fusion.25), channel_id=1, source_target_pairs={{0,1},{1,0},{2,3},{3,2},{4,5},{5,4},{6,7},{7,6},{8,9},{9,8},{10,11... | collective-permute-start | bytes 3145736 | tf_op jit(solution)/shard_map/ppermute | solution.py:154

commit v11 on v10

--- a/solution.py
+++ b/solution.py
@@ -140,10 +140,13 @@
         return jnp.dot(place_mat, payload, preferred_element_type=jnp.float32).astype(payload.dtype)
 
     def to_items(values):
-        hi = values.astype(jnp.bfloat16)
-        lo = (values - hi.astype(jnp.float32)).astype(jnp.bfloat16)
+        hi = lax.reduce_precision(values, exponent_bits=8, mantissa_bits=7)
+        lo = values - hi
         pick = lambda part: lax.dot_general(
-            place_mat, part, (((0,), (0,)), ((), ())), preferred_element_type=jnp.float32
+            place_mat,
+            part.astype(jnp.bfloat16),
+            (((0,), (0,)), ((), ())),
+            preferred_element_type=jnp.float32,
         )
         return pick(hi) + pick(lo)
 

time: 300 us -> 301 us (level)
  no operation moved by 1% of the time
where the time goes in v11:
time: 301 us; the launch traced here: 300 us
  blocking collectives  186 us (62%)
  Pallas kernels  61.2 us (20%)
  matrix products  29.4 us (10%)
  other arithmetic  10.7 us (4%)
  starting transfers between devices  8.16 us (3%)
  waiting for transfers between devices  3.43 us (1%)
    all_to_all x3, blocking collectives, exchange(): return lax.all_to_all(buffer, 'gx', split_axis=0, concat_axis=0, tiled=True)  186 us
    pallas_call x1, Pallas kernels, all_to_all(): pl.pallas_call(functools.partial(a2a_kernel, count), out_shape=[jax.Shape...  61.2 us
    dot_general x4, matrix products, to_items(): lax.dot_general(place_mat, part.astype(jnp.bfloat16), (((0,), (0,)), ((),...  9.43 us
    ppermute x3, starting transfers between devices, other_core(): return lax.ppermute(values, 'ta', perm=[(0, 1), (1, 0)])  8.16 us
    dot_general x1, matrix products, bucket_weights(): lax.dot_general(unit[start:start + block], unit, (((1,), (1,)), ((), ()))...  7.46 us
    dot_general x2, matrix products, weighted_sums(): jnp.dot(w, feats, preferred_element_type=jnp.float32)  6.51 us
  transfers between devices with their start and end apart: 3, of which 2 were waited for; matrix products, arithmetic and copies ran while one was open for 0% of the time, Pallas kernels for 0%

profile of v11, /device:TPU:1, one launch (start us, length us, event | category | flops | bytes accessed | tf_op | source)
XLA Modules:
  0.0 300.2 jit_solution(3637888566935606453)
XLA Ops:
  0.0 0.0 copy-start
  0.0 1.3 convert_reduce_fusion.2
  1.3 0.7 multiply_add_fusion
  2.0 1.5 fusion.16
  3.5 0.9 convert_reduce_fusion.1
  4.4 1.5 fusion.17
  6.0 0.0 copy-done
  6.0 4.1 %and_select_fusion = bf16[2048,768]{1,0:T(8,128)(2,1)S(1)} fusion(pred[768]{0:T(1024)(128)(4,1)S(1)} %iota_compare_fusion.19, pred[2048]{0:T(1024)(128)(4,1)S(1)} %compare_not_fusion, s32[1024]{0:T(1024)S(1)} %multiply_add_fusion, bf16[1024,256]{1,0:T(8,128)(2,1)S(1)} %copy-done, bf16[1024,512]{1,0:T(8,128)(2,1)S(1)} %fusion.17), kind=kOutput, calls=%fused_computation.13 | convolution fusion | flops 3231186944 | bytes 4725504 | tf_op jit(solution)/shard_map/dot_general | solution.py:140
  10.1 87.0 %all_to_all.15 = bf16[128,16,768]{2,1,0:T(8,128)(2,1)S(1)} all-to-all(bf16[128,16,768]{2,1,0:T(8,128)(2,1)S(1)} %bitcast.25), channel_id=1, replica_groups=mesh['gx'=128,'ta'=2] {'gx'}, dimensions={0} | all-to-all | bytes 6291456 | tf_op jit(solution)/shard_map/all_to_all | solution.py:154
  97.1 0.2 convert_reduce_fusion.3
  97.3 7.5 %convert_reduce_fusion = (f32[2048]{0:T(1024)S(1)}, bf16[2048,2048]{1,0:T(8,128)(2,1)S(1)}) fusion(f32[2048]{0:T(1024)S(1)} %convert_reduce_fusion.3, bf16[2048,768]{1,0:T(8,128)(2,1)S(1)} %bitcast.23), kind=kOutput, calls=%fused_computation | convolution fusion | flops 4324325376 | bytes 10502144 | tf_op jit(solution)/shard_map/dot_general | solution.py:103
  104.8 0.0 copy-start.2
  104.8 4.0 %fusion.26 = f32[2048,256]{1,0:T(8,128)} fusion(bf16[2048,2048]{1,0:T(8,128)(2,1)S(1)} %get-tuple-element.14, bf16[2048,768]{1,0:T(8,128)(2,1)S(1)} %bitcast.24), kind=kOutput, calls=%fused_computation.41 | convolution fusion | flops 2147483648 | bytes 11534336 | tf_op jit(solution)/shard_map/dot_general | solution.py:120
  108.8 0.0 copy-done.2
  108.8 0.7 reshape.64.refs_1_
  109.5 61.2 %shard_map.37 = (f32[128,16,256]{2,1,0:T(8,128)}, f32[128,16]{1,0:T(8,128)}) custom-call(f32[128,16,256]{2,1,0:T(8,128)} %bitcast.26, f32[128,16]{1,0:T(8,128)} %reshape.64.refs_1_), custom_call_target="tpu_custom_call" | custom-call | tf_op jit(solution)/shard_map/pallas_call | solution.py:82
  170.7 1.9 reduce-precision_convert_fusion.1
  172.6 2.4 fusion.3
  174.9 0.0 copy-start.1
  174.9 2.4 fusion.24
  177.3 3.1 %collective-permute-start = (f32[1024,256]{1,0:T(8,128)S(1)}, f32[1024,256]{1,0:T(8,128)S(1)}, u32[]{:S(2)}, u32[]{:S(2)}) collective-permute-start(f32[1024,256]{1,0:T(8,128)S(1)} %fusion.24), channel_id=1, source_target_pairs={{0,1},{1,0},{2,3},{3,2},{4,5},{5,4},{6,7},{7,6},{8,9},{9,8},{10,11... | collective-permute-start | bytes 3145736 | tf_op jit(solution)/shard_map/ppermute | solution.py:157
  180.4 0.0 copy-done.1
  180.4 0.1 broadcast_in_dim.15
  180.5 1.0 select_reduce_fusion
  181.4 0.1 collective-permute-start.1
  181.5 1.1 collective-permute-done.1
  182.7 0.0 slice-start
  182.7 0.0 slice-start.1
  182.7 0.0 collective-permute-done
  182.7 1.9 fusion.15
  184.6 43.2 %all_to_all.16 = bf16[128,16,256]{2,1,0:T(8,128)(2,1)S(1)} all-to-all(bf16[128,16,256]{2,1,0:T(8,128)(2,1)S(1)} %bitcast.27), channel_id=1, replica_groups=mesh['gx'=128,'ta'=2] {'gx'}, dimensions={0} | all-to-all | bytes 2097152 | tf_op jit(solution)/shard_map/all_to_all | solution.py:154
  227.8 0.0 slice-done
  227.8 0.0 slice-done.1
  227.8 2.5 fusion.31
  230.3 56.2 %all_to_all.17 = f32[128,16,256]{2,1,0:T(8,128)S(1)} all-to-all(f32[128,16,256]{2,1,0:T(8,128)S(1)} %fusion.31), channel_id=1, replica_groups=mesh['gx'=128,'ta'=2] {'gx'}, dimensions={0} | all-to-all | bytes 4194304 | tf_op jit(solution)/shard_map/all_to_all | solution.py:154
  286.5 0.3 reduce-precision_convert_fusion
  286.9 2.4 fusion
  289.2 2.4 fusion.25
  291.6 5.0 %collective-permute-start.2 = (f32[1024,256]{1,0:T(8,128)S(1)}, f32[1024,256]{1,0:T(8,128)S(1)}, u32[]{:S(2)}, u32[]{:S(2)}) collective-permute-start(f32[1024,256]{1,0:T(8,128)S(1)} %fusion.25), channel_id=1, source_target_pairs={{0,1},{1,0},{2,3},{3,2},{4,5},{5,4},{6,7},{7,6},{8,9},{9,8},{10,11... | collective-permute-start | bytes 3145736 | tf_op jit(solution)/shard_map/ppermute | solution.py:157
  296.6 2.3 collective-permute-done.2
  298.9 1.3 divide_add_fusion
  (5 shorter events, 0.0 us)
Async XLA Ops:
  0.0 6.0 %copy-start = (bf16[1024,256]{1,0:T(8,128)(2,1)S(1)}, bf16[1024,256]{1,0:T(8,128)(2,1)}, u32[]{:S(2)}) copy-start(bf16[1024,256]{1,0:T(8,128)(2,1)} %param.4) | copy-start | bytes 1572868
  104.8 4.0 %copy-start.2 = (bf16[2048,2048]{1,0:T(8,128)(2,1)}, bf16[2048,2048]{1,0:T(8,128)(2,1)S(1)}, u32[]{:S(2)}) copy-start(bf16[2048,2048]{1,0:T(8,128)(2,1)S(1)} %get-tuple-element.14) | copy-start | bytes 25165828
  174.9 5.4 %copy-start.1 = (f32[128,16]{1,0:T(8,128)S(1)}, f32[128,16]{1,0:T(8,128)}, u32[]{:S(2)}) copy-start(f32[128,16]{1,0:T(8,128)} %get-tuple-element.8) | copy-start | bytes 24580
  177.3 5.4 %collective-permute-start = (f32[1024,256]{1,0:T(8,128)S(1)}, f32[1024,256]{1,0:T(8,128)S(1)}, u32[]{:S(2)}, u32[]{:S(2)}) collective-permute-start(f32[1024,256]{1,0:T(8,128)S(1)} %fusion.24), channel_id=1, source_target_pairs={{0,1},{1,0},{2,3},{3,2},{4,5},{5,4},{6,7},{7,6},{8,9},{9,8},{10,11... | collective-permute-start | bytes 3145736 | tf_op jit(solution)/shard_map/ppermute | solution.py:157
  181.4 1.3 collective-permute-start.1
  182.7 45.1 %slice-start = ((s8[8388608]{0:T(1024)(128)(4,1)}), s8[4194304]{0:T(1024)(128)(4,1)S(1)}, s32[]{:S(2)}) async-start(s8[8388608]{0:T(1024)(128)(4,1)} %bitcast.31), calls=%async_computation.3 | async-start | bytes 8388608
  182.7 45.1 %slice-start.1 = ((s8[8388608]{0:T(1024)(128)(4,1)}), s8[4194304]{0:T(1024)(128)(4,1)S(1)}, s32[]{:S(2)}) async-start(s8[8388608]{0:T(1024)(128)(4,1)} %bitcast.31), calls=%async_computation.4 | async-start | bytes 8388608
  291.6 7.3 %collective-permute-start.2 = (f32[1024,256]{1,0:T(8,128)S(1)}, f32[1024,256]{1,0:T(8,128)S(1)}, u32[]{:S(2)}, u32[]{:S(2)}) collective-permute-start(f32[1024,256]{1,0:T(8,128)S(1)} %fusion.25), channel_id=1, source_target_pairs={{0,1},{1,0},{2,3},{3,2},{4,5},{5,4},{6,7},{7,6},{8,9},{9,8},{10,11... | collective-permute-start | bytes 3145736 | tf_op jit(solution)/shard_map/ppermute | solution.py:157

commit v12 on v11

--- a/solution.py
+++ b/solution.py
@@ -56,8 +56,11 @@
             device_id_type=mesh_ids,
         )
 
+    def partner(i):
+        return lax.rem(me + (1 - 2 * lax.rem(i, 2)) * (i // 2 + 1) + n, n)
+
     def send(i, carry):
-        peer = lax.rem(me + 1 + i, n)
+        peer = partner(i)
         for k in range(count):
             copy_with(k, peer, peer, me).start()
         return carry
@@ -65,7 +68,7 @@
     lax.fori_loop(0, n - 1, send, 0)
 
     def finish(i, carry):
-        peer = lax.rem(me + 1 + i, n)
+        peer = partner(i)
         for k in range(count):
             copy_with(k, peer, peer, me).wait_send()
             copy_with(k, peer, peer, peer).wait_recv()

time: 301 us -> 297 us (0.987)
  blocking collectives: 186 us -> 180 us
    all_to_all x3, blocking collectives: 186 us -> 180 us  [exchange(): return lax.all_to_all(buffer, 'gx', split_axis=0, concat_axis=0, tiled=True)]
where the time goes in v12:
time: 297 us
  blocking collectives  180 us (61%)
  Pallas kernels  62.3 us (21%)
  matrix products  29.4 us (10%)
  other arithmetic  10.7 us (4%)
  starting transfers between devices  10.1 us (3%)
  waiting for transfers between devices  3.43 us (1%)
    all_to_all x3, blocking collectives, exchange(): return lax.all_to_all(buffer, 'gx', split_axis=0, concat_axis=0, tiled=True)  180 us
    pallas_call x1, Pallas kernels, all_to_all(): pl.pallas_call(functools.partial(a2a_kernel, count), out_shape=[jax.Shape...  62.3 us
    ppermute x3, starting transfers between devices, other_core(): return lax.ppermute(values, 'ta', perm=[(0, 1), (1, 0)])  10.1 us
    dot_general x4, matrix products, to_items(): lax.dot_general(place_mat, part.astype(jnp.bfloat16), (((0,), (0,)), ((),...  9.43 us
    dot_general x1, matrix products, bucket_weights(): lax.dot_general(unit[start:start + block], unit, (((1,), (1,)), ((), ()))...  7.46 us
    dot_general x2, matrix products, weighted_sums(): jnp.dot(w, feats, preferred_element_type=jnp.float32)  6.51 us
    dot_general x2, matrix products, place(): jnp.dot(place_mat, payload, preferred_element_type=jnp.float32)  5.98 us
  transfers between devices with their start and end apart: 3, of which 2 were waited for; matrix products, arithmetic and copies ran while one was open for 0% of the time, Pallas kernels for 0%

profile of v12, /device:TPU:1, one launch (start us, length us, event | category | flops | bytes accessed | tf_op | source)
XLA Modules:
  0.0 296.7 jit_solution(11245826219181625751)
XLA Ops:
  0.0 0.0 copy-start
  0.0 1.3 convert_reduce_fusion.2
  1.3 0.7 multiply_add_fusion
  2.0 1.5 fusion.16
  3.5 0.9 convert_reduce_fusion.1
  4.4 1.5 fusion.17
  6.0 0.0 copy-done
  6.0 4.1 %and_select_fusion = bf16[2048,768]{1,0:T(8,128)(2,1)S(1)} fusion(pred[768]{0:T(1024)(128)(4,1)S(1)} %iota_compare_fusion.19, pred[2048]{0:T(1024)(128)(4,1)S(1)} %compare_not_fusion, s32[1024]{0:T(1024)S(1)} %multiply_add_fusion, bf16[1024,256]{1,0:T(8,128)(2,1)S(1)} %copy-done, bf16[1024,512]{1,0:T(8,128)(2,1)S(1)} %fusion.17), kind=kOutput, calls=%fused_computation.13 | convolution fusion | flops 3231186944 | bytes 4725504 | tf_op jit(solution)/shard_map/dot_general | solution.py:143
  10.1 87.0 %all_to_all.15 = bf16[128,16,768]{2,1,0:T(8,128)(2,1)S(1)} all-to-all(bf16[128,16,768]{2,1,0:T(8,128)(2,1)S(1)} %bitcast.25), channel_id=1, replica_groups=mesh['gx'=128,'ta'=2] {'gx'}, dimensions={0} | all-to-all | bytes 6291456 | tf_op jit(solution)/shard_map/all_to_all | solution.py:157
  97.1 0.2 convert_reduce_fusion.3
  97.3 7.5 %convert_reduce_fusion = (f32[2048]{0:T(1024)S(1)}, bf16[2048,2048]{1,0:T(8,128)(2,1)S(1)}) fusion(f32[2048]{0:T(1024)S(1)} %convert_reduce_fusion.3, bf16[2048,768]{1,0:T(8,128)(2,1)S(1)} %bitcast.23), kind=kOutput, calls=%fused_computation | convolution fusion | flops 4324325376 | bytes 10502144 | tf_op jit(solution)/shard_map/dot_general | solution.py:106
  104.8 0.0 copy-start.2
  104.8 4.0 %fusion.26 = f32[2048,256]{1,0:T(8,128)} fusion(bf16[2048,2048]{1,0:T(8,128)(2,1)S(1)} %get-tuple-element.14, bf16[2048,768]{1,0:T(8,128)(2,1)S(1)} %bitcast.24), kind=kOutput, calls=%fused_computation.41 | convolution fusion | flops 2147483648 | bytes 11534336 | tf_op jit(solution)/shard_map/dot_general | solution.py:123
  108.8 0.0 copy-done.2
  108.8 0.7 reshape.64.refs_1_
  109.5 62.3 %shard_map.37 = (f32[128,16,256]{2,1,0:T(8,128)}, f32[128,16]{1,0:T(8,128)}) custom-call(f32[128,16,256]{2,1,0:T(8,128)} %bitcast.26, f32[128,16]{1,0:T(8,128)} %reshape.64.refs_1_), custom_call_target="tpu_custom_call" | custom-call | tf_op jit(solution)/shard_map/pallas_call | solution.py:85
  171.8 1.9 reduce-precision_convert_fusion.1
  173.7 2.4 fusion.3
  176.1 0.0 copy-start.1
  176.1 2.4 fusion.24
  178.4 5.0 %collective-permute-start = (f32[1024,256]{1,0:T(8,128)S(1)}, f32[1024,256]{1,0:T(8,128)S(1)}, u32[]{:S(2)}, u32[]{:S(2)}) collective-permute-start(f32[1024,256]{1,0:T(8,128)S(1)} %fusion.24), channel_id=1, source_target_pairs={{0,1},{1,0},{2,3},{3,2},{4,5},{5,4},{6,7},{7,6},{8,9},{9,8},{10,11... | collective-permute-start | bytes 3145736 | tf_op jit(solution)/shard_map/ppermute | solution.py:160
  183.4 0.0 copy-done.1
  183.4 0.1 broadcast_in_dim.15
  183.5 1.0 select_reduce_fusion
  184.5 0.1 collective-permute-start.1
  184.6 1.1 collective-permute-done.1
  185.7 0.0 slice-start
  185.7 0.0 slice-start.1
  185.7 0.0 collective-permute-done
  185.8 1.9 fusion.15
  187.6 36.7 %all_to_all.16 = bf16[128,16,256]{2,1,0:T(8,128)(2,1)S(1)} all-to-all(bf16[128,16,256]{2,1,0:T(8,128)(2,1)S(1)} %bitcast.27), channel_id=1, replica_groups=mesh['gx'=128,'ta'=2] {'gx'}, dimensions={0} | all-to-all | bytes 2097152 | tf_op jit(solution)/shard_map/all_to_all | solution.py:157
  224.3 0.0 slice-done
  224.3 0.0 slice-done.1
  224.3 2.5 fusion.31
  226.8 56.2 %all_to_all.17 = f32[128,16,256]{2,1,0:T(8,128)S(1)} all-to-all(f32[128,16,256]{2,1,0:T(8,128)S(1)} %fusion.31), channel_id=1, replica_groups=mesh['gx'=128,'ta'=2] {'gx'}, dimensions={0} | all-to-all | bytes 4194304 | tf_op jit(solution)/shard_map/all_to_all | solution.py:157
  283.1 0.3 reduce-precision_convert_fusion
  283.4 2.4 fusion
  285.8 2.4 fusion.25
  288.2 5.0 %collective-permute-start.2 = (f32[1024,256]{1,0:T(8,128)S(1)}, f32[1024,256]{1,0:T(8,128)S(1)}, u32[]{:S(2)}, u32[]{:S(2)}) collective-permute-start(f32[1024,256]{1,0:T(8,128)S(1)} %fusion.25), channel_id=1, source_target_pairs={{0,1},{1,0},{2,3},{3,2},{4,5},{5,4},{6,7},{7,6},{8,9},{9,8},{10,11... | collective-permute-start | bytes 3145736 | tf_op jit(solution)/shard_map/ppermute | solution.py:160
  293.1 2.3 collective-permute-done.2
  295.4 1.3 divide_add_fusion
  (5 shorter events, 0.0 us)
Async XLA Ops:
  0.0 6.0 %copy-start = (bf16[1024,256]{1,0:T(8,128)(2,1)S(1)}, bf16[1024,256]{1,0:T(8,128)(2,1)}, u32[]{:S(2)}) copy-start(bf16[1024,256]{1,0:T(8,128)(2,1)} %param.4) | copy-start | bytes 1572868
  104.8 4.0 %copy-start.2 = (bf16[2048,2048]{1,0:T(8,128)(2,1)}, bf16[2048,2048]{1,0:T(8,128)(2,1)S(1)}, u32[]{:S(2)}) copy-start(bf16[2048,2048]{1,0:T(8,128)(2,1)S(1)} %get-tuple-element.14) | copy-start | bytes 25165828
  176.1 7.4 %copy-start.1 = (f32[128,16]{1,0:T(8,128)S(1)}, f32[128,16]{1,0:T(8,128)}, u32[]{:S(2)}) copy-start(f32[128,16]{1,0:T(8,128)} %get-tuple-element.8) | copy-start | bytes 24580
  178.4 7.3 %collective-permute-start = (f32[1024,256]{1,0:T(8,128)S(1)}, f32[1024,256]{1,0:T(8,128)S(1)}, u32[]{:S(2)}, u32[]{:S(2)}) collective-permute-start(f32[1024,256]{1,0:T(8,128)S(1)} %fusion.24), channel_id=1, source_target_pairs={{0,1},{1,0},{2,3},{3,2},{4,5},{5,4},{6,7},{7,6},{8,9},{9,8},{10,11... | collective-permute-start | bytes 3145736 | tf_op jit(solution)/shard_map/ppermute | solution.py:160
  184.5 1.3 collective-permute-start.1
  185.7 38.6 %slice-start = ((s8[8388608]{0:T(1024)(128)(4,1)}), s8[4194304]{0:T(1024)(128)(4,1)S(1)}, s32[]{:S(2)}) async-start(s8[8388608]{0:T(1024)(128)(4,1)} %bitcast.31), calls=%async_computation.3 | async-start | bytes 8388608
  185.7 38.6 %slice-start.1 = ((s8[8388608]{0:T(1024)(128)(4,1)}), s8[4194304]{0:T(1024)(128)(4,1)S(1)}, s32[]{:S(2)}) async-start(s8[8388608]{0:T(1024)(128)(4,1)} %bitcast.31), calls=%async_computation.4 | async-start | bytes 8388608
  288.2 7.3 %collective-permute-start.2 = (f32[1024,256]{1,0:T(8,128)S(1)}, f32[1024,256]{1,0:T(8,128)S(1)}, u32[]{:S(2)}, u32[]{:S(2)}) collective-permute-start(f32[1024,256]{1,0:T(8,128)S(1)} %fusion.25), channel_id=1, source_target_pairs={{0,1},{1,0},{2,3},{3,2},{4,5},{5,4},{6,7},{7,6},{8,9},{9,8},{10,11... | collective-permute-start | bytes 3145736 | tf_op jit(solution)/shard_map/ppermute | solution.py:160

commit v13 on v12

--- a/solution.py
+++ b/solution.py
@@ -185,7 +185,8 @@
 
     feats1 = exchange(place(first.astype(jnp.bfloat16)).reshape(groups, slot, -1))
     num2 = weighted_sums(blocks, feats1.reshape(groups * slot, -1))
-    back2 = exchange(num2.reshape(groups, slot, -1)).reshape(groups * slot, -1)
+    (back2,) = all_to_all([num2.reshape(groups, slot, width_l)], 1)
+    back2 = back2.reshape(groups * slot, width_l)
     row_num2 = to_items(back2)
     total_num2 = row_num2 + other_core(row_num2)
     return (1.0 - alpha_mix) * prior + alpha_mix * total_num2 / scale

time: 297 us -> 298 us (level)
  blocking collectives: 180 us -> 124 us
  Pallas kernels: 62.3 us -> 115 us
    all_to_all x3 -> x2, blocking collectives: 180 us -> 124 us  [exchange(): return lax.all_to_all(buffer, 'gx', split_axis=0, concat_axis=0, tiled=True)]
    pallas_call x1 -> x2, Pallas kernels: 62.3 us -> 115 us  [all_to_all(): pl.pallas_call(functools.partial(a2a_kernel, count), out_shape=[jax.Shape...]
where the time goes in v13:
time: 298 us
  blocking collectives  124 us (42%)
  Pallas kernels  115 us (39%)
  matrix products  30.6 us (10%)
  other arithmetic  12.3 us (4%)
  starting transfers between devices  11.3 us (4%)
  waiting for transfers between devices  3.43 us (1%)
    all_to_all x2, blocking collectives, exchange(): return lax.all_to_all(buffer, 'gx', split_axis=0, concat_axis=0, tiled=True)  124 us
    pallas_call x2, Pallas kernels, all_to_all(): pl.pallas_call(functools.partial(a2a_kernel, count), out_shape=[jax.Shape...  115 us
    ppermute x3, starting transfers between devices, other_core(): return lax.ppermute(values, 'ta', perm=[(0, 1), (1, 0)])  11.3 us
    dot_general x4, matrix products, to_items(): lax.dot_general(place_mat, part.astype(jnp.bfloat16), (((0,), (0,)), ((),...  9.43 us
    dot_general x2, matrix products, weighted_sums(): jnp.dot(w, feats, preferred_element_type=jnp.float32)  7.77 us
    dot_general x1, matrix products, bucket_weights(): lax.dot_general(unit[start:start + block], unit, (((1,), (1,)), ((), ()))...  7.46 us
    dot_general x2, matrix products, place(): jnp.dot(place_mat, payload, preferred_element_type=jnp.float32)  5.98 us
  transfers between devices with their start and end apart: 3, of which 2 were waited for; matrix products, arithmetic and copies ran while one was open for 0% of the time, Pallas kernels for 0%

profile of v13, /device:TPU:1, one launch (start us, length us, event | category | flops | bytes accessed | tf_op | source)
XLA Modules:
  0.0 297.5 jit_solution(3285676494341153310)
XLA Ops:
  0.0 0.0 copy-start
  0.0 1.3 convert_reduce_fusion.2
  1.3 0.7 multiply_add_fusion
  2.0 1.5 fusion.16
  3.5 0.9 convert_reduce_fusion.1
  4.4 1.5 fusion.17
  6.0 0.0 copy-done
  6.0 4.1 %and_select_fusion = bf16[2048,768]{1,0:T(8,128)(2,1)S(1)} fusion(pred[768]{0:T(1024)(128)(4,1)S(1)} %iota_compare_fusion.19, pred[2048]{0:T(1024)(128)(4,1)S(1)} %compare_not_fusion, s32[1024]{0:T(1024)S(1)} %multiply_add_fusion, bf16[1024,256]{1,0:T(8,128)(2,1)S(1)} %copy-done, bf16[1024,512]{1,0:T(8,128)(2,1)S(1)} %fusion.17), kind=kOutput, calls=%fused_computation.13 | convolution fusion | flops 3231186944 | bytes 4725504 | tf_op jit(solution)/shard_map/dot_general | solution.py:143
  10.1 87.0 %all_to_all.10 = bf16[128,16,768]{2,1,0:T(8,128)(2,1)S(1)} all-to-all(bf16[128,16,768]{2,1,0:T(8,128)(2,1)S(1)} %bitcast.25), channel_id=1, replica_groups=mesh['gx'=128,'ta'=2] {'gx'}, dimensions={0} | all-to-all | bytes 6291456 | tf_op jit(solution)/shard_map/all_to_all | solution.py:157
  97.1 0.2 convert_reduce_fusion.3
  97.3 7.5 %convert_reduce_fusion = (f32[2048]{0:T(1024)S(1)}, bf16[2048,2048]{1,0:T(8,128)(2,1)S(1)}) fusion(f32[2048]{0:T(1024)S(1)} %convert_reduce_fusion.3, bf16[2048,768]{1,0:T(8,128)(2,1)S(1)} %bitcast.23), kind=kOutput, calls=%fused_computation | convolution fusion | flops 4324325376 | bytes 10502144 | tf_op jit(solution)/shard_map/dot_general | solution.py:106
  104.8 0.0 copy-start.2
  104.8 4.0 %fusion.26 = f32[2048,256]{1,0:T(8,128)} fusion(bf16[2048,2048]{1,0:T(8,128)(2,1)S(1)} %get-tuple-element.14, bf16[2048,768]{1,0:T(8,128)(2,1)S(1)} %bitcast.24), kind=kOutput, calls=%fused_computation.41 | convolution fusion | flops 2147483648 | bytes 11534336 | tf_op jit(solution)/shard_map/dot_general | solution.py:123
  108.8 0.0 copy-done.2
  108.8 0.7 reshape.64.refs_1_
  109.5 62.3 %shard_map.37 = (f32[128,16,256]{2,1,0:T(8,128)}, f32[128,16]{1,0:T(8,128)}) custom-call(f32[128,16,256]{2,1,0:T(8,128)} %bitcast.26, f32[128,16]{1,0:T(8,128)} %reshape.64.refs_1_), custom_call_target="tpu_custom_call" | custom-call | tf_op jit(solution)/shard_map/pallas_call | solution.py:85
  171.8 1.9 reduce-precision_convert_fusion.1
  173.7 2.4 fusion.3
  176.1 0.0 copy-start.1
  176.1 2.4 fusion.24
  178.4 5.0 %collective-permute-start = (f32[1024,256]{1,0:T(8,128)S(1)}, f32[1024,256]{1,0:T(8,128)S(1)}, u32[]{:S(2)}, u32[]{:S(2)}) collective-permute-start(f32[1024,256]{1,0:T(8,128)S(1)} %fusion.24), channel_id=1, source_target_pairs={{0,1},{1,0},{2,3},{3,2},{4,5},{5,4},{6,7},{7,6},{8,9},{9,8},{10,11... | collective-permute-start | bytes 3145736 | tf_op jit(solution)/shard_map/ppermute | solution.py:160
  183.4 0.0 copy-done.1
  183.4 0.1 broadcast_in_dim.15
  183.5 1.0 select_reduce_fusion
  184.5 0.1 collective-permute-start.1
  184.6 1.1 collective-permute-done.1
  185.7 0.0 slice-start
  185.7 0.0 slice-start.1
  185.7 0.0 collective-permute-done
  185.8 1.9 fusion.15
  187.6 36.7 %all_to_all.11 = bf16[128,16,256]{2,1,0:T(8,128)(2,1)S(1)} all-to-all(bf16[128,16,256]{2,1,0:T(8,128)(2,1)S(1)} %bitcast.27), channel_id=1, replica_groups=mesh['gx'=128,'ta'=2] {'gx'}, dimensions={0} | all-to-all | bytes 2097152 | tf_op jit(solution)/shard_map/all_to_all | solution.py:157
  224.3 0.0 slice-done
  224.3 0.0 slice-done.1
  224.3 3.8 %fusion.31.refs_0_ = f32[128,16,256]{2,1,0:T(8,128)} fusion(bf16[128,16,2048]{2,1,0:T(8,128)(2,1)S(1)} %bitcast.33, bf16[2048,256,1]{1,0,2:T(8,128)(2,1)S(1)} %bitcast.28), kind=kOutput, calls=%fused_computation.56 | convolution fusion | flops 2147483648 | bytes 11534336 | tf_op jit(solution)/shard_map/dot_general | solution.py:123
  228.1 52.9 %shard_map.38 = f32[128,16,256]{2,1,0:T(8,128)} custom-call(f32[128,16,256]{2,1,0:T(8,128)} %fusion.31.refs_0_), custom_call_target="tpu_custom_call" | custom-call | tf_op jit(solution)/shard_map/pallas_call | solution.py:85
  281.0 1.9 reduce-precision_convert_fusion
  283.0 2.4 fusion
  285.3 2.4 fusion.25
  287.7 6.2 %collective-permute-start.2 = (f32[1024,256]{1,0:T(8,128)S(1)}, f32[1024,256]{1,0:T(8,128)S(1)}, u32[]{:S(2)}, u32[]{:S(2)}) collective-permute-start(f32[1024,256]{1,0:T(8,128)S(1)} %fusion.25), channel_id=1, source_target_pairs={{0,1},{1,0},{2,3},{3,2},{4,5},{5,4},{6,7},{7,6},{8,9},{9,8},{10,11... | collective-permute-start | bytes 3145736 | tf_op jit(solution)/shard_map/ppermute | solution.py:160
  293.9 2.3 collective-permute-done.2
  296.2 1.3 divide_add_fusion
  (5 shorter events, 0.0 us)
Async XLA Ops:
  0.0 6.0 %copy-start = (bf16[1024,256]{1,0:T(8,128)(2,1)S(1)}, bf16[1024,256]{1,0:T(8,128)(2,1)}, u32[]{:S(2)}) copy-start(bf16[1024,256]{1,0:T(8,128)(2,1)} %param.4) | copy-start | bytes 1572868
  104.8 4.0 %copy-start.2 = (bf16[2048,2048]{1,0:T(8,128)(2,1)}, bf16[2048,2048]{1,0:T(8,128)(2,1)S(1)}, u32[]{:S(2)}) copy-start(bf16[2048,2048]{1,0:T(8,128)(2,1)S(1)} %get-tuple-element.14) | copy-start | bytes 25165828
  176.1 7.4 %copy-start.1 = (f32[128,16]{1,0:T(8,128)S(1)}, f32[128,16]{1,0:T(8,128)}, u32[]{:S(2)}) copy-start(f32[128,16]{1,0:T(8,128)} %get-tuple-element.8) | copy-start | bytes 24580
  178.4 7.3 %collective-permute-start = (f32[1024,256]{1,0:T(8,128)S(1)}, f32[1024,256]{1,0:T(8,128)S(1)}, u32[]{:S(2)}, u32[]{:S(2)}) collective-permute-start(f32[1024,256]{1,0:T(8,128)S(1)} %fusion.24), channel_id=1, source_target_pairs={{0,1},{1,0},{2,3},{3,2},{4,5},{5,4},{6,7},{7,6},{8,9},{9,8},{10,11... | collective-permute-start | bytes 3145736 | tf_op jit(solution)/shard_map/ppermute | solution.py:160
  184.5 1.3 collective-permute-start.1
  185.7 38.6 %slice-start = ((s8[8388608]{0:T(1024)(128)(4,1)}), s8[4194304]{0:T(1024)(128)(4,1)S(1)}, s32[]{:S(2)}) async-start(s8[8388608]{0:T(1024)(128)(4,1)} %bitcast.31), calls=%async_computation.2 | async-start | bytes 8388608
  185.7 38.6 %slice-start.1 = ((s8[8388608]{0:T(1024)(128)(4,1)}), s8[4194304]{0:T(1024)(128)(4,1)S(1)}, s32[]{:S(2)}) async-start(s8[8388608]{0:T(1024)(128)(4,1)} %bitcast.31), calls=%async_computation.3 | async-start | bytes 8388608
  287.7 8.5 %collective-permute-start.2 = (f32[1024,256]{1,0:T(8,128)S(1)}, f32[1024,256]{1,0:T(8,128)S(1)}, u32[]{:S(2)}, u32[]{:S(2)}) collective-permute-start(f32[1024,256]{1,0:T(8,128)S(1)} %fusion.25), channel_id=1, source_target_pairs={{0,1},{1,0},{2,3},{3,2},{4,5},{5,4},{6,7},{7,6},{8,9},{9,8},{10,11... | collective-permute-start | bytes 3145736 | tf_op jit(solution)/shard_map/ppermute | solution.py:160

commit v14 on v6

--- a/solution.py
+++ b/solution.py
@@ -56,8 +56,11 @@
             device_id_type=mesh_ids,
         )
 
+    def partner(i):
+        return lax.rem(me + (1 - 2 * lax.rem(i, 2)) * (i // 2 + 1) + n, n)
+
     def send(i, carry):
-        peer = lax.rem(me + 1 + i, n)
+        peer = partner(i)
         for k in range(count):
             copy_with(k, peer, peer, me).start()
         return carry
@@ -65,7 +68,7 @@
     lax.fori_loop(0, n - 1, send, 0)
 
     def finish(i, carry):
-        peer = lax.rem(me + 1 + i, n)
+        peer = partner(i)
         for k in range(count):
             copy_with(k, peer, peer, me).wait_send()
             copy_with(k, peer, peer, peer).wait_recv()

time: 301 us -> 298 us (0.990)
  blocking collectives: 43.5 us -> 37 us
    all_to_all x1, blocking collectives: 43.5 us -> 37 us  [exchange(): return lax.all_to_all(buffer, 'gx', split_axis=0, concat_axis=0, tiled=True)]
where the time goes in v14:
time: 298 us; the launch traced here: 297 us
  waiting for transfers between devices  121 us (41%)
  Pallas kernels  62.1 us (21%)
  blocking collectives  37 us (12%)
  starting transfers between devices  34.7 us (12%)
  matrix products  22.4 us (8%)
  other arithmetic  10.6 us (4%)
  local copies, waits for them, and re-layouts  9.07 us (3%)
    all_to_all x2, waiting for transfers between devices, exchange(): return lax.all_to_all(buffer, 'gx', split_axis=0, concat_axis=0, tiled=True)  119 us
    pallas_call x1, Pallas kernels, all_to_all(): pl.pallas_call(functools.partial(a2a_kernel, count), out_shape=[jax.Shape...  62.1 us
    all_to_all x1, blocking collectives, exchange(): return lax.all_to_all(buffer, 'gx', split_axis=0, concat_axis=0, tiled=True)  37 us
    all_to_all x2, starting transfers between devices, exchange(): return lax.all_to_all(buffer, 'gx', split_axis=0, concat_axis=0, tiled=True)  24.3 us
    ppermute x4, starting transfers between devices, other_core(): return lax.ppermute(values, 'ta', perm=[(0, 1), (1, 0)])  10.4 us
    dot_general x2, matrix products, weighted_sums(): jnp.dot(w, feats, preferred_element_type=jnp.float32)  7.73 us
    dot_general x1, matrix products, bucket_weights(): lax.dot_general(unit[start:start + block], unit, (((1,), (1,)), ((), ()))...  7.6 us
    dot_general x2, matrix products, place(): jnp.dot(place_mat, payload, preferred_element_type=jnp.float32)  7.1 us
  transfers between devices with their start and end apart: 6, of which 4 were waited for; matrix products, arithmetic and copies ran while one was open for 1% of the time, Pallas kernels for 0%

profile of v14, /device:TPU:1, one launch (start us, length us, event | category | flops | bytes accessed | tf_op | source)
XLA Modules:
  0.0 297.1 jit_solution(15908719813622553279)
XLA Ops:
  0.0 0.0 copy-start
  0.0 1.3 convert_reduce_fusion.2
  1.3 0.7 multiply_add_fusion
  2.0 0.9 convert_reduce_fusion.1
  2.9 1.5 fusion.8
  4.4 1.5 fusion.9
  6.0 0.0 copy-done
  6.0 5.2 %and_select_fusion = bf16[2048,768]{1,0:T(8,128)(2,1)} fusion(pred[768]{0:T(1024)(128)(4,1)S(1)} %iota_compare_fusion.11, pred[2048]{0:T(1024)(128)(4,1)S(1)} %compare_not_fusion, s32[1024]{0:T(1024)S(1)} %multiply_add_fusion, bf16[1024,256]{1,0:T(8,128)(2,1)S(1)} %copy-done, bf16[1024,512]{1,0:T(8,128)(2,1)S(1)} %fusion.9), kind=kOutput, calls=%fused_computation.12 | convolution fusion | flops 3231186944 | bytes 4725504 | tf_op jit(solution)/shard_map/dot_general | solution.py:143
  11.2 0.0 copy-start.3
  11.2 16.6 %all-to-all-start = ((bf16[128,16,768]{2,1,0:T(8,128)(2,1)}), bf16[128,16,768]{2,1,0:T(8,128)(2,1)S(1)}, u32[]{:S(2)}, u32[]{:S(2)}) async-start(bf16[128,16,768]{2,1,0:T(8,128)(2,1)} %bitcast.26), calls=%async_computation | async-start | bytes 6291456 | tf_op jit(solution)/shard_map/all_to_all | solution.py:146
  27.9 0.0 copy-done.3
  27.9 70.6 %all-to-all-done = bf16[128,16,768]{2,1,0:T(8,128)(2,1)S(1)} async-done(((bf16[128,16,768]{2,1,0:T(8,128)(2,1)}), bf16[128,16,768]{2,1,0:T(8,128)(2,1)S(1)}, u32[]{:S(2)}, u32[]{:S(2)}) %all-to-all-start) | async-done | bytes 3145760 | tf_op jit(solution)/shard_map/all_to_all | solution.py:146
  98.5 0.2 convert_reduce_fusion.3
  98.8 7.6 %convert_reduce_fusion = (f32[2048]{0:T(1024)S(1)}, bf16[2048,2048]{1,0:T(8,128)(2,1)S(1)}) fusion(f32[2048]{0:T(1024)S(1)} %convert_reduce_fusion.3, bf16[2048,768]{1,0:T(8,128)(2,1)S(1)} %bitcast.24), kind=kOutput, calls=%fused_computation.3 | convolution fusion | flops 4324325376 | bytes 10502144 | tf_op jit(solution)/shard_map/dot_general | solution.py:106
  106.4 0.0 copy-start.4
  106.4 4.0 %fusion.14 = f32[2048,256]{1,0:T(8,128)} fusion(bf16[2048,2048]{1,0:T(8,128)(2,1)S(1)} %get-tuple-element.16, bf16[2048,768]{1,0:T(8,128)(2,1)S(1)} %bitcast.25), kind=kOutput, calls=%fused_computation.28 | convolution fusion | flops 2147483648 | bytes 11534336 | tf_op jit(solution)/shard_map/dot_general | solution.py:123
  110.4 0.0 copy-done.4
  110.4 0.7 reshape.96.refs_1_
  111.1 62.1 %shard_map.37 = (f32[128,16,256]{2,1,0:T(8,128)}, f32[128,16]{1,0:T(8,128)}) custom-call(f32[128,16,256]{2,1,0:T(8,128)} %bitcast.27, f32[128,16]{1,0:T(8,128)} %reshape.96.refs_1_), custom_call_target="tpu_custom_call" | custom-call | tf_op jit(solution)/shard_map/pallas_call | solution.py:85
  173.2 0.0 copy-start.2
  173.2 0.0 copy-start.1
  173.2 5.1 %gather_fusion = f32[1024,256]{1,0:T(8,128)S(1)} fusion(f32[2048,256]{1,0:T(8,128)} %bitcast.22, s32[1024]{0:T(1024)S(1)} %broadcast_clamp_fusion), kind=kCustom, calls=%fused_computation | custom fusion | bytes 2101248 | tf_op jit(solution)/shard_map/gather | solution.py:167
  178.4 4.9 %collective-permute-start = (f32[1024,256]{1,0:T(8,128)S(1)}, f32[1024,256]{1,0:T(8,128)S(1)}, u32[]{:S(2)}, u32[]{:S(2)}) collective-permute-start(f32[1024,256]{1,0:T(8,128)S(1)} %gather_fusion), channel_id=1, source_target_pairs={{0,1},{1,0},{2,3},{3,2},{4,5},{5,4},{6,7},{7,6},{8,9},{9,8},{10,11... | collective-permute-start | bytes 3145736 | tf_op jit(solution)/shard_map/ppermute | solution.py:149
  183.3 0.0 copy-done.2
  183.3 0.1 broadcast_in_dim.23
  183.4 1.0 select_reduce_fusion
  184.3 0.1 collective-permute-start.1
  184.4 1.1 collective-permute-done.1
  185.6 0.0 slice-start
  185.6 0.0 slice-start.1
  185.6 0.0 collective-permute-done
  185.6 0.0 copy-done.1
  185.6 1.8 fusion.7
  187.5 37.0 %all_to_all.15 = bf16[128,16,256]{2,1,0:T(8,128)(2,1)S(1)} all-to-all(bf16[128,16,256]{2,1,0:T(8,128)(2,1)S(1)} %bitcast.28), channel_id=1, replica_groups=mesh['gx'=128,'ta'=2] {'gx'}, dimensions={0} | all-to-all | bytes 2097152 | tf_op jit(solution)/shard_map/all_to_all | solution.py:146
  224.5 0.0 slice-done
  224.5 0.0 slice-done.1
  224.5 3.8 %fusion.23 = f32[128,16,256]{2,1,0:T(8,128)} fusion(bf16[128,16,2048]{2,1,0:T(8,128)(2,1)S(1)} %bitcast.36, bf16[2048,256,1]{1,0,2:T(8,128)(2,1)S(1)} %bitcast.29), kind=kOutput, calls=%fused_computation.55 | convolution fusion | flops 2147483648 | bytes 11534336 | tf_op jit(solution)/shard_map/dot_general | solution.py:123
  228.2 7.6 %all-to-all-start.2 = ((f32[128,16,256]{2,1,0:T(8,128)}), f32[128,16,256]{2,1,0:T(8,128)S(1)}, u32[]{:S(2)}, u32[]{:S(2)}) async-start(f32[128,16,256]{2,1,0:T(8,128)} %fusion.23), calls=%async_computation.2 | async-start | bytes 4194304 | tf_op jit(solution)/shard_map/all_to_all | solution.py:146
  235.9 48.4 %all-to-all-done.2 = f32[128,16,256]{2,1,0:T(8,128)S(1)} async-done(((f32[128,16,256]{2,1,0:T(8,128)}), f32[128,16,256]{2,1,0:T(8,128)S(1)}, u32[]{:S(2)}, u32[]{:S(2)}) %all-to-all-start.2) | async-done | bytes 2097184 | tf_op jit(solution)/shard_map/all_to_all | solution.py:146
  284.3 1.6 gather_fusion.2
  285.9 5.3 %collective-permute-start.3 = (f32[512,256]{1,0:T(8,128)S(1)}, f32[512,256]{1,0:T(8,128)}, u32[]{:S(2)}, u32[]{:S(2)}) collective-permute-start(f32[512,256]{1,0:T(8,128)S(1)} %gather_fusion.2), channel_id=1, source_target_pairs={{0,1},{1,0},{2,3},{3,2},{4,5},{5,4},{6,7},{7,6},{8,9},{9,8},{10,11... | collective-permute-start | bytes 1572872 | tf_op jit(solution)/shard_map/ppermute | solution.py:149
  291.2 1.6 gather_fusion.1
  292.8 0.1 collective-permute-start.2
  292.9 1.1 convert_element_type.52
  294.0 0.0 collective-permute-done.3
  294.0 0.7 collective-permute-done.2
  294.8 2.3 fusion.17
  (12 shorter events, 0.1 us)
Async XLA Ops:
  0.0 6.0 %copy-start = (bf16[1024,256]{1,0:T(8,128)(2,1)S(1)}, bf16[1024,256]{1,0:T(8,128)(2,1)}, u32[]{:S(2)}) copy-start(bf16[1024,256]{1,0:T(8,128)(2,1)} %param.4) | copy-start | bytes 1572868
  11.2 16.7 %copy-start.3 = (s32[1,1024,1]{1,2,0:T(1,128)S(1)}, s32[1,1024,1]{1,2,0:T(1,128)}, u32[]{:S(2)}) copy-start(s32[1,1024,1]{1,2,0:T(1,128)} %param.5) | copy-start | bytes 12292
  11.2 87.3 %all-to-all-start = ((bf16[128,16,768]{2,1,0:T(8,128)(2,1)}), bf16[128,16,768]{2,1,0:T(8,128)(2,1)S(1)}, u32[]{:S(2)}, u32[]{:S(2)}) async-start(bf16[128,16,768]{2,1,0:T(8,128)(2,1)} %bitcast.26), calls=%async_computation | async-start | bytes 6291456 | tf_op jit(solution)/shard_map/all_to_all | solution.py:146
  106.4 4.0 %copy-start.4 = (bf16[2048,2048]{1,0:T(8,128)(2,1)}, bf16[2048,2048]{1,0:T(8,128)(2,1)S(1)}, u32[]{:S(2)}) copy-start(bf16[2048,2048]{1,0:T(8,128)(2,1)S(1)} %get-tuple-element.16) | copy-start | bytes 25165828
  173.2 10.1 %copy-start.2 = (f32[128,16]{1,0:T(8,128)S(1)}, f32[128,16]{1,0:T(8,128)}, u32[]{:S(2)}) copy-start(f32[128,16]{1,0:T(8,128)} %get-tuple-element.8) | copy-start | bytes 24580
  173.2 12.4 %copy-start.1 = (bf16[1024,256]{1,0:T(8,128)(2,1)S(1)}, bf16[1024,256]{1,0:T(8,128)(2,1)}, u32[]{:S(2)}) copy-start(bf16[1024,256]{1,0:T(8,128)(2,1)} %param.4) | copy-start | bytes 1572868
  178.4 7.3 %collective-permute-start = (f32[1024,256]{1,0:T(8,128)S(1)}, f32[1024,256]{1,0:T(8,128)S(1)}, u32[]{:S(2)}, u32[]{:S(2)}) collective-permute-start(f32[1024,256]{1,0:T(8,128)S(1)} %gather_fusion), channel_id=1, source_target_pairs={{0,1},{1,0},{2,3},{3,2},{4,5},{5,4},{6,7},{7,6},{8,9},{9,8},{10,11... | collective-permute-start | bytes 3145736 | tf_op jit(solution)/shard_map/ppermute | solution.py:149
  184.3 1.3 collective-permute-start.1
  185.6 38.9 %slice-start = ((s8[8388608]{0:T(1024)(128)(4,1)}), s8[4194304]{0:T(1024)(128)(4,1)S(1)}, s32[]{:S(2)}) async-start(s8[8388608]{0:T(1024)(128)(4,1)} %bitcast.34), calls=%async_computation.3 | async-start | bytes 8388608
  185.6 38.9 %slice-start.1 = ((s8[8388608]{0:T(1024)(128)(4,1)}), s8[4194304]{0:T(1024)(128)(4,1)S(1)}, s32[]{:S(2)}) async-start(s8[8388608]{0:T(1024)(128)(4,1)} %bitcast.34), calls=%async_computation.4 | async-start | bytes 8388608
  228.2 56.1 %all-to-all-start.2 = ((f32[128,16,256]{2,1,0:T(8,128)}), f32[128,16,256]{2,1,0:T(8,128)S(1)}, u32[]{:S(2)}, u32[]{:S(2)}) async-start(f32[128,16,256]{2,1,0:T(8,128)} %fusion.23), calls=%async_computation.2 | async-start | bytes 4194304 | tf_op jit(solution)/shard_map/all_to_all | solution.py:146
  285.9 8.1 %collective-permute-start.3 = (f32[512,256]{1,0:T(8,128)S(1)}, f32[512,256]{1,0:T(8,128)}, u32[]{:S(2)}, u32[]{:S(2)}) collective-permute-start(f32[512,256]{1,0:T(8,128)S(1)} %gather_fusion.2), channel_id=1, source_target_pairs={{0,1},{1,0},{2,3},{3,2},{4,5},{5,4},{6,7},{7,6},{8,9},{9,8},{10,11... | collective-permute-start | bytes 1572872 | tf_op jit(solution)/shard_map/ppermute | solution.py:149
  292.8 2.0 collective-permute-start.2

commit v15 on v12

--- a/solution.py
+++ b/solution.py
@@ -183,7 +183,7 @@
     scale = (1.0 + total_den)[:, None]
     first = (1.0 - alpha_mix) * prior + alpha_mix * total_num / scale
 
-    feats1 = exchange(place(first.astype(jnp.bfloat16)).reshape(groups, slot, -1))
+    (feats1,) = all_to_all([place(first.astype(jnp.bfloat16)).reshape(groups, slot, -1)], 1)
     num2 = weighted_sums(blocks, feats1.reshape(groups * slot, -1))
     back2 = exchange(num2.reshape(groups, slot, -1)).reshape(groups * slot, -1)
     row_num2 = to_items(back2)

time: 297 us -> 300 us (1.010)
  blocking collectives: 180 us -> 147 us
  Pallas kernels: 62.3 us -> 92.9 us
  matrix products: 29.4 us -> 33.8 us
    all_to_all x3 -> x2, blocking collectives: 180 us -> 147 us  [exchange(): return lax.all_to_all(buffer, 'gx', split_axis=0, concat_axis=0, tiled=True)]
    pallas_call x1 -> x2, Pallas kernels: 62.3 us -> 92.9 us  [all_to_all(): pl.pallas_call(functools.partial(a2a_kernel, count), out_shape=[jax.Shape...]
    dot_general x2, matrix products: 6.51 us -> 9.94 us  [weighted_sums(): jnp.dot(w, feats, preferred_element_type=jnp.float32)]
where the time goes in v15:
time: 300 us
  blocking collectives  147 us (49%)
  Pallas kernels  92.9 us (31%)
  matrix products  33.8 us (11%)
  starting transfers between devices  10.9 us (4%)
  other arithmetic  10.7 us (4%)
  waiting for transfers between devices  3.43 us (1%)
    all_to_all x2, blocking collectives, exchange(): return lax.all_to_all(buffer, 'gx', split_axis=0, concat_axis=0, tiled=True)  147 us
    pallas_call x2, Pallas kernels, all_to_all(): pl.pallas_call(functools.partial(a2a_kernel, count), out_shape=[jax.Shape...  92.9 us
    ppermute x3, starting transfers between devices, other_core(): return lax.ppermute(values, 'ta', perm=[(0, 1), (1, 0)])  10.9 us
    dot_general x2, matrix products, weighted_sums(): jnp.dot(w, feats, preferred_element_type=jnp.float32)  9.94 us
    dot_general x4, matrix products, to_items(): lax.dot_general(place_mat, part.astype(jnp.bfloat16), (((0,), (0,)), ((),...  9.41 us
    dot_general x1, matrix products, bucket_weights(): lax.dot_general(unit[start:start + block], unit, (((1,), (1,)), ((), ()))...  7.48 us
    dot_general x2, matrix products, place(): jnp.dot(place_mat, payload, preferred_element_type=jnp.float32)  6.93 us
  transfers between devices with their start and end apart: 3, of which 2 were waited for; matrix products, arithmetic and copies ran while one was open for 0% of the time, Pallas kernels for 0%

profile of v15, /device:TPU:1, one launch (start us, length us, event | category | flops | bytes accessed | tf_op | source)
XLA Modules:
  0.0 299.8 jit_solution(1718409378339676824)
XLA Ops:
  0.0 0.0 copy-start
  0.0 1.3 convert_reduce_fusion.2
  1.3 0.7 multiply_add_fusion
  2.0 1.5 fusion.16
  3.5 0.9 convert_reduce_fusion.1
  4.4 1.5 fusion.17
  6.0 0.0 copy-done
  6.0 4.1 %and_select_fusion = bf16[2048,768]{1,0:T(8,128)(2,1)S(1)} fusion(pred[768]{0:T(1024)(128)(4,1)S(1)} %iota_compare_fusion.19, pred[2048]{0:T(1024)(128)(4,1)S(1)} %compare_not_fusion, s32[1024]{0:T(1024)S(1)} %multiply_add_fusion, bf16[1024,256]{1,0:T(8,128)(2,1)S(1)} %copy-done, bf16[1024,512]{1,0:T(8,128)(2,1)S(1)} %fusion.17), kind=kOutput, calls=%fused_computation.13 | convolution fusion | flops 3231186944 | bytes 4725504 | tf_op jit(solution)/shard_map/dot_general | solution.py:143
  10.1 87.0 %all_to_all.10 = bf16[128,16,768]{2,1,0:T(8,128)(2,1)S(1)} all-to-all(bf16[128,16,768]{2,1,0:T(8,128)(2,1)S(1)} %bitcast.25), channel_id=1, replica_groups=mesh['gx'=128,'ta'=2] {'gx'}, dimensions={0} | all-to-all | bytes 6291456 | tf_op jit(solution)/shard_map/all_to_all | solution.py:157
  97.0 0.2 convert_reduce_fusion.3
  97.3 7.5 %convert_reduce_fusion = (f32[2048]{0:T(1024)S(1)}, bf16[2048,2048]{1,0:T(8,128)(2,1)S(1)}) fusion(f32[2048]{0:T(1024)S(1)} %convert_reduce_fusion.3, bf16[2048,768]{1,0:T(8,128)(2,1)S(1)} %bitcast.23), kind=kOutput, calls=%fused_computation | convolution fusion | flops 4324325376 | bytes 10502144 | tf_op jit(solution)/shard_map/dot_general | solution.py:106
  104.8 0.0 copy-start.2
  104.8 4.0 %fusion.26 = f32[2048,256]{1,0:T(8,128)} fusion(bf16[2048,2048]{1,0:T(8,128)(2,1)S(1)} %get-tuple-element.14, bf16[2048,768]{1,0:T(8,128)(2,1)S(1)} %bitcast.24), kind=kOutput, calls=%fused_computation.41 | convolution fusion | flops 2147483648 | bytes 11534336 | tf_op jit(solution)/shard_map/dot_general | solution.py:123
  108.8 0.0 copy-done.2
  108.8 0.7 reshape.64.refs_1_
  109.5 62.3 %shard_map.37 = (f32[128,16,256]{2,1,0:T(8,128)}, f32[128,16]{1,0:T(8,128)}) custom-call(f32[128,16,256]{2,1,0:T(8,128)} %bitcast.26, f32[128,16]{1,0:T(8,128)} %reshape.64.refs_1_), custom_call_target="tpu_custom_call" | custom-call | tf_op jit(solution)/shard_map/pallas_call | solution.py:85
  171.8 1.9 reduce-precision_convert_fusion.1
  173.7 2.3 fusion.3
  176.0 0.0 copy-start.1
  176.0 2.4 fusion.24
  178.4 5.0 %collective-permute-start = (f32[1024,256]{1,0:T(8,128)S(1)}, f32[1024,256]{1,0:T(8,128)S(1)}, u32[]{:S(2)}, u32[]{:S(2)}) collective-permute-start(f32[1024,256]{1,0:T(8,128)S(1)} %fusion.24), channel_id=1, source_target_pairs={{0,1},{1,0},{2,3},{3,2},{4,5},{5,4},{6,7},{7,6},{8,9},{9,8},{10,11... | collective-permute-start | bytes 3145736 | tf_op jit(solution)/shard_map/ppermute | solution.py:160
  183.4 0.0 copy-done.1
  183.4 0.1 broadcast_in_dim.15
  183.5 1.0 select_reduce_fusion
  184.4 0.1 collective-permute-start.1
  184.6 1.1 collective-permute-done.1
  185.7 0.0 collective-permute-done
  185.7 2.8 fusion.15
  188.6 30.6 %shard_map.38 = bf16[128,16,256]{2,1,0:T(8,128)(2,1)} custom-call(bf16[128,16,256]{2,1,0:T(8,128)(2,1)} %bitcast.27), custom_call_target="tpu_custom_call" | custom-call | tf_op jit(solution)/shard_map/pallas_call | solution.py:85
  219.1 6.0 %fusion.31 = f32[128,16,256]{2,1,0:T(8,128)S(1)} fusion(bf16[128,16,2048]{2,1,0:T(8,128)(2,1)} %bitcast.31, bf16[2048,256,1]{1,0,2:T(8,128)(2,1)} %bitcast.28), kind=kOutput, calls=%fused_computation.56 | convolution fusion | flops 2147483648 | bytes 11534336 | tf_op jit(solution)/shard_map/dot_general | solution.py:123
  225.1 60.3 %all_to_all.11 = f32[128,16,256]{2,1,0:T(8,128)S(1)} all-to-all(f32[128,16,256]{2,1,0:T(8,128)S(1)} %fusion.31), channel_id=1, replica_groups=mesh['gx'=128,'ta'=2] {'gx'}, dimensions={0} | all-to-all | bytes 4194304 | tf_op jit(solution)/shard_map/all_to_all | solution.py:157
  285.4 0.3 reduce-precision_convert_fusion
  285.7 2.3 fusion
  288.1 2.4 fusion.25
  290.4 5.8 %collective-permute-start.2 = (f32[1024,256]{1,0:T(8,128)S(1)}, f32[1024,256]{1,0:T(8,128)S(1)}, u32[]{:S(2)}, u32[]{:S(2)}) collective-permute-start(f32[1024,256]{1,0:T(8,128)S(1)} %fusion.25), channel_id=1, source_target_pairs={{0,1},{1,0},{2,3},{3,2},{4,5},{5,4},{6,7},{7,6},{8,9},{9,8},{10,11... | collective-permute-start | bytes 3145736 | tf_op jit(solution)/shard_map/ppermute | solution.py:160
  296.2 2.3 collective-permute-done.2
  298.5 1.3 divide_add_fusion
  (4 shorter events, 0.0 us)
Async XLA Ops:
  0.0 6.0 %copy-start = (bf16[1024,256]{1,0:T(8,128)(2,1)S(1)}, bf16[1024,256]{1,0:T(8,128)(2,1)}, u32[]{:S(2)}) copy-start(bf16[1024,256]{1,0:T(8,128)(2,1)} %param.4) | copy-start | bytes 1572868
  104.8 4.0 %copy-start.2 = (bf16[2048,2048]{1,0:T(8,128)(2,1)}, bf16[2048,2048]{1,0:T(8,128)(2,1)S(1)}, u32[]{:S(2)}) copy-start(bf16[2048,2048]{1,0:T(8,128)(2,1)S(1)} %get-tuple-element.14) | copy-start | bytes 25165828
  176.0 7.4 %copy-start.1 = (f32[128,16]{1,0:T(8,128)S(1)}, f32[128,16]{1,0:T(8,128)}, u32[]{:S(2)}) copy-start(f32[128,16]{1,0:T(8,128)} %get-tuple-element.8) | copy-start | bytes 24580
  178.4 7.3 %collective-permute-start = (f32[1024,256]{1,0:T(8,128)S(1)}, f32[1024,256]{1,0:T(8,128)S(1)}, u32[]{:S(2)}, u32[]{:S(2)}) collective-permute-start(f32[1024,256]{1,0:T(8,128)S(1)} %fusion.24), channel_id=1, source_target_pairs={{0,1},{1,0},{2,3},{3,2},{4,5},{5,4},{6,7},{7,6},{8,9},{9,8},{10,11... | collective-permute-start | bytes 3145736 | tf_op jit(solution)/shard_map/ppermute | solution.py:160
  184.4 1.3 collective-permute-start.1
  290.4 8.1 %collective-permute-start.2 = (f32[1024,256]{1,0:T(8,128)S(1)}, f32[1024,256]{1,0:T(8,128)S(1)}, u32[]{:S(2)}, u32[]{:S(2)}) collective-permute-start(f32[1024,256]{1,0:T(8,128)S(1)} %fusion.25), channel_id=1, source_target_pairs={{0,1},{1,0},{2,3},{3,2},{4,5},{5,4},{6,7},{7,6},{8,9},{9,8},{10,11... | collective-permute-start | bytes 3145736 | tf_op jit(solution)/shard_map/ppermute | solution.py:160

commit v16 on v12

--- a/solution.py
+++ b/solution.py
@@ -57,7 +57,8 @@
         )
 
     def partner(i):
-        return lax.rem(me + (1 - 2 * lax.rem(i, 2)) * (i // 2 + 1) + n, n)
+        j = n - 2 - i
+        return lax.rem(me + (1 - 2 * lax.rem(j, 2)) * (j // 2 + 1) + n, n)
 
     def send(i, carry):
         peer = partner(i)

time: 297 us -> 298 us (level)
  Pallas kernels: 62.3 us -> 66.5 us
  starting transfers between devices: 10.1 us -> 5.98 us
    pallas_call x1, Pallas kernels: 62.3 us -> 66.5 us  [all_to_all(): pl.pallas_call(functools.partial(a2a_kernel, count), out_shape=[jax.Shape...]
    ppermute x3, starting transfers between devices: 10.1 us -> 5.98 us  [other_core(): return lax.ppermute(values, 'ta', perm=[(0, 1), (1, 0)])]
where the time goes in v16:
time: 298 us; the launch traced here: 297 us
  blocking collectives  180 us (60%)
  Pallas kernels  66.5 us (22%)
  matrix products  29.4 us (10%)
  other arithmetic  10.7 us (4%)
  starting transfers between devices  5.98 us (2%)
  waiting for transfers between devices  3.43 us (1%)
    all_to_all x3, blocking collectives, exchange(): return lax.all_to_all(buffer, 'gx', split_axis=0, concat_axis=0, tiled=True)  180 us
    pallas_call x1, Pallas kernels, all_to_all(): pl.pallas_call(functools.partial(a2a_kernel, count), out_shape=[jax.Shape...  66.5 us
    dot_general x4, matrix products, to_items(): lax.dot_general(place_mat, part.astype(jnp.bfloat16), (((0,), (0,)), ((),...  9.43 us
    dot_general x1, matrix products, bucket_weights(): lax.dot_general(unit[start:start + block], unit, (((1,), (1,)), ((), ()))...  7.46 us
    dot_general x2, matrix products, weighted_sums(): jnp.dot(w, feats, preferred_element_type=jnp.float32)  6.5 us
    dot_general x2, matrix products, place(): jnp.dot(place_mat, payload, preferred_element_type=jnp.float32)  5.98 us
    ppermute x3, starting transfers between devices, other_core(): return lax.ppermute(values, 'ta', perm=[(0, 1), (1, 0)])  5.98 us
  transfers between devices with their start and end apart: 3, of which 2 were waited for; matrix products, arithmetic and copies ran while one was open for 0% of the time, Pallas kernels for 0%

profile of v16, /device:TPU:1, one launch (start us, length us, event | category | flops | bytes accessed | tf_op | source)
XLA Modules:
  0.0 297.3 jit_solution(6513631449225682968)
XLA Ops:
  0.0 0.0 copy-start
  0.0 1.3 convert_reduce_fusion.2
  1.3 0.7 multiply_add_fusion
  2.0 1.5 fusion.16
  3.5 0.9 convert_reduce_fusion.1
  4.4 1.5 fusion.17
  6.0 0.0 copy-done
  6.0 4.1 %and_select_fusion = bf16[2048,768]{1,0:T(8,128)(2,1)S(1)} fusion(pred[768]{0:T(1024)(128)(4,1)S(1)} %iota_compare_fusion.19, pred[2048]{0:T(1024)(128)(4,1)S(1)} %compare_not_fusion, s32[1024]{0:T(1024)S(1)} %multiply_add_fusion, bf16[1024,256]{1,0:T(8,128)(2,1)S(1)} %copy-done, bf16[1024,512]{1,0:T(8,128)(2,1)S(1)} %fusion.17), kind=kOutput, calls=%fused_computation.13 | convolution fusion | flops 3231186944 | bytes 4725504 | tf_op jit(solution)/shard_map/dot_general | solution.py:144
  10.1 87.0 %all_to_all.15 = bf16[128,16,768]{2,1,0:T(8,128)(2,1)S(1)} all-to-all(bf16[128,16,768]{2,1,0:T(8,128)(2,1)S(1)} %bitcast.25), channel_id=1, replica_groups=mesh['gx'=128,'ta'=2] {'gx'}, dimensions={0} | all-to-all | bytes 6291456 | tf_op jit(solution)/shard_map/all_to_all | solution.py:158
  97.1 0.2 convert_reduce_fusion.3
  97.3 7.5 %convert_reduce_fusion = (f32[2048]{0:T(1024)S(1)}, bf16[2048,2048]{1,0:T(8,128)(2,1)S(1)}) fusion(f32[2048]{0:T(1024)S(1)} %convert_reduce_fusion.3, bf16[2048,768]{1,0:T(8,128)(2,1)S(1)} %bitcast.23), kind=kOutput, calls=%fused_computation | convolution fusion | flops 4324325376 | bytes 10502144 | tf_op jit(solution)/shard_map/dot_general | solution.py:107
  104.8 0.0 copy-start.2
  104.8 4.0 %fusion.26 = f32[2048,256]{1,0:T(8,128)} fusion(bf16[2048,2048]{1,0:T(8,128)(2,1)S(1)} %get-tuple-element.14, bf16[2048,768]{1,0:T(8,128)(2,1)S(1)} %bitcast.24), kind=kOutput, calls=%fused_computation.41 | convolution fusion | flops 2147483648 | bytes 11534336 | tf_op jit(solution)/shard_map/dot_general | solution.py:124
  108.8 0.0 copy-done.2
  108.8 0.7 reshape.64.refs_1_
  109.5 66.5 %shard_map.37 = (f32[128,16,256]{2,1,0:T(8,128)}, f32[128,16]{1,0:T(8,128)}) custom-call(f32[128,16,256]{2,1,0:T(8,128)} %bitcast.26, f32[128,16]{1,0:T(8,128)} %reshape.64.refs_1_), custom_call_target="tpu_custom_call" | custom-call | tf_op jit(solution)/shard_map/pallas_call | solution.py:86
  176.0 1.9 reduce-precision_convert_fusion.1
  177.9 2.4 fusion.3
  180.3 0.0 copy-start.1
  180.3 2.4 fusion.24
  182.7 0.9 collective-permute-start
  183.5 0.0 copy-done.1
  183.5 0.1 broadcast_in_dim.15
  183.6 1.0 select_reduce_fusion
  184.6 0.1 collective-permute-start.1
  184.7 1.1 collective-permute-done.1
  185.8 0.0 slice-start
  185.9 0.0 slice-start.1
  185.9 0.0 collective-permute-done
  185.9 1.9 fusion.15
  187.7 37.1 %all_to_all.16 = bf16[128,16,256]{2,1,0:T(8,128)(2,1)S(1)} all-to-all(bf16[128,16,256]{2,1,0:T(8,128)(2,1)S(1)} %bitcast.27), channel_id=1, replica_groups=mesh['gx'=128,'ta'=2] {'gx'}, dimensions={0} | all-to-all | bytes 2097152 | tf_op jit(solution)/shard_map/all_to_all | solution.py:158
  224.9 0.0 slice-done
  224.9 0.0 slice-done.1
  224.9 2.5 fusion.31
  227.4 56.2 %all_to_all.17 = f32[128,16,256]{2,1,0:T(8,128)S(1)} all-to-all(f32[128,16,256]{2,1,0:T(8,128)S(1)} %fusion.31), channel_id=1, replica_groups=mesh['gx'=128,'ta'=2] {'gx'}, dimensions={0} | all-to-all | bytes 4194304 | tf_op jit(solution)/shard_map/all_to_all | solution.py:158
  283.7 0.3 reduce-precision_convert_fusion
  284.0 2.4 fusion
  286.4 2.4 fusion.25
  288.7 5.0 %collective-permute-start.2 = (f32[1024,256]{1,0:T(8,128)S(1)}, f32[1024,256]{1,0:T(8,128)S(1)}, u32[]{:S(2)}, u32[]{:S(2)}) collective-permute-start(f32[1024,256]{1,0:T(8,128)S(1)} %fusion.25), channel_id=1, source_target_pairs={{0,1},{1,0},{2,3},{3,2},{4,5},{5,4},{6,7},{7,6},{8,9},{9,8},{10,11... | collective-permute-start | bytes 3145736 | tf_op jit(solution)/shard_map/ppermute | solution.py:161
  293.7 2.3 collective-permute-done.2
  296.0 1.3 divide_add_fusion
  (5 shorter events, 0.0 us)
Async XLA Ops:
  0.0 6.0 %copy-start = (bf16[1024,256]{1,0:T(8,128)(2,1)S(1)}, bf16[1024,256]{1,0:T(8,128)(2,1)}, u32[]{:S(2)}) copy-start(bf16[1024,256]{1,0:T(8,128)(2,1)} %param.4) | copy-start | bytes 1572868
  104.8 4.0 %copy-start.2 = (bf16[2048,2048]{1,0:T(8,128)(2,1)}, bf16[2048,2048]{1,0:T(8,128)(2,1)S(1)}, u32[]{:S(2)}) copy-start(bf16[2048,2048]{1,0:T(8,128)(2,1)S(1)} %get-tuple-element.14) | copy-start | bytes 25165828
  180.3 3.3 %copy-start.1 = (f32[128,16]{1,0:T(8,128)S(1)}, f32[128,16]{1,0:T(8,128)}, u32[]{:S(2)}) copy-start(f32[128,16]{1,0:T(8,128)} %get-tuple-element.8) | copy-start | bytes 24580
  182.7 3.2 %collective-permute-start = (f32[1024,256]{1,0:T(8,128)S(1)}, f32[1024,256]{1,0:T(8,128)S(1)}, u32[]{:S(2)}, u32[]{:S(2)}) collective-permute-start(f32[1024,256]{1,0:T(8,128)S(1)} %fusion.24), channel_id=1, source_target_pairs={{0,1},{1,0},{2,3},{3,2},{4,5},{5,4},{6,7},{7,6},{8,9},{9,8},{10,11... | collective-permute-start | bytes 3145736 | tf_op jit(solution)/shard_map/ppermute | solution.py:161
  184.6 1.3 collective-permute-start.1
  185.8 39.0 %slice-start = ((s8[8388608]{0:T(1024)(128)(4,1)}), s8[4194304]{0:T(1024)(128)(4,1)S(1)}, s32[]{:S(2)}) async-start(s8[8388608]{0:T(1024)(128)(4,1)} %bitcast.31), calls=%async_computation.3 | async-start | bytes 8388608
  185.9 39.0 %slice-start.1 = ((s8[8388608]{0:T(1024)(128)(4,1)}), s8[4194304]{0:T(1024)(128)(4,1)S(1)}, s32[]{:S(2)}) async-start(s8[8388608]{0:T(1024)(128)(4,1)} %bitcast.31), calls=%async_computation.4 | async-start | bytes 8388608
  288.7 7.3 %collective-permute-start.2 = (f32[1024,256]{1,0:T(8,128)S(1)}, f32[1024,256]{1,0:T(8,128)S(1)}, u32[]{:S(2)}, u32[]{:S(2)}) collective-permute-start(f32[1024,256]{1,0:T(8,128)S(1)} %fusion.25), channel_id=1, source_target_pairs={{0,1},{1,0},{2,3},{3,2},{4,5},{5,4},{6,7},{7,6},{8,9},{9,8},{10,11... | collective-permute-start | bytes 3145736 | tf_op jit(solution)/shard_map/ppermute | solution.py:161

commit v17 on v16

--- a/solution.py
+++ b/solution.py
@@ -160,6 +160,14 @@
     def other_core(values):
         return lax.ppermute(values, "ta", perm=[(0, 1), (1, 0)])
 
+    def both_tables(values):
+        half = values.shape[1] // 2
+        parts = []
+        for c in range(2):
+            mine = to_items(values[:, c * half : (c + 1) * half])
+            parts.append(mine + other_core(mine))
+        return jnp.concatenate(parts, axis=1)
+
     unit_here = normalize(embeddings)
     placed = place(jnp.concatenate([unit_here, labels], axis=1))
     column = lax.broadcasted_iota(jnp.int32, placed.shape, 1)
@@ -176,19 +184,16 @@
     back_num, back_den = all_to_all([num1.reshape(groups, slot, width_l), den.reshape(groups, slot)], 0)
     back_num = back_num.reshape(groups * slot, width_l)
     back_den = back_den.reshape(groups * slot)
-    row_num = to_items(back_num)
     row_den = jnp.sum(jnp.where(target[None, :] == slots[:, None], back_den[:, None], 0.0), axis=0)
-    other_num, other_den = other_core((row_num, row_den))
-    total_num = row_num + other_num
-    total_den = row_den + other_den
+    total_den = row_den + other_core(row_den)
+    total_num = both_tables(back_num)
     scale = (1.0 + total_den)[:, None]
     first = (1.0 - alpha_mix) * prior + alpha_mix * total_num / scale
 
     feats1 = exchange(place(first.astype(jnp.bfloat16)).reshape(groups, slot, -1))
     num2 = weighted_sums(blocks, feats1.reshape(groups * slot, -1))
     back2 = exchange(num2.reshape(groups, slot, -1)).reshape(groups * slot, -1)
-    row_num2 = to_items(back2)
-    total_num2 = row_num2 + other_core(row_num2)
+    total_num2 = both_tables(back2)
     return (1.0 - alpha_mix) * prior + alpha_mix * total_num2 / scale
 
 

time: 298 us -> 308 us (1.034); the launches traced: 297 us -> 303 us
  matrix products: 29.4 us -> 35.4 us
  other arithmetic: 10.7 us -> 7.61 us
    dot_general x4 -> x8, matrix products: 9.43 us -> 15.5 us  [to_items(): lax.dot_general(place_mat, part.astype(jnp.bfloat16), (((0,), (0,)), ((),...]
    ppermute x3 -> x5, starting transfers between devices: 5.98 us -> 6.77 us  [other_core(): return lax.ppermute(values, 'ta', perm=[(0, 1), (1, 0)])]
  transfers between devices with their start and end apart: 3 -> 5, of which waited for: 2 -> 2; matrix products, arithmetic and copies ran while one was open for 0% -> 1% of each run, Pallas kernels for 0% -> 0%
where the time goes in v17:
time: 308 us; the launch traced here: 303 us
  blocking collectives  181 us (59%)
  Pallas kernels  67 us (22%)
  matrix products  35.4 us (11%)
  other arithmetic  7.61 us (2%)
  starting transfers between devices  6.77 us (2%)
    all_to_all x3, blocking collectives, exchange(): return lax.all_to_all(buffer, 'gx', split_axis=0, concat_axis=0, tiled=True)  181 us
    pallas_call x1, Pallas kernels, all_to_all(): pl.pallas_call(functools.partial(a2a_kernel, count), out_shape=[jax.Shape...  67 us
    dot_general x8, matrix products, to_items(): lax.dot_general(place_mat, part.astype(jnp.bfloat16), (((0,), (0,)), ((),...  15.5 us
    dot_general x1, matrix products, bucket_weights(): lax.dot_general(unit[start:start + block], unit, (((1,), (1,)), ((), ()))...  7.57 us
    ppermute x5, starting transfers between devices, other_core(): return lax.ppermute(values, 'ta', perm=[(0, 1), (1, 0)])  6.77 us
    dot_general x2, matrix products, weighted_sums(): jnp.dot(w, feats, preferred_element_type=jnp.float32)  6.42 us
  transfers between devices with their start and end apart: 5, of which 2 were waited for; matrix products, arithmetic and copies ran while one was open for 1% of the time, Pallas kernels for 0%

profile of v17, /device:TPU:1, one launch (start us, length us, event | category | flops | bytes accessed | tf_op | source)
XLA Modules:
  0.0 302.7 jit_solution(2393230468154964289)
XLA Ops:
  0.0 0.0 copy-start
  0.0 1.3 convert_reduce_fusion.2
  1.3 0.7 multiply_add_fusion
  2.0 0.9 convert_reduce_fusion.1
  2.9 1.5 fusion.24
  4.4 1.5 fusion.25
  6.0 0.0 copy-done
  6.0 4.1 %and_select_fusion = bf16[2048,768]{1,0:T(8,128)(2,1)S(1)} fusion(pred[768]{0:T(1024)(128)(4,1)S(1)} %iota_compare_fusion.27, pred[2048]{0:T(1024)(128)(4,1)S(1)} %compare_not_fusion, s32[1024]{0:T(1024)S(1)} %multiply_add_fusion, bf16[1024,256]{1,0:T(8,128)(2,1)S(1)} %copy-done, bf16[1024,512]{1,0:T(8,128)(2,1)S(1)} %fusion.25), kind=kOutput, calls=%fused_computation.17 | convolution fusion | flops 3231186944 | bytes 4725504 | tf_op jit(solution)/shard_map/dot_general | solution.py:144
  10.1 87.2 %all_to_all.15 = bf16[128,16,768]{2,1,0:T(8,128)(2,1)S(1)} all-to-all(bf16[128,16,768]{2,1,0:T(8,128)(2,1)S(1)} %bitcast.17), channel_id=1, replica_groups=mesh['gx'=128,'ta'=2] {'gx'}, dimensions={0} | all-to-all | bytes 6291456 | tf_op jit(solution)/shard_map/all_to_all | solution.py:158
  97.3 0.2 convert_reduce_fusion.3
  97.6 7.6 %convert_reduce_fusion = (f32[2048]{0:T(1024)S(1)}, bf16[2048,2048]{1,0:T(8,128)(2,1)S(1)}) fusion(f32[2048]{0:T(1024)S(1)} %convert_reduce_fusion.3, bf16[2048,768]{1,0:T(8,128)(2,1)S(1)} %bitcast.15), kind=kOutput, calls=%fused_computation | convolution fusion | flops 4324325376 | bytes 10502144 | tf_op jit(solution)/shard_map/dot_general | solution.py:107
  105.2 0.0 copy-start.4
  105.2 4.0 %fusion.38 = f32[2048,256]{1,0:T(8,128)} fusion(bf16[2048,2048]{1,0:T(8,128)(2,1)S(1)} %get-tuple-element.10, bf16[2048,768]{1,0:T(8,128)(2,1)S(1)} %bitcast.16), kind=kOutput, calls=%fused_computation.57 | convolution fusion | flops 2147483648 | bytes 11534336 | tf_op jit(solution)/shard_map/dot_general | solution.py:124
  109.2 0.0 copy-done.4
  109.2 0.7 reshape.64.refs_1_
  109.9 67.0 %shard_map.37 = (f32[128,16,256]{2,1,0:T(8,128)}, f32[128,16]{1,0:T(8,128)}) custom-call(f32[128,16,256]{2,1,0:T(8,128)} %bitcast.22, f32[128,16]{1,0:T(8,128)} %reshape.64.refs_1_), custom_call_target="tpu_custom_call" | custom-call | tf_op jit(solution)/shard_map/pallas_call | solution.py:86
  176.9 0.0 copy-start.2
  176.9 3.0 fusion.7
  179.9 0.0 copy-done.2
  179.9 0.0 copy-start.1
  179.9 1.6 fusion.5
  181.6 0.0 copy-done.1
  181.6 0.1 broadcast_in_dim.15
  181.6 0.0 copy-start.3
  181.6 2.9 fusion.30
  184.6 0.8 collective-permute-start
  185.4 0.0 copy-done.3
  185.4 1.6 fusion.31
  187.0 0.1 collective-permute-start.1
  187.1 1.0 select_reduce_fusion
  188.1 0.7 collective-permute-start.2
  188.8 0.2 copy.14
  189.0 0.6 collective-permute-done.2
  189.6 0.0 collective-permute-done
  189.6 0.1 add.61
  189.7 0.0 collective-permute-done.1
  189.7 0.0 slice-start
  189.7 0.1 add.63
  189.8 0.0 slice-start.1
  189.8 1.8 fusion.23
  191.6 37.0 %all_to_all.16 = bf16[128,16,256]{2,1,0:T(8,128)(2,1)S(1)} all-to-all(bf16[128,16,256]{2,1,0:T(8,128)(2,1)S(1)} %bitcast.23), channel_id=1, replica_groups=mesh['gx'=128,'ta'=2] {'gx'}, dimensions={0} | all-to-all | bytes 2097152 | tf_op jit(solution)/shard_map/all_to_all | solution.py:158
  228.6 0.0 slice-done
  228.6 0.0 slice-done.1
  228.6 2.4 fusion.54
  231.0 56.4 %all_to_all.17 = f32[128,16,256]{2,1,0:T(8,128)S(1)} all-to-all(f32[128,16,256]{2,1,0:T(8,128)S(1)} %fusion.54), channel_id=1, replica_groups=mesh['gx'=128,'ta'=2] {'gx'}, dimensions={0} | all-to-all | bytes 4194304 | tf_op jit(solution)/shard_map/all_to_all | solution.py:158
  287.5 1.6 fusion.2
  289.1 1.6 fusion
  290.7 1.6 fusion.32
  292.3 5.0 %collective-permute-start.3 = (f32[1024,128]{0,1:T(8,128)S(1)}, f32[1024,128]{0,1:T(8,128)S(1)}, u32[]{:S(2)}, u32[]{:S(2)}) collective-permute-start(f32[1024,128]{0,1:T(8,128)S(1)} %fusion.32), channel_id=1, source_target_pairs={{0,1},{1,0},{2,3},{3,2},{4,5},{5,4},{6,7},{7,6},{8,9},{9,8},{10,11... | collective-permute-start | bytes 1572872 | tf_op jit(solution)/shard_map/ppermute | solution.py:161
  297.3 1.6 fusion.33
  298.9 0.1 collective-permute-start.4
  299.0 0.0 collective-permute-done.3
  299.0 0.1 add.69
  299.1 1.8 collective-permute-done.4
  300.9 0.1 add.71
  300.9 0.2 fusion.43
  301.2 1.3 copy.15
  (5 shorter events, 0.0 us)
Async XLA Ops:
  0.0 6.0 %copy-start = (bf16[1024,256]{1,0:T(8,128)(2,1)S(1)}, bf16[1024,256]{1,0:T(8,128)(2,1)}, u32[]{:S(2)}) copy-start(bf16[1024,256]{1,0:T(8,128)(2,1)} %param.4) | copy-start | bytes 1572868
  105.2 4.0 %copy-start.4 = (bf16[2048,2048]{1,0:T(8,128)(2,1)}, bf16[2048,2048]{1,0:T(8,128)(2,1)S(1)}, u32[]{:S(2)}) copy-start(bf16[2048,2048]{1,0:T(8,128)(2,1)S(1)} %get-tuple-element.10) | copy-start | bytes 25165828
  176.9 3.0 copy-start.2
  179.9 1.6 copy-start.1
  181.6 3.8 %copy-start.3 = (f32[128,16,256]{2,1,0:T(8,128)S(1)}, f32[128,16,256]{2,1,0:T(8,128)}, u32[]{:S(2)}) copy-start(f32[128,16,256]{2,1,0:T(8,128)} %get-tuple-element.7) | copy-start | bytes 6291460
  184.6 5.0 %collective-permute-start = (f32[1024,128]{0,1:T(8,128)S(1)}, f32[1024,128]{0,1:T(8,128)S(1)}, u32[]{:S(2)}, u32[]{:S(2)}) collective-permute-start(f32[1024,128]{0,1:T(8,128)S(1)} %fusion.30), channel_id=1, source_target_pairs={{0,1},{1,0},{2,3},{3,2},{4,5},{5,4},{6,7},{7,6},{8,9},{9,8},{10,11... | collective-permute-start | bytes 1572872 | tf_op jit(solution)/shard_map/ppermute | solution.py:161
  187.0 2.7 collective-permute-start.1
  188.1 1.6 collective-permute-start.2
  189.7 38.9 %slice-start = ((s8[8388608]{0:T(1024)(128)(4,1)}), s8[4194304]{0:T(1024)(128)(4,1)S(1)}, s32[]{:S(2)}) async-start(s8[8388608]{0:T(1024)(128)(4,1)} %bitcast.31), calls=%async_computation.3 | async-start | bytes 8388608
  189.8 38.8 %slice-start.1 = ((s8[8388608]{0:T(1024)(128)(4,1)}), s8[4194304]{0:T(1024)(128)(4,1)S(1)}, s32[]{:S(2)}) async-start(s8[8388608]{0:T(1024)(128)(4,1)} %bitcast.31), calls=%async_computation.4 | async-start | bytes 8388608
  292.3 6.7 %collective-permute-start.3 = (f32[1024,128]{0,1:T(8,128)S(1)}, f32[1024,128]{0,1:T(8,128)S(1)}, u32[]{:S(2)}, u32[]{:S(2)}) collective-permute-start(f32[1024,128]{0,1:T(8,128)S(1)} %fusion.32), channel_id=1, source_target_pairs={{0,1},{1,0},{2,3},{3,2},{4,5},{5,4},{6,7},{7,6},{8,9},{9,8},{10,11... | collective-permute-start | bytes 1572872 | tf_op jit(solution)/shard_map/ppermute | solution.py:161
  298.9 2.0 collective-permute-start.4

commit v18 on v12

--- a/solution.py
+++ b/solution.py
@@ -32,9 +32,12 @@
     mesh_ids = pl.DeviceIdType.MESH
     barrier = pltpu.get_barrier_semaphore()
 
+    def partner(i):
+        j = n - 2 - i
+        return lax.rem(me + (1 - 2 * lax.rem(j, 2)) * (j // 2 + 1) + n, n)
+
     def greet(i, carry):
-        peer = lax.rem(me + 1 + i, n)
-        pl.semaphore_signal(barrier, 1, device_id=(peer, core), device_id_type=mesh_ids)
+        pl.semaphore_signal(barrier, 1, device_id=(partner(i), core), device_id_type=mesh_ids)
         return carry
 
     lax.fori_loop(0, n - 1, greet, 0)
@@ -55,9 +58,6 @@
             device_id=(peer, core),
             device_id_type=mesh_ids,
         )
-
-    def partner(i):
-        return lax.rem(me + (1 - 2 * lax.rem(i, 2)) * (i // 2 + 1) + n, n)
 
     def send(i, carry):
         peer = partner(i)

time: 297 us -> 298 us (level)
  starting transfers between devices: 10.1 us -> 5.94 us
  Pallas kernels: 62.3 us -> 66.1 us
    ppermute x3, starting transfers between devices: 10.1 us -> 5.94 us  [other_core(): return lax.ppermute(values, 'ta', perm=[(0, 1), (1, 0)])]
    pallas_call x1, Pallas kernels: 62.3 us -> 66.1 us  [all_to_all(): pl.pallas_call(functools.partial(a2a_kernel, count), out_shape=[jax.Shape...]
where the time goes in v18:
time: 298 us
  blocking collectives  181 us (61%)
  Pallas kernels  66.1 us (22%)
  matrix products  29.4 us (10%)
  other arithmetic  10.7 us (4%)
  starting transfers between devices  5.94 us (2%)
  waiting for transfers between devices  3.43 us (1%)
    all_to_all x3, blocking collectives, exchange(): return lax.all_to_all(buffer, 'gx', split_axis=0, concat_axis=0, tiled=True)  181 us
    pallas_call x1, Pallas kernels, all_to_all(): pl.pallas_call(functools.partial(a2a_kernel, count), out_shape=[jax.Shape...  66.1 us
    dot_general x4, matrix products, to_items(): lax.dot_general(place_mat, part.astype(jnp.bfloat16), (((0,), (0,)), ((),...  9.43 us
    dot_general x1, matrix products, bucket_weights(): lax.dot_general(unit[start:start + block], unit, (((1,), (1,)), ((), ()))...  7.46 us
    dot_general x2, matrix products, weighted_sums(): jnp.dot(w, feats, preferred_element_type=jnp.float32)  6.51 us
    dot_general x2, matrix products, place(): jnp.dot(place_mat, payload, preferred_element_type=jnp.float32)  5.98 us
  transfers between devices with their start and end apart: 3, of which 2 were waited for; matrix products, arithmetic and copies ran while one was open for 0% of the time, Pallas kernels for 0%

profile of v18, /device:TPU:1, one launch (start us, length us, event | category | flops | bytes accessed | tf_op | source)
XLA Modules:
  0.0 297.7 jit_solution(12202901370441032215)
XLA Ops:
  0.0 0.0 copy-start
  0.0 1.3 convert_reduce_fusion.2
  1.3 0.7 multiply_add_fusion
  2.0 1.5 fusion.16
  3.5 0.9 convert_reduce_fusion.1
  4.4 1.5 fusion.17
  6.0 0.0 copy-done
  6.0 4.1 %and_select_fusion = bf16[2048,768]{1,0:T(8,128)(2,1)S(1)} fusion(pred[768]{0:T(1024)(128)(4,1)S(1)} %iota_compare_fusion.19, pred[2048]{0:T(1024)(128)(4,1)S(1)} %compare_not_fusion, s32[1024]{0:T(1024)S(1)} %multiply_add_fusion, bf16[1024,256]{1,0:T(8,128)(2,1)S(1)} %copy-done, bf16[1024,512]{1,0:T(8,128)(2,1)S(1)} %fusion.17), kind=kOutput, calls=%fused_computation.13 | convolution fusion | flops 3231186944 | bytes 4725504 | tf_op jit(solution)/shard_map/dot_general | solution.py:143
  10.1 87.0 %all_to_all.15 = bf16[128,16,768]{2,1,0:T(8,128)(2,1)S(1)} all-to-all(bf16[128,16,768]{2,1,0:T(8,128)(2,1)S(1)} %bitcast.25), channel_id=1, replica_groups=mesh['gx'=128,'ta'=2] {'gx'}, dimensions={0} | all-to-all | bytes 6291456 | tf_op jit(solution)/shard_map/all_to_all | solution.py:157
  97.1 0.2 convert_reduce_fusion.3
  97.3 7.5 %convert_reduce_fusion = (f32[2048]{0:T(1024)S(1)}, bf16[2048,2048]{1,0:T(8,128)(2,1)S(1)}) fusion(f32[2048]{0:T(1024)S(1)} %convert_reduce_fusion.3, bf16[2048,768]{1,0:T(8,128)(2,1)S(1)} %bitcast.23), kind=kOutput, calls=%fused_computation | convolution fusion | flops 4324325376 | bytes 10502144 | tf_op jit(solution)/shard_map/dot_general | solution.py:106
  104.8 0.0 copy-start.2
  104.8 4.0 %fusion.26 = f32[2048,256]{1,0:T(8,128)} fusion(bf16[2048,2048]{1,0:T(8,128)(2,1)S(1)} %get-tuple-element.14, bf16[2048,768]{1,0:T(8,128)(2,1)S(1)} %bitcast.24), kind=kOutput, calls=%fused_computation.41 | convolution fusion | flops 2147483648 | bytes 11534336 | tf_op jit(solution)/shard_map/dot_general | solution.py:123
  108.8 0.0 copy-done.2
  108.8 0.7 reshape.64.refs_1_
  109.5 66.1 %shard_map.37 = (f32[128,16,256]{2,1,0:T(8,128)}, f32[128,16]{1,0:T(8,128)}) custom-call(f32[128,16,256]{2,1,0:T(8,128)} %bitcast.26, f32[128,16]{1,0:T(8,128)} %reshape.64.refs_1_), custom_call_target="tpu_custom_call" | custom-call | tf_op jit(solution)/shard_map/pallas_call | solution.py:85
  175.5 1.9 reduce-precision_convert_fusion.1
  177.5 2.4 fusion.3
  179.8 0.0 copy-start.1
  179.8 2.4 fusion.24
  182.2 0.8 collective-permute-start
  183.0 0.0 copy-done.1
  183.0 0.1 broadcast_in_dim.15
  183.1 1.0 select_reduce_fusion
  184.1 0.1 collective-permute-start.1
  184.2 1.1 collective-permute-done.1
  185.4 0.0 slice-start
  185.4 0.0 slice-start.1
  185.4 0.0 collective-permute-done
  185.4 1.9 fusion.15
  187.2 38.0 %all_to_all.16 = bf16[128,16,256]{2,1,0:T(8,128)(2,1)S(1)} all-to-all(bf16[128,16,256]{2,1,0:T(8,128)(2,1)S(1)} %bitcast.27), channel_id=1, replica_groups=mesh['gx'=128,'ta'=2] {'gx'}, dimensions={0} | all-to-all | bytes 2097152 | tf_op jit(solution)/shard_map/all_to_all | solution.py:157
  225.3 0.0 slice-done
  225.3 0.0 slice-done.1
  225.3 2.5 fusion.31
  227.8 56.2 %all_to_all.17 = f32[128,16,256]{2,1,0:T(8,128)S(1)} all-to-all(f32[128,16,256]{2,1,0:T(8,128)S(1)} %fusion.31), channel_id=1, replica_groups=mesh['gx'=128,'ta'=2] {'gx'}, dimensions={0} | all-to-all | bytes 4194304 | tf_op jit(solution)/shard_map/all_to_all | solution.py:157
  284.1 0.3 reduce-precision_convert_fusion
  284.4 2.4 fusion
  286.8 2.4 fusion.25
  289.1 5.0 %collective-permute-start.2 = (f32[1024,256]{1,0:T(8,128)S(1)}, f32[1024,256]{1,0:T(8,128)S(1)}, u32[]{:S(2)}, u32[]{:S(2)}) collective-permute-start(f32[1024,256]{1,0:T(8,128)S(1)} %fusion.25), channel_id=1, source_target_pairs={{0,1},{1,0},{2,3},{3,2},{4,5},{5,4},{6,7},{7,6},{8,9},{9,8},{10,11... | collective-permute-start | bytes 3145736 | tf_op jit(solution)/shard_map/ppermute | solution.py:160
  294.1 2.3 collective-permute-done.2
  296.4 1.3 divide_add_fusion
  (5 shorter events, 0.0 us)
Async XLA Ops:
  0.0 6.0 %copy-start = (bf16[1024,256]{1,0:T(8,128)(2,1)S(1)}, bf16[1024,256]{1,0:T(8,128)(2,1)}, u32[]{:S(2)}) copy-start(bf16[1024,256]{1,0:T(8,128)(2,1)} %param.4) | copy-start | bytes 1572868
  104.8 4.0 %copy-start.2 = (bf16[2048,2048]{1,0:T(8,128)(2,1)}, bf16[2048,2048]{1,0:T(8,128)(2,1)S(1)}, u32[]{:S(2)}) copy-start(bf16[2048,2048]{1,0:T(8,128)(2,1)S(1)} %get-tuple-element.14) | copy-start | bytes 25165828
  179.8 3.2 %copy-start.1 = (f32[128,16]{1,0:T(8,128)S(1)}, f32[128,16]{1,0:T(8,128)}, u32[]{:S(2)}) copy-start(f32[128,16]{1,0:T(8,128)} %get-tuple-element.8) | copy-start | bytes 24580
  182.2 3.2 %collective-permute-start = (f32[1024,256]{1,0:T(8,128)S(1)}, f32[1024,256]{1,0:T(8,128)S(1)}, u32[]{:S(2)}, u32[]{:S(2)}) collective-permute-start(f32[1024,256]{1,0:T(8,128)S(1)} %fusion.24), channel_id=1, source_target_pairs={{0,1},{1,0},{2,3},{3,2},{4,5},{5,4},{6,7},{7,6},{8,9},{9,8},{10,11... | collective-permute-start | bytes 3145736 | tf_op jit(solution)/shard_map/ppermute | solution.py:160
  184.1 1.3 collective-permute-start.1
  185.4 39.9 %slice-start = ((s8[8388608]{0:T(1024)(128)(4,1)}), s8[4194304]{0:T(1024)(128)(4,1)S(1)}, s32[]{:S(2)}) async-start(s8[8388608]{0:T(1024)(128)(4,1)} %bitcast.31), calls=%async_computation.3 | async-start | bytes 8388608
  185.4 39.9 %slice-start.1 = ((s8[8388608]{0:T(1024)(128)(4,1)}), s8[4194304]{0:T(1024)(128)(4,1)S(1)}, s32[]{:S(2)}) async-start(s8[8388608]{0:T(1024)(128)(4,1)} %bitcast.31), calls=%async_computation.4 | async-start | bytes 8388608
  289.1 7.3 %collective-permute-start.2 = (f32[1024,256]{1,0:T(8,128)S(1)}, f32[1024,256]{1,0:T(8,128)S(1)}, u32[]{:S(2)}, u32[]{:S(2)}) collective-permute-start(f32[1024,256]{1,0:T(8,128)S(1)} %fusion.25), channel_id=1, source_target_pairs={{0,1},{1,0},{2,3},{3,2},{4,5},{5,4},{6,7},{7,6},{8,9},{9,8},{10,11... | collective-permute-start | bytes 3145736 | tf_op jit(solution)/shard_map/ppermute | solution.py:160
